TPU v7x, 32 devices: a whole 2x2x4 slice. The times are simulated.
32 devices in a mesh: groups: 2 (over y), fsdp: 8 (over z, core), band: 2 (over x).
Axes of the slice: x: 2, y: 2, z: 4, core: 2. Of those that a mesh axis runs over, the one named last changes fastest.
Arguments:
- hidden_in: bfloat16 [16, 4, 64, 5632], P(('groups', 'fsdp'), 'band'), parts along dimension 0, may hold values from -6 to 6
- tap_weights: bfloat16 [9, 5632], P(None, 'fsdp'), may hold values from -2 to 2
- tap_bias: bfloat16 [5632], P('fsdp'), may hold values from -3 to 3
- w_out: bfloat16 [2816, 2240], P('fsdp'), may hold values from -0.109375 to 0.109375
- cotangent: bfloat16 [16, 4, 64, 2240], P(('groups', 'fsdp'), 'band'), parts along dimension 0, may hold values from -0.59765625 to 0.59765625
Outputs:
- block_out: bfloat16 [16, 4, 64, 2240], P(('groups', 'fsdp'), 'band'), parts along dimension 0
- d_hidden: bfloat16 [16, 4, 64, 5632], P(('groups', 'fsdp'), 'band'), parts along dimension 0
- d_taps: float32 [18, 5632], P('groups', 'fsdp'), parts along dimension 0
- d_tap_bias: float32 [11264], P(('groups', 'fsdp')), parts along dimension 0
There are 2 independent parts, one for each index of `groups`. A program takes and returns all parts, laid end to end along the dimension named above; an argument that names none is the same for every part. Nothing has to cross between parts.
All inputs are finite; a program needn't handle non-finite values.
Results may differ from a plain program's by a relative error of at most 0.0049.
Values may be sent and summed in bfloat16 or wider, within the bound.
No kernel may reach another device: no remote copies, remote signals or barrier semaphores. Data moves between devices by JAX's collectives and lax.ppermute only.
A program may use at most 128 MiB of HBM per device.

v0:
```python
import jax
import jax.numpy as jnp
from jax import lax
from jax.sharding import PartitionSpec as P


def with_halo(cells, sides, width):
    for axis, dim in sides:
        count = lax.axis_size(axis)
        ends = count - 1
        head = lax.slice_in_dim(cells, 0, width, axis=dim)
        tail = lax.slice_in_dim(cells, cells.shape[dim] - width, cells.shape[dim], axis=dim)
        cells = jnp.concatenate(
            [
                lax.ppermute(tail, axis, [(i, (i + 1) % count) for i in range(ends)]),
                cells,
                lax.ppermute(head, axis, [((i + 1) % count, i) for i in range(ends)]),
            ],
            axis=dim,
        )
    return cells


def body(hidden_in, tap_weights, tap_bias, w_out, cotangent):
    kernel_all, offset_all = (
        lax.all_gather(tap_weights, "fsdp", axis=1, tiled=True),
        lax.all_gather(tap_bias, "fsdp", axis=0, tiled=True),
    )
    kernel = kernel_all.astype(jnp.float32)
    offset = offset_all.astype(jnp.float32)
    image_count, row_count, col_count, channels = hidden_in.shape
    hidden_units = channels // 2
    token_count = image_count * row_count * col_count
    extended = with_halo(hidden_in, (("band", 1),), 1)
    padded = jnp.pad(extended, ((0, 0), (0, 0), (1, 1), (0, 0)))
    summed = jnp.zeros((image_count, row_count, col_count, channels), jnp.float32) + offset
    for tap_row in range(3):
        for tap_col in range(3):
            window = padded[:, tap_row : tap_row + row_count, tap_col : tap_col + col_count, :]
            summed = summed + kernel[3 * tap_row + tap_col] * window
    values_half = summed[..., :hidden_units]
    gate_half = summed[..., hidden_units:]
    sigmoid_gate = jax.nn.sigmoid(gate_half)
    silu_gate = gate_half * sigmoid_gate
    glu_flat = (values_half * silu_gate).astype(jnp.bfloat16).reshape(token_count, hidden_units)
    grad_flat = cotangent.reshape(token_count, cotangent.shape[3])
    features = grad_flat.shape[1]
    piece = lax.all_gather(w_out, "fsdp", axis=0, tiled=True)
    out_sum = jnp.dot(glu_flat, piece, preferred_element_type=jnp.float32)
    d_piece = lax.dot_general(
        grad_flat, piece, (((1,), (1,)), ((), ())), preferred_element_type=jnp.float32
    )
    out_sum, d_glu = (out_sum, d_piece)
    block_out = out_sum.astype(jnp.bfloat16).reshape(image_count, row_count, col_count, features)
    d_glu = d_glu.reshape(image_count, row_count, col_count, hidden_units)
    slope = sigmoid_gate * (1.0 + gate_half * (1.0 - sigmoid_gate))
    d_pre = jnp.concatenate([d_glu * silu_gate, d_glu * values_half * slope], axis=-1).astype(
        jnp.bfloat16
    )
    d_extended = with_halo(d_pre, (("band", 1),), 1)
    d_pad = jnp.pad(d_extended, ((0, 0), (0, 0), (1, 1), (0, 0)))
    d_image = jnp.zeros((image_count, row_count, col_count, channels), jnp.float32)
    tap_terms = []
    for tap_row in range(3):
        for tap_col in range(3):
            d_window = d_pad[
                :, 2 - tap_row : 2 - tap_row + row_count, 2 - tap_col : 2 - tap_col + col_count, :
            ]
            d_image = d_image + kernel[3 * tap_row + tap_col] * d_window
            window = padded[:, tap_row : tap_row + row_count, tap_col : tap_col + col_count, :]
            tap_terms.append(
                jnp.einsum("srck,srck->k", window, d_pre, preferred_element_type=jnp.float32)
            )
    d_hidden = d_image.astype(jnp.bfloat16)
    tap_grad = jnp.stack(tap_terms)
    bias_grad = jnp.sum(d_pre.astype(jnp.float32), axis=(0, 1, 2))
    tap_grad, bias_grad = lax.psum((tap_grad, bias_grad), "band")
    tap_share, bias_share = (
        lax.psum_scatter(tap_grad, "fsdp", scatter_dimension=1, tiled=True),
        lax.psum_scatter(bias_grad, "fsdp", scatter_dimension=0, tiled=True),
    )
    return (block_out, d_hidden, tap_share, bias_share)


def solution(mesh):
    placed = (
        P(("groups", "fsdp"), "band", None, None),
        P(None, "fsdp"),
        P("fsdp"),
        P("fsdp", None),
        P(("groups", "fsdp"), "band", None, None),
    )
    return jax.shard_map(
        body,
        mesh=mesh,
        in_specs=placed,
        out_specs=(
            P(("groups", "fsdp"), "band", None, None),
            P(("groups", "fsdp"), "band", None, None),
            P("groups", "fsdp"),
            P(("groups", "fsdp")),
        ),
        check_vma=False,
    )
```

profile of v0, /device:TPU:0, one launch (start us, length us, event | category | flops | bytes accessed | tf_op | source)
XLA Modules:
  0.0 235.5 jit_solution(369298379283991862)
XLA Ops:
  7.2 0.0 copy-start
  7.2 0.0 copy-start.22
  7.2 0.0 copy-start.3
  7.2 0.0 copy-start.23
  7.2 0.0 copy-start.21
  7.2 0.0 all-gather.3.cloned.1.call-start
  7.3 0.7 all-gather.3.cloned.1.call-update
  8.0 0.0 reduce-scatter.4.cloned.1.call-start
  8.0 2.6 %fusion.26 = (bf16[1,1,64,5632]{3,2,1,0:T(8,128)(2,1)}, bf16[1,1,64,5632]{3,2,1,0:T(8,128)(2,1)}) fusion(bf16[1,2,64,5632]{3,2,1,0:T(8,128)(2,1)} %param.5), kind=kLoop, calls=%fused_computation.70 | loop fusion | bytes 2883584 | tf_op jit(solution)/shard_map/slice | solution.py:11
  10.6 1.3 collective-permute-start.1
  11.9 5.0 %collective-permute-start = (bf16[1,1,64,5632]{3,2,1,0:T(8,128)(2,1)}, bf16[1,1,64,5632]{3,2,1,0:T(8,128)(2,1)S(1)}, u32[]{:S(2)}, u32[]{:S(2)}) collective-permute-start(bf16[1,1,64,5632]{3,2,1,0:T(8,128)(2,1)} %get-tuple-element.40), channel_id=1, source_target_pairs={{0,1},{2,3},{4,5},{6,7},{8,9},{10,11},{12,13},{14,15},{16,17},{18,... | collective-permute-start | bytes 2162696 | tf_op jit(solution)/shard_map/ppermute | solution.py:15
  16.8 0.0 copy-done.22
  16.9 0.6 fusion.27
  18.1 0.0 copy-done.23
  18.1 0.2 dynamic-update-slice
  18.4 31.5 %all-reduce.2 = bf16[5632]{0:T(1024)(128)(2,1)S(1)} all-reduce(bf16[5632]{0:T(1024)(128)(2,1)S(1)} %dynamic-update-slice), channel_id=1, replica_groups=mesh['groups'=2,'fsdp'=8,'band'=2] {'fsdp'}, use_global_device_ids=true, to_apply=%add.2 | all-reduce | flops 5632 | bytes 22528
  49.8 0.6 convert_element_type.109
  50.4 0.0 copy-done.21
  50.5 25.0 %all-gather = bf16[8,704,9]{1,2,0:T(8,128)(2,1)S(1)} all-gather(bf16[1,704,9]{1,2,0:T(8,128)(2,1)S(1)} %bitcast.101), channel_id=1, replica_groups=mesh['groups'=2,'fsdp'=8,'band'=2] {'fsdp'}, dimensions={0}, use_global_device_ids=true | all-gather | bytes 114048 | tf_op jit(solution)/shard_map/all_gather | solution.py:26
  75.5 0.7 copy_convert_fusion
  76.2 1.8 reshape.190
  78.7 2.4 %slice_reduce_fusion.8 = (f32[5632]{0:T(1024)S(1)}, f32[5632]{0:T(1024)S(1)}, f32[5632]{0:T(1024)S(1)}, f32[5632]{0:T(1024)S(1)}, f32[5632]{0:T(1024)S(1)}, /*in...) fusion(f32[9,5632]{1,0:T(8,128)} %bitcast.97), kind=kLoop, calls=%fused_computation.69 | loop fusion | bytes 405504 | tf_op jit(solution)/shard_map/slice | solution.py:40
  81.0 0.0 copy-start.8
  81.0 0.0 copy-start.10
  81.1 0.0 copy-start.12
  81.1 0.0 copy-start.14
  81.1 0.0 copy-start.20
  81.1 0.0 collective-permute-done.1
  81.1 0.0 copy-start.4
  81.1 0.0 collective-permute-done
  81.2 1.1 select_maximum_fusion.3
  82.3 1.6 copy-done.1
  83.9 3.9 %multiply_add_fusion = f32[1,2,64,5632]{3,2,1,0:T(8,128)} fusion(bf16[1,2,64,5632]{3,2,1,0:T(8,128)(2,1)S(1)} %copy-done.3, f32[5632]{0:T(1024)S(1)} %get-tuple-element.18, f32[5632]{0:T(1024)S(1)} %get-tuple-element.19, f32[5632]{0:T(1024)S(1)} %get-tuple-element.20, f32[5632]{0:T(1024)S(1)} %get-tuple-element.21, f32[5632]{0:T(1024)S(1)} %get-tuple-element.22, ...), kind=kLoop, calls=%fused_computation.39 | loop fusion | flops 20905984 | bytes 14643200 | tf_op jit(solution)/shard_map/add | solution.py:40
  87.8 46.5 %all-gather.3.cloned.1.call-done = bf16[2816,2240]{1,0:T(8,128)(2,1)} async-done(((bf16[352,2240]{1,0:T(8,128)(2,1)}), bf16[2816,2240]{1,0:T(8,128)(2,1)}) %all-gather.3.cloned.1.call-update) | async-done | bytes 12615696 | tf_op jit(solution)/shard_map/all_gather | solution.py:48
  134.3 10.8 %multiply_convert_fusion = (bf16[1,2,64,2816]{3,2,1,0:T(8,128)(2,1)S(1)}, bf16[1,2,64,2816]{3,2,1,0:T(8,128)(2,1)S(1)}, bf16[1,2,64,2816]{3,2,1,0:T(8,128)(2,1)}) fusion(f32[1,2,64,5632]{3,2,1,0:T(8,128)} %multiply_add_fusion, bf16[2816,2240]{1,0:T(8,128)(2,1)} %all-gather.3.cloned.1.call-done, bf16[1,2,64,2240]{3,2,1,0:T(8,128)(2,1)S(1)} %copy-done), kind=kOutput, calls=%fused_computation.52 | convolution fusion | flops 1620213760 | bytes 18235392 | tf_op jit(solution)/shard_map/dot_general | solution.py:50
  145.1 1.2 fusion.23
  146.3 0.2 copy-done.5
  146.5 0.5 copy-done.7
  147.0 3.8 %fusion.19 = (f32[5632]{0:T(1024)S(1)}, f32[5632]{0:T(1024)S(1)}, f32[5632]{0:T(1024)S(1)}, f32[5632]{0:T(1024)S(1)}, f32[5632]{0:T(1024)S(1)}, /*index=5*/f32[5...) fusion(bf16[1,1,64,5632]{3,2,1,0:T(8,128)(2,1)S(1)} %copy-done.5, ...), kind=kLoop, calls=%fused_computation.36 | loop fusion | flops 28785152 | bytes 13178880 | tf_op jit(solution)/shard_map/srck,srck->k/dot_general | solution.py:72
  150.8 0.6 stack.37
  151.4 0.6 stack.31
  152.0 0.6 stack.34
  152.7 0.6 stack.30
  153.3 0.6 stack.32
  153.9 0.6 stack.33
  154.5 0.6 stack.35
  155.2 0.6 stack.36
  155.8 0.6 stack.38
  156.4 3.3 %collective-permute-start.2 = (bf16[1,1,64,5632]{3,2,1,0:T(8,128)(2,1)}, bf16[1,1,64,5632]{3,2,1,0:T(8,128)(2,1)S(1)}, u32[]{:S(2)}, u32[]{:S(2)}) collective-permute-start(bf16[1,1,64,5632]{3,2,1,0:T(8,128)(2,1)} %get-tuple-element.37), channel_id=1, source_target_pairs={{0,1},{2,3},{4,5},{6,7},{8,9},{10,11},{12,13},{14,15},{16,17},{18,... | collective-permute-start | bytes 2162696 | tf_op jit(solution)/shard_map/ppermute | solution.py:15
  159.7 1.5 collective-permute-start.3
  161.2 3.2 %stack.39 = f32[9,5632]{1,0:T(8,128)} concatenate(f32[1,5632]{1,0:T(1,128)} %stack.30, f32[1,5632]{1,0:T(1,128)} %stack.31, f32[1,5632]{1,0:T(1,128)} %stack.32, f32[1,5632]{1,0:T(1,128)} %stack.33, f32[1,5632]{1,0:T(1,128)} %stack.34, f32[1,5632]{1,0:T(1,128)} %stack.35, f32[1,5632]{1,0:T(1,128)} %stack.36, f32[1,5632]{1,0:T(1,128)} %stack.37, f32[1,5632]{1,0:T(1,128)} %stack.38), dimensions={0} | concatenate | bytes 405504 | tf_op jit(solution)/shard_map/stack | solution.py:75
  164.4 3.0 %copy.79 = f32[9,5632]{0,1:T(8,128)} copy(f32[9,5632]{1,0:T(8,128)} %stack.39) | data formatting | bytes 405504
  167.3 0.0 reduce-scatter.4.cloned.1.call-update
  167.3 10.8 %convolution_convert_fusion = bf16[128,2240]{0,1:T(8,128)(2,1)} fusion(bf16[128,2816]{1,0:T(8,128)(2,1)} %bitcast.98, bf16[2816,2240]{1,0:T(8,128)(2,1)} %all-gather.3.cloned.1.call-done), kind=kOutput, calls=%fused_computation.15 | convolution fusion | flops 1615093760 | bytes 13910016 | tf_op jit(solution)/shard_map/dot_general | solution.py:49
  178.2 2.1 copy.15
  180.3 0.8 convert_reduce_fusion
  181.1 27.7 %all-reduce.3 = f32[5632]{0:T(1024)} all-reduce(f32[5632]{0:T(1024)} %convert_reduce_fusion), channel_id=3, replica_groups=mesh['groups'=2,'fsdp'=8,'band'=2] {'fsdp'}, use_global_device_ids=true, to_apply=%region_4.5.clone | all-reduce | flops 5632 | bytes 45056
  208.8 0.8 dynamic-slice.2
  209.6 1.8 copy.80
  211.4 11.0 %all-reduce.4 = (f32[9,704]{1,0:T(8,128)}, f32[704]{0:T(1024)}) all-reduce(f32[9,704]{1,0:T(8,128)} %copy.80, f32[704]{0:T(1024)S(1)} %dynamic-slice.2), channel_id=1, replica_groups=mesh['groups'=2,'fsdp'=8,'band'=2] {'band'}, use_global_device_ids=true, to_apply=%region_0.1 | all-reduce | flops 7040 | bytes 56320 | tf_op jit(solution)/shard_map/psum | solution.py:77
  222.4 0.0 collective-permute-done.2
  222.4 0.0 collective-permute-done.3
  222.4 1.8 select_maximum_fusion
  224.2 4.5 %fusion.12 = bf16[1,2,64,5632]{3,2,1,0:T(8,128)(2,1)} fusion(bf16[1,4,66,5632]{3,2,1,0:T(8,128)(2,1)S(1)} %select_maximum_fusion, bf16[1,1,64,5632]{3,2,1,0:T(8,128)(2,1)S(1)} %collective-permute-done.2, bf16[1,2,64,2816]{3,2,1,0:T(8,128)(2,1)S(1)} %get-tuple-element.28, bf16[1,2,64,2816]{3,2,1,0:T(8,128)(2,1)S(1)} %get-tuple-element.29, ...), kind=kLoop, calls=%fused_computation.29 | loop fusion | flops 28835840 | bytes 13178880 | tf_op jit(solution)/shard_map/convert_element_type | solution.py:74
  (33 shorter events, 0.1 us)
Async XLA Ops:
  7.2 127.2 %copy-start = (bf16[1,2,64,2240]{3,2,1,0:T(8,128)(2,1)S(1)}, bf16[1,2,64,2240]{3,2,1,0:T(8,128)(2,1)}, u32[]{:S(2)}) copy-start(bf16[1,2,64,2240]{3,2,1,0:T(8,128)(2,1)} %param.9) | copy-start | bytes 1720324
  7.2 9.7 %copy-start.22 = (u32[32]{0:T(128)S(1)}, u32[32]{0:T(128)}, u32[]{:S(2)}) copy-start(u32[32]{0:T(128)} %constant.15) | copy-start | bytes 388
  7.2 73.9 %copy-start.3 = (bf16[1,2,64,5632]{3,2,1,0:T(8,128)(2,1)S(1)}, bf16[1,2,64,5632]{3,2,1,0:T(8,128)(2,1)}, u32[]{:S(2)}) copy-start(bf16[1,2,64,5632]{3,2,1,0:T(8,128)(2,1)} %param.5) | copy-start | bytes 4325380
  7.2 10.9 %copy-start.23 = (bf16[704]{0:T(1024)(128)(2,1)S(1)}, bf16[704]{0:T(1024)(128)(2,1)}, u32[]{:S(2)}) copy-start(bf16[704]{0:T(1024)(128)(2,1)} %param.7) | copy-start | bytes 4228
  7.2 43.2 %copy-start.21 = (bf16[9,704]{1,0:T(8,128)(2,1)S(1)}, bf16[9,704]{1,0:T(8,128)(2,1)}, u32[]{:S(2)}) copy-start(bf16[9,704]{1,0:T(8,128)(2,1)} %param.6) | copy-start | bytes 38020
  7.2 127.1 %all-gather.3.cloned.1.call-start = ((), (), s32[]{:S(2)}) async-start(), calls=%async_computation.1 | async-start | bytes 14598144 | tf_op jit(solution)/shard_map/all_gather | solution.py:48
  8.0 201.7 %reduce-scatter.4.cloned.1.call-start = ((), (), s32[]{:S(2)}) async-start(), calls=%async_computation.2 | async-start | bytes 3244032
  10.6 70.5 %collective-permute-start.1 = (bf16[1,1,64,5632]{3,2,1,0:T(8,128)(2,1)}, bf16[1,1,64,5632]{3,2,1,0:T(8,128)(2,1)S(1)}, u32[]{:S(2)}, u32[]{:S(2)}) collective-permute-start(bf16[1,1,64,5632]{3,2,1,0:T(8,128)(2,1)} %get-tuple-element.39), channel_id=1, source_target_pairs={{1,0},{3,2},{5,4},{7,6},{9,8},{11,10},{13,12},{15,14},{17,16},{19,... | collective-permute-start | bytes 2162696 | tf_op jit(solution)/shard_map/ppermute | solution.py:17
  11.9 69.3 %collective-permute-start = (bf16[1,1,64,5632]{3,2,1,0:T(8,128)(2,1)}, bf16[1,1,64,5632]{3,2,1,0:T(8,128)(2,1)S(1)}, u32[]{:S(2)}, u32[]{:S(2)}) collective-permute-start(bf16[1,1,64,5632]{3,2,1,0:T(8,128)(2,1)} %get-tuple-element.40), channel_id=1, source_target_pairs={{0,1},{2,3},{4,5},{6,7},{8,9},{10,11},{12,13},{14,15},{16,17},{18,... | collective-permute-start | bytes 2162696 | tf_op jit(solution)/shard_map/ppermute | solution.py:15
  81.0 1.2 copy-start.8
  81.0 1.2 copy-start.10
  81.1 1.2 copy-start.12
  81.1 1.2 copy-start.14
  81.1 1.2 copy-start.16
  81.1 1.2 copy-start.18
  81.1 2.8 %copy-start.20 = (f32[5632]{0:T(1024)S(1)}, f32[5632]{0:T(1024)}, u32[]{:S(2)}) copy-start(f32[5632]{0:T(1024)} %convert_element_type.109) | copy-start | bytes 67588
  81.1 1.2 copy-start.4
  81.2 1.2 copy-start.6
  82.2 1.7 copy-start.1
  134.3 12.0 %copy-start.2 = (bf16[1,4,66,5632]{3,2,1,0:T(8,128)(2,1)S(1)}, bf16[1,4,66,5632]{3,2,1,0:T(8,128)(2,1)}, u32[]{:S(2)}) copy-start(bf16[1,4,66,5632]{3,2,1,0:T(8,128)(2,1)} %copy-done.1) | copy-start | bytes 8921092
  145.1 1.4 copy-start.5
  145.1 1.8 copy-start.7
  156.4 66.0 %collective-permute-start.2 = (bf16[1,1,64,5632]{3,2,1,0:T(8,128)(2,1)}, bf16[1,1,64,5632]{3,2,1,0:T(8,128)(2,1)S(1)}, u32[]{:S(2)}, u32[]{:S(2)}) collective-permute-start(bf16[1,1,64,5632]{3,2,1,0:T(8,128)(2,1)} %get-tuple-element.37), channel_id=1, source_target_pairs={{0,1},{2,3},{4,5},{6,7},{8,9},{10,11},{12,13},{14,15},{16,17},{18,... | collective-permute-start | bytes 2162696 | tf_op jit(solution)/shard_map/ppermute | solution.py:15
  159.7 62.7 %collective-permute-start.3 = (bf16[1,1,64,5632]{3,2,1,0:T(8,128)(2,1)}, bf16[1,1,64,5632]{3,2,1,0:T(8,128)(2,1)S(1)}, u32[]{:S(2)}, u32[]{:S(2)}) collective-permute-start(bf16[1,1,64,5632]{3,2,1,0:T(8,128)(2,1)} %get-tuple-element.38), channel_id=1, source_target_pairs={{1,0},{3,2},{5,4},{7,6},{9,8},{11,10},{13,12},{15,14},{17,16},{19,... | collective-permute-start | bytes 2162696 | tf_op jit(solution)/shard_map/ppermute | solution.py:17
  222.3 1.8 copy-start.9
  222.3 1.8 copy-start.11
  222.3 1.8 copy-start.13
  222.3 1.8 copy-start.15
  222.3 1.8 copy-start.17
  222.4 1.8 copy-start.19
Sparse Core Ops, SparseCore 0:
  9.7 124.6 all-gather.2
  167.5 38.8 reduce-scatter.3
where the time goes:
time: 236 us
  blocking collectives  95.2 us (40%)
  waiting for transfers between devices  47.2 us (20%)
  local copies, waits for them, and re-layouts  26.3 us (11%)
  matrix products  21.6 us (9%)
  other arithmetic  18.4 us (8%)
  between operations  15.7 us (7%)
  starting transfers between devices  11.1 us (5%)
    unnamed x2, blocking collectives  59.2 us
    all_gather x1, waiting for transfers between devices, body(): piece = lax.all_gather(w_out, 'fsdp', axis=0, tiled=True)  46.5 us
    all_gather x1, blocking collectives, body(): lax.all_gather(tap_weights, 'fsdp', axis=1, tiled=True)  25 us
    psum x1, blocking collectives, body(): tap_grad, bias_grad = lax.psum((tap_grad, bias_grad), 'band')  11 us
    dot_general x1, matrix products, body(): out_sum = jnp.dot(glu_flat, piece, preferred_element_type=jnp.float32)  10.8 us
    dot_general x1, matrix products, body(): lax.dot_general(grad_flat, piece, (((1,), (1,)), ((), ())), preferred_ele...  10.8 us
    another operation x10, local copies, waits for them, and re-layouts, body(): tap_grad = jnp.stack(tap_terms)  8.77 us
    unnamed x54, local copies, waits for them, and re-layouts  8.64 us
  transfers between devices with their start and end apart: 6, of which 1 were waited for; matrix products, arithmetic and copies ran while one was open for 15% of the time, Pallas kernels for 0%

commit v1 on v0

v1 whole, which is shorter than its diff:
```python
import functools

import jax
import jax.numpy as jnp
from jax import lax
from jax.experimental import pallas as pl
from jax.experimental.pallas import tpu as pltpu
from jax.sharding import PartitionSpec as P

F32 = jnp.float32
BF16 = jnp.bfloat16
LANES = 128


def up(value, step):
    return -(-value // step) * step


def pack_kernel(n, jb, blk, s_ref, x_ref, *outs):
    b = s_ref[0]
    tokens = x_ref.shape[0]
    rows, cols = outs[0].shape[2:4]
    chans = x_ref.shape[1]
    for vg in range(2):
        for jz in range(jb):
            for t in range(n):
                start = ((vg * jb + jz) * n + t) * blk
                low = start // LANES * LANES
                high = min(up(start + blk, LANES), chans)
                wide = x_ref[:, low:high].astype(F32)
                if start != low:
                    wide = pltpu.roll(wide, high - low - (start - low), 1)
                piece = wide[:, :blk].astype(BF16).reshape(rows, cols, blk)
                for k in range(n):

                    @pl.when(lax.rem(b + k, n) == t)
                    def _():
                        outs[k][vg, jz] = piece


def place_rows(n, rl, b, xs, own, received):
    for vg in range(2):
        for i in range(rl):
            xs[vg, b * rl + i] = own[vg, 0, i].astype(F32)
            for k in range(1, n):
                src = lax.rem(b - k + n, n)
                xs[vg, src * rl + i] = received[k - 1][vg, 0, i].astype(F32)


def shifted(row):
    cols = row.shape[0]
    at = lax.broadcasted_iota(jnp.int32, row.shape, 0)
    prev = jnp.where(at == 0, 0.0, pltpu.roll(row, 1, 0))
    nxt = jnp.where(at == cols - 1, 0.0, pltpu.roll(row, cols - 1, 0))
    return prev, row, nxt


def conv_kernel(n, jb, rl, s_ref, own, *refs):
    received, (taps, glu, silu, slope, xs) = refs[: n - 1], refs[n - 1 :]
    b, tap_mask = s_ref[0], s_ref[1]
    jz = pl.program_id(0)
    place_rows(n, rl, b, xs, own, received)
    total = n * rl
    pre = []
    for vg in range(2):
        w = taps[(vg * jb + jz) ^ tap_mask].astype(F32)
        acc = [None] * total
        for r in range(total):
            parts = shifted(xs[vg, r])
            for i in range(3):
                to = r + 1 - i
                if 0 <= to < total:
                    for j in range(3):
                        term = w[3 * i + j : 3 * i + j + 1] * parts[j]
                        acc[to] = term if acc[to] is None else acc[to] + term
        pre.append([a + w[9:10] for a in acc])
    for r in range(total):
        rel = lax.rem(r // rl - b + n, n)
        values, gate = pre[0][r], pre[1][r]
        sigma = jax.nn.sigmoid(gate)
        act = gate * sigma
        cols = values.shape[0]
        spot = pl.ds(r % rl * cols, cols)
        glu[0, rel, spot, :] = (values * act).astype(BF16)
        silu[0, rel, spot, :] = act
        slope[0, rel, spot, :] = values * (sigma * (1.0 + gate * (1.0 - sigma)))


def load_weights(s_ref, copies, w_refs, w_buf, sems):
    own_core = s_ref[2]
    waits = []
    for k, (main, other) in enumerate(copies):
        def run(options, action, k=k):
            for src, slot in options:
                where = w_buf.at[k] if slot is None else w_buf.at[k, slot]
                getattr(pltpu.make_async_copy(src, where, sems.at[k]), action)()

        def both(action, main=main, other=other, run=run):
            if other is None:
                run(main(s_ref, w_refs), action)
                return
            @pl.when(own_core == 1)
            def _():
                run(main(s_ref, w_refs), action)

            @pl.when(own_core == 0)
            def _():
                run(other(s_ref, w_refs), action)

        both("start")
        waits.append(functools.partial(both, "wait"))
    return waits


def out_kernel(n, jb, copies, n_w, s_ref, glu, *refs):
    w_refs, outs, (w_buf, acc, sems) = refs[:n_w], refs[n_w : n_w + n], refs[n_w + n :]
    waits = load_weights(s_ref, copies, w_refs, w_buf, sems)
    tokens = glu.shape[2]
    for k in range(len(copies)):
        waits[k]()
        jz = s_ref[3] ^ k
        part = jnp.dot(
            glu[jz].reshape(n * tokens, glu.shape[3]),
            w_buf[k].reshape(glu.shape[3], w_buf.shape[3]),
            preferred_element_type=F32,
        )
        if k == 0:
            acc[...] = part
        else:
            acc[...] += part
    for k in range(n):
        outs[k][...] = acc[k * tokens : (k + 1) * tokens, :].astype(outs[k].dtype)


def grad_kernel(n, jb, rl, copies, n_w, s_ref, own, *refs):
    received = refs[: n - 1]
    taps, silu, slope = refs[n - 1 : n + 2]
    cots = refs[n + 2 : 2 * n + 2]
    w_refs = refs[2 * n + 2 : 2 * n + 2 + n_w]
    rest = refs[2 * n + 2 + n_w :]
    outs, (tap_grad, xs, dp, dh, w_buf, sems) = rest[:n], rest[n:]
    b, tap_mask = s_ref[0], s_ref[1]
    step = pl.program_id(0)
    jz = s_ref[3] ^ step

    @pl.when(step == 0)
    def _():
        load_weights(s_ref, copies, w_refs, w_buf, sems)

    for k in range(len(copies)):
        @pl.when(step == k)
        def _():
            wait_weights(s_ref, copies, w_refs, w_buf, sems, k)

    place_rows(n, rl, b, xs, own, received)
    total = n * rl
    tokens, blk = silu.shape[2:]
    cols = tokens // rl
    w_now = w_buf[step].reshape(blk, w_buf.shape[3])
    for k in range(n):
        d_glu = lax.dot_general(
            cots[k][...], w_now, (((1,), (1,)), ((), ())), preferred_element_type=F32
        )
        dp[0, k] = (d_glu * silu[0, k]).astype(BF16).astype(F32).reshape(rl, cols, blk)
        dp[1, k] = (d_glu * slope[0, k]).astype(BF16).astype(F32).reshape(rl, cols, blk)
    for vg in range(2):
        w = taps[(vg * jb + jz) ^ tap_mask].astype(F32)
        acc = [None] * total
        sums = [None] * 10
        for r in range(total):
            rel = lax.rem(r // rl - b + n, n)
            row = dp[vg, rel, r % rl]
            nxt_prev = shifted(row)
            sums[9] = row if sums[9] is None else sums[9] + row
            for i in range(3):
                to = r - 1 + i
                if 0 <= to < total:
                    x = xs[vg, to]
                    for j in range(3):
                        seen = nxt_prev[2 - j]
                        tap = 3 * i + j
                        term = w[tap : tap + 1] * seen
                        acc[to] = term if acc[to] is None else acc[to] + term
                        prod = x * seen
                        sums[tap] = prod if sums[tap] is None else sums[tap] + prod
        for r in range(total):
            rel = lax.rem(r // rl - b + n, n)
            dh[rel, vg, r % rl] = acc[r].astype(BF16)
        tap_grad[vg, 0, :10, :] = jnp.concatenate(
            [jnp.sum(s, axis=0, keepdims=True) for s in sums], axis=0
        )
    for k in range(n):
        for vg in range(2):
            outs[k][vg, 0] = dh[k, vg]


def wait_weights(s_ref, copies, w_refs, w_buf, sems, k):
    main, other = copies[k]

    def run(options):
        for src, slot in options:
            where = w_buf.at[k] if slot is None else w_buf.at[k, slot]
            pltpu.make_async_copy(src, where, sems.at[k]).wait()

    if other is None:
        run(main(s_ref, w_refs))
        return

    @pl.when(s_ref[2] == 1)
    def _():
        run(main(s_ref, w_refs))

    @pl.when(s_ref[2] == 0)
    def _():
        run(other(s_ref, w_refs))


def unpack_kernel(n, jb, blk, s_ref, *refs):
    ins, out, (held,) = refs[:n], refs[n], refs[n + 1 :]
    b = s_ref[0]
    rl, cols = ins[0].shape[2:4]
    for k in range(n):
        held[lax.rem(b - k + n, n)] = ins[k][...]
    for vg in range(2):
        for jz in range(jb):
            for t in range(n):
                start = ((vg * jb + jz) * n + t) * blk
                out[:, start : start + blk] = held[t, vg, jz].reshape(rl * cols, blk)


def body(hidden_in, tap_weights, tap_bias, w_out, cotangent):
    groups, shards, n = (lax.axis_size(a) for a in ("groups", "fsdp", "band"))
    images, rl, cols, chans = hidden_in.shape
    hidden = chans // 2
    blk = w_out.shape[0]
    jb = shards // n
    feats = w_out.shape[1]
    tokens = rl * cols
    g, f, b = (lax.axis_index(a) for a in ("groups", "fsdp", "band"))
    fast = n == 2 and groups == 2 and shards % 4 == 0 and shards & (shards - 1) == 0 and blk % 32 == 0
    assert images == 1 and shards % n == 0

    tap_block = jnp.concatenate(
        [tap_weights, tap_bias[None], jnp.zeros((6, tap_bias.shape[0]), BF16)], axis=0
    )
    if fast:
        scalars = jnp.stack([b, f, jnp.where(f % 2 == b, 1, 0), f // n, g]).astype(jnp.int32)
    else:
        scalars = jnp.stack([b, 0 * f, 0 * f + 1, 0 * f, g]).astype(jnp.int32)

    if fast:
        every = ("groups", "fsdp", "band")
        zr = jb

        def across(x, flip, name):
            pairs = [(s * n + t, (s ^ flip) * n + t) for s in range(shards) for t in range(n) if s % 2 == t]
            with jax.named_scope(name):
                return lax.ppermute(x, ("fsdp", "band"), pairs)

        def other_group(x, name):
            size = shards * n
            pairs = [
                (p * size + s * n + t, (1 - p) * size + s * n + t)
                for p in range(2) for s in range(shards) for t in range(n) if s % 2 == t
            ]
            with jax.named_scope(name):
                return lax.ppermute(x, every, pairs)

        half = lax.dynamic_slice_in_dim(w_out, g * (blk // 2), blk // 2, 0)
        mine = {0: half}
        flips = 1
        order = []
        bit = zr // 2
        while bit:
            order.append(bit)
            bit //= 2
        for bit in order:
            for k in list(mine):
                mine[k ^ bit] = across(mine[k], 2 * bit, f"wz{k ^ bit}")
        w_args, copies = [], []
        for k in range(zr):
            base = len(w_args)
            if k == 0:
                whole = w_out.reshape(2, blk // 2, feats)
                w_args += [whole, across(w_out, 1, "wc0").reshape(2, blk // 2, feats)]
                copies.append((
                    lambda s, w, i=base: [(w[i], None)],
                    lambda s, w, i=base + 1: [(w[i], None)],
                ))
            else:
                a, y = mine[k], other_group(mine[k], f"wy{k}")
                w_args += [a, y, across(a, 1, f"wca{k}"), across(y, 1, f"wcy{k}")]
                copies.append((
                    lambda s, w, i=base: [(w[i], s[4]), (w[i + 1], 1 - s[4])],
                    lambda s, w, i=base + 2: [(w[i], s[4]), (w[i + 1], 1 - s[4])],
                ))
        parts = 2
    else:
        w_all = lax.all_gather(w_out, "fsdp", axis=0, tiled=True).reshape(jb, n, 1, blk, feats)
        w_args = [lax.dynamic_index_in_dim(w_all, b, 1, keepdims=False)]
        copies = [(lambda s, w, k=k: [(w[0].at[k], None)], None) for k in range(jb)]
        parts = 1

    if fast:
        tap_all = lax.dynamic_slice_in_dim(tap_block, b * blk, blk, 1)[None]
        step = 1
        while step < shards:
            with jax.named_scope(f"tap{step}"):
                other = lax.ppermute(tap_all, "fsdp", [(i, i ^ step) for i in range(shards)])
            tap_all = jnp.concatenate([tap_all, other], axis=0)
            step *= 2
    else:
        tap_all = lax.all_gather(tap_block, "fsdp", axis=1, tiled=True)
        tap_all = tap_all.reshape(16, 2 * jb, n, blk)
        tap_all = lax.dynamic_index_in_dim(tap_all, b, 2, keepdims=False).transpose(1, 0, 2)

    vmem = pl.BlockSpec(memory_space=pltpu.VMEM)
    smem = pl.BlockSpec(memory_space=pltpu.SMEM)
    part_shape = (2, jb, rl, cols, blk)
    packed = pl.pallas_call(
        functools.partial(pack_kernel, n, jb, blk),
        out_shape=[jax.ShapeDtypeStruct(part_shape, BF16)] * n,
        in_specs=[smem, vmem],
        out_specs=[vmem] * n,
        name="pack",
    )(scalars, hidden_in.reshape(tokens, chans))
    def turn(x, k, name):
        with jax.named_scope(name):
            return lax.ppermute(x, "band", [(i, (i + k) % n) for i in range(n)])
    hid_in = [turn(packed[k], k, f"hid{k}") for k in range(1, n)]
    cot = cotangent.reshape(tokens, feats)
    cots = [cot] + [turn(cot, n - k, f"cot{k}") for k in range(1, n)]

    part_spec = pl.BlockSpec((2, 1, rl, cols, blk), lambda j, s: (0, j, 0, 0, 0))
    tap_spec = pl.BlockSpec((2 * jb, 16, blk), lambda j, s: (0, 0, 0))
    act_spec = pl.BlockSpec((1, n, tokens, blk), lambda j, s: (j, 0, 0, 0))
    act_shape = (jb, n, tokens, blk)
    glu, silu, slope = pl.pallas_call(
        functools.partial(conv_kernel, n, jb, rl),
        grid_spec=pltpu.PrefetchScalarGridSpec(
            num_scalar_prefetch=1,
            grid=(jb,),
            in_specs=[part_spec] * n + [tap_spec],
            out_specs=[act_spec] * 3,
            scratch_shapes=[pltpu.VMEM((2, n * rl, cols, blk), F32)],
        ),
        out_shape=[
            jax.ShapeDtypeStruct(act_shape, BF16),
            jax.ShapeDtypeStruct(act_shape, F32),
            jax.ShapeDtypeStruct(act_shape, F32),
        ],
        name="conv",
    )(scalars, packed[0], *hid_in, tap_all)

    any_spec = pl.BlockSpec(memory_space=pl.ANY)
    w_scratch = pltpu.VMEM((jb, parts, blk // parts, feats), BF16)
    partial_out = pl.pallas_call(
        functools.partial(out_kernel, n, jb, copies, len(w_args)),
        in_specs=[smem, vmem] + [any_spec] * len(w_args),
        out_specs=[vmem] * n,
        out_shape=[jax.ShapeDtypeStruct((tokens, feats), F32 if k == 0 else BF16) for k in range(n)],
        scratch_shapes=[w_scratch, pltpu.VMEM((n * tokens, feats), F32), pltpu.SemaphoreType.DMA((jb,))],
        name="project",
    )(scalars, glu, *w_args)
    block_out = partial_out[0]
    for k in range(1, n):
        block_out = block_out + turn(partial_out[k], k, f"bo{k}").astype(F32)
    block_out = block_out.astype(BF16)

    part_at = pl.BlockSpec((2, 1, rl, cols, blk), lambda j, s: (0, s[3] ^ j, 0, 0, 0))
    act_at = pl.BlockSpec((1, n, tokens, blk), lambda j, s: (s[3] ^ j, 0, 0, 0))
    cot_spec = pl.BlockSpec((tokens, feats), lambda j, s: (0, 0))
    grads = pl.pallas_call(
        functools.partial(grad_kernel, n, jb, rl, copies, len(w_args)),
        grid_spec=pltpu.PrefetchScalarGridSpec(
            num_scalar_prefetch=1,
            grid=(jb,),
            in_specs=[part_at] * n + [tap_spec, act_at, act_at] + [cot_spec] * n + [any_spec] * len(w_args),
            out_specs=[part_at] * n + [pl.BlockSpec((2, 1, 16, blk), lambda j, s: (0, s[3] ^ j, 0, 0))],
            scratch_shapes=[
                pltpu.VMEM((2, n * rl, cols, blk), F32),
                pltpu.VMEM((2, n, rl, cols, blk), F32),
                pltpu.VMEM((n, 2, rl, cols, blk), BF16),
                w_scratch,
                pltpu.SemaphoreType.DMA((jb,)),
            ],
        ),
        out_shape=[jax.ShapeDtypeStruct(part_shape, BF16)] * n + [jax.ShapeDtypeStruct((2, jb, 16, blk), F32)],
        name="grad",
    )(scalars, packed[0], *hid_in, tap_all, silu, slope, *cots, *w_args)
    d_parts, tap_grad = grads[:n], grads[n]
    d_recv = [turn(d_parts[k], k, f"dh{k}") for k in range(1, n)]
    d_hidden = pl.pallas_call(
        functools.partial(unpack_kernel, n, jb, blk),
        in_specs=[smem] + [vmem] * n,
        out_specs=vmem,
        out_shape=jax.ShapeDtypeStruct((tokens, chans), BF16),
        scratch_shapes=[pltpu.VMEM((n,) + part_shape, BF16)],
        name="unpack",
    )(scalars, d_parts[0], *d_recv)

    tap_grad = tap_grad.reshape(2 * jb, 16, blk)
    if fast:
        pieces = lax.all_to_all(tap_grad, "fsdp", 0, 0, tiled=True)
        mine_sum = jnp.sum(pieces, axis=0)
        theirs = turn(mine_sum, 1, "tg")
        first = jnp.where(b == 0, mine_sum, theirs)
        second = jnp.where(b == 0, theirs, mine_sum)
        share = jnp.concatenate([first, second], axis=1)
    else:
        spread = jnp.where(
            (jnp.arange(n) == b)[None, None, :, None], tap_grad.transpose(1, 0, 2)[:, :, None, :], 0.0
        ).reshape(16, chans)
        share = lax.psum(spread, "band")
        share = lax.psum_scatter(share, "fsdp", scatter_dimension=1, tiled=True)
    return (
        block_out.reshape(images, rl, cols, feats),
        d_hidden.reshape(hidden_in.shape),
        share[:9],
        share[9],
    )


def solution(mesh):
    placed = (
        P(("groups", "fsdp"), "band", None, None),
        P(None, "fsdp"),
        P("fsdp"),
        P("fsdp", None),
        P(("groups", "fsdp"), "band", None, None),
    )
    return jax.shard_map(
        body,
        mesh=mesh,
        in_specs=placed,
        out_specs=(
            P(("groups", "fsdp"), "band", None, None),
            P(("groups", "fsdp"), "band", None, None),
            P("groups", "fsdp"),
            P(("groups", "fsdp")),
        ),
        check_vma=False,
    )
```

time: 236 us -> 170 us (0.72)
  blocking collectives: 95.2 us -> 0 us
  starting transfers between devices: 11.1 us -> 47.9 us
  Pallas kernels: 0 us -> 35 us
  waiting for transfers between devices: 47.2 us -> 70.7 us
  matrix products: 21.6 us -> 0 us
  other arithmetic: 18.4 us -> 3.09 us
  between operations: 15.7 us -> 0.95 us
  local copies, waits for them, and re-layouts: 26.3 us -> 11.9 us
    ppermute x4 -> x21, waiting for transfers between devices: 0.01 us -> 70.7 us  [the longest x5 40.4 us: turn(): return lax.ppermute(x, 'band', [(i, (i + k) % n) for i in range(n)])]
    unnamed x2 -> x0, blocking collectives: 59.2 us -> none
    all_gather x1 -> x0, waiting for transfers between devices: 46.5 us -> none  [body(): piece = lax.all_gather(w_out, 'fsdp', axis=0, tiled=True)]
    pallas_call x0 -> x5, Pallas kernels: none -> 35 us  [the longest x1 14.3 us: body(): pl.pallas_call(functools.partial(grad_kernel, n, jb, rl, copies, len(w_ar...]
    ppermute x4 -> x21, starting transfers between devices: 11 us -> 43.1 us  [the longest x10 26.3 us: across(): return lax.ppermute(x, ('fsdp', 'band'), pairs)]
    all_gather x1 -> x0, blocking collectives: 25 us -> none  [body(): lax.all_gather(tap_weights, 'fsdp', axis=1, tiled=True)]
    dot_general x2 -> x0, matrix products: 21.6 us -> none  [the longest x1 10.8 us: body(): out_sum = jnp.dot(glu_flat, piece, preferred_element_type=jnp.float32)]
    psum x1 -> x0, blocking collectives: 11 us -> none  [body(): tap_grad, bias_grad = lax.psum((tap_grad, bias_grad), 'band')]
  transfers between devices with their start and end apart: 6 -> 22, of which waited for: 1 -> 8; matrix products, arithmetic and copies ran while one was open for 15% -> 6% of each run, Pallas kernels for 0% -> 10%
where the time goes in v1:
time: 170 us
  waiting for transfers between devices  70.7 us (42%)
  starting transfers between devices  47.9 us (28%)
  Pallas kernels  35 us (21%)
  local copies, waits for them, and re-layouts  11.9 us (7%)
  other arithmetic  3.09 us (2%)
    ppermute x5, waiting for transfers between devices, turn(): return lax.ppermute(x, 'band', [(i, (i + k) % n) for i in range(n)])  40.4 us
    ppermute x10, starting transfers between devices, across(): return lax.ppermute(x, ('fsdp', 'band'), pairs)  26.3 us
    pallas_call x1, Pallas kernels, body(): pl.pallas_call(functools.partial(grad_kernel, n, jb, rl, copies, len(w_ar...  14.3 us
    ppermute x10, waiting for transfers between devices, across(): return lax.ppermute(x, ('fsdp', 'band'), pairs)  13.1 us
    ppermute x3, waiting for transfers between devices, other_group(): return lax.ppermute(x, every, pairs)  10.1 us
    ppermute x3, starting transfers between devices, other_group(): return lax.ppermute(x, every, pairs)  9.58 us
    pallas_call x1, Pallas kernels, body(): pl.pallas_call(functools.partial(out_kernel, n, jb, copies, len(w_args)),...  7.18 us
    ppermute x3, waiting for transfers between devices, body(): lax.ppermute(tap_all, 'fsdp', [(i, i ^ step) for i in range(shards)])  7.04 us
  transfers between devices with their start and end apart: 22, of which 8 were waited for; matrix products, arithmetic and copies ran while one was open for 6% of the time, Pallas kernels for 10%

profile of v1, /device:TPU:0, one launch (start us, length us, event | category | flops | bytes accessed | tf_op | source)
XLA Modules:
  0.0 169.5 jit_solution(16647436222311695862)
XLA Ops:
  0.6 0.0 copy-start
  0.7 2.2 %constant_dynamic-slice_fusion = bf16[176,2240]{1,0:T(8,128)(2,1)} fusion(bf16[352,2240]{1,0:T(8,128)(2,1)} %param.8, s32[]{:T(128)S(6)} %select_n.37), kind=kLoop, calls=%fused_computation.14 | loop fusion | bytes 1576964 | tf_op jit(solution)/shard_map/dynamic_slice | solution.py:269
  2.9 6.0 %collective-permute-start.9 = (bf16[176,2240]{1,0:T(8,128)(2,1)}, bf16[176,2240]{1,0:T(8,128)(2,1)}, u32[]{:S(2)}, u32[]{:S(2)}) collective-permute-start(bf16[176,2240]{1,0:T(8,128)(2,1)} %constant_dynamic-slice_fusion), channel_id=1, source_target_pairs={{0,8},{3,11},{4,12},{7,15},{8,0},{11,3},{12,4},{15,7},{16,24},{19,... | collective-permute-start | bytes 2365448 | tf_op jit(solution)/shard_map/wz2/ppermute | solution.py:258
  8.9 0.1 pad.13.clone
  9.0 0.1 fusion.2
  9.1 0.1 collective-permute-start.1
  9.1 2.5 %collective-permute-start.4 = (bf16[352,2240]{1,0:T(8,128)(2,1)S(1)}, bf16[352,2240]{1,0:T(8,128)(2,1)S(1)}, u32[]{:S(2)}, u32[]{:S(2)}) collective-permute-start(bf16[352,2240]{1,0:T(8,128)(2,1)S(1)} %copy-done), channel_id=1, source_target_pairs={{0,2},{3,1},{4,6},{7,5},{8,10},{11,9},{12,14},{15,13},{16,18},{19,... | collective-permute-start | bytes 4730888 | tf_op jit(solution)/shard_map/wc0/ppermute | solution.py:258
  11.6 3.5 %collective-permute-start.5 = (bf16[176,2240]{1,0:T(8,128)(2,1)}, bf16[176,2240]{1,0:T(8,128)(2,1)}, u32[]{:S(2)}, u32[]{:S(2)}) collective-permute-start(bf16[176,2240]{1,0:T(8,128)(2,1)} %constant_dynamic-slice_fusion), channel_id=1, source_target_pairs={{0,4},{3,7},{4,0},{7,3},{8,12},{11,15},{12,8},{15,11},{16,20},{19,... | collective-permute-start | bytes 2365448 | tf_op jit(solution)/shard_map/wz1/ppermute | solution.py:258
  15.1 13.0 %collective-permute-done.9.refs_6_.refs_12_ = bf16[176,2240]{1,0:T(8,128)(2,1)} collective-permute-done((bf16[176,2240]{1,0:T(8,128)(2,1)}, bf16[176,2240]{1,0:T(8,128)(2,1)}, u32[]{:S(2)}, u32[]{:S(2)}) %collective-permute-start.9) | collective-permute-done | bytes 788512 | tf_op jit(solution)/shard_map/wz2/ppermute | solution.py:258
  28.2 2.8 %collective-permute-start.13 = (bf16[176,2240]{1,0:T(8,128)(2,1)}, bf16[176,2240]{1,0:T(8,128)(2,1)}, u32[]{:S(2)}, u32[]{:S(2)}) collective-permute-start(bf16[176,2240]{1,0:T(8,128)(2,1)} %collective-permute-done.9.refs_6_.refs_12_), channel_id=1, source_target_pairs={{0,4},{3,7},{4,0},{7,3},{8,12},{11,15},{12,8},{15,11},{16,20},{19,... | collective-permute-start | bytes 2365448 | tf_op jit(solution)/shard_map/wz3/ppermute | solution.py:258
  31.0 0.0 collective-permute-done.1
  31.0 1.2 collective-permute-start.2
  32.2 0.6 stack.23.s_ref
  32.8 4.0 %pack.1 = (bf16[2,4,2,64,352]{4,3,2,1,0:T(8,128)(2,1)}, bf16[2,4,2,64,352]{4,3,2,1,0:T(8,128)(2,1)}) custom-call(s32[5]{0:T(128)} %stack.23.s_ref, bf16[128,5632]{1,0:T(8,128)(2,1)} %bitcast.20), custom_call_target="tpu_custom_call" | custom-call | tf_op jit(solution)/shard_map/pack/pallas_call | solution.py:320
  36.8 0.0 collective-permute-start
  36.8 6.5 %collective-permute-done.2 = bf16[2,16,352]{2,1,0:T(8,128)(2,1)S(1)} collective-permute-done((bf16[2,16,352]{2,1,0:T(8,128)(2,1)S(1)}, bf16[2,16,352]{2,1,0:T(8,128)(2,1)S(1)}, u32[]{:S(2)}, u32[]{:S(2)}) %collective-permute-start.2) | collective-permute-done | bytes 22560 | tf_op jit(solution)/shard_map/tap2/ppermute | solution.py:309
  43.3 2.4 %collective-permute-start.3 = (bf16[4,16,352]{2,1,0:T(8,128)(2,1)S(1)}, bf16[4,16,352]{2,1,0:T(8,128)(2,1)S(1)}, u32[]{:S(2)}, u32[]{:S(2)}) collective-permute-start(bf16[4,16,352]{2,1,0:T(8,128)(2,1)S(1)} %pad_maximum_fusion.1), channel_id=1, source_target_pairs={{0,8},{2,10},{4,12},{6,14},{8,0},{10,2},{12,4},{14,6},{1,9},{3,11}... | collective-permute-start | bytes 135176 | tf_op jit(solution)/shard_map/tap4/ppermute | solution.py:309
  45.7 2.1 %copy.11 = bf16[128,2240]{0,1:T(8,128)(2,1)} copy(bf16[128,2240]{1,0:T(8,128)(2,1)} %bitcast.18) | data formatting | bytes 1146880 | tf_op jit(solution)/shard_map/reshape | solution.py:331
  47.9 0.5 collective-permute-done.3
  48.4 0.0 collective-permute-start.18
  48.4 0.0 collective-permute-done.5.refs_2_.refs_8_
  48.4 3.7 %collective-permute-start.6 = (bf16[176,2240]{1,0:T(8,128)(2,1)}, bf16[176,2240]{1,0:T(8,128)(2,1)}, u32[]{:S(2)}, u32[]{:S(2)}) collective-permute-start(bf16[176,2240]{1,0:T(8,128)(2,1)} %collective-permute-done.5.refs_2_.refs_8_), channel_id=1, source_target_pairs={{0,16},{3,19},{4,20},{7,23},{8,24},{11,27},{12,28},{15,31},{16,0},... | collective-permute-start | bytes 2365448 | tf_op jit(solution)/shard_map/wy1/ppermute | solution.py:267
  52.1 14.8 %collective-permute-done.18 = bf16[128,2240]{0,1:T(8,128)(2,1)S(1)} collective-permute-done((bf16[128,2240]{0,1:T(8,128)(2,1)}, bf16[128,2240]{0,1:T(8,128)(2,1)S(1)}, u32[]{:S(2)}, u32[]{:S(2)}) %collective-permute-start.18) | collective-permute-done | bytes 573472 | tf_op jit(solution)/shard_map/cot1/ppermute | solution.py:329
  66.9 2.2 %collective-permute-start.7 = (bf16[176,2240]{1,0:T(8,128)(2,1)}, bf16[176,2240]{1,0:T(8,128)(2,1)}, u32[]{:S(2)}, u32[]{:S(2)}) collective-permute-start(bf16[176,2240]{1,0:T(8,128)(2,1)} %collective-permute-done.5.refs_2_.refs_8_), channel_id=1, source_target_pairs={{0,2},{3,1},{4,6},{7,5},{8,10},{11,9},{12,14},{15,13},{16,18},{19,... | collective-permute-start | bytes 2365448 | tf_op jit(solution)/shard_map/wca1/ppermute | solution.py:258
  69.2 0.0 collective-permute-done.refs_0_
  69.2 3.4 %collective-permute-start.10 = (bf16[176,2240]{1,0:T(8,128)(2,1)}, bf16[176,2240]{1,0:T(8,128)(2,1)}, u32[]{:S(2)}, u32[]{:S(2)}) collective-permute-start(bf16[176,2240]{1,0:T(8,128)(2,1)} %collective-permute-done.9.refs_6_.refs_12_), channel_id=1, source_target_pairs={{0,16},{3,19},{4,20},{7,23},{8,24},{11,27},{12,28},{15,31},{16,0},... | collective-permute-start | bytes 2365448 | tf_op jit(solution)/shard_map/wy2/ppermute | solution.py:267
  72.6 0.0 collective-permute-done.13.refs_10_.refs_16_
  72.6 2.4 %collective-permute-start.14 = (bf16[176,2240]{1,0:T(8,128)(2,1)}, bf16[176,2240]{1,0:T(8,128)(2,1)}, u32[]{:S(2)}, u32[]{:S(2)}) collective-permute-start(bf16[176,2240]{1,0:T(8,128)(2,1)} %collective-permute-done.13.refs_10_.refs_16_), channel_id=1, source_target_pairs={{0,16},{3,19},{4,20},{7,23},{8,24},{11,27},{12,28},{15,31},{16,0},... | collective-permute-start | bytes 2365448 | tf_op jit(solution)/shard_map/wy3/ppermute | solution.py:267
  75.0 0.0 collective-permute-done.4
  75.1 1.3 collective-permute-start.11
  76.4 0.0 collective-permute-done.6.refs_3_.refs_9_
  76.4 1.3 collective-permute-start.15
  77.8 0.0 collective-permute-done.7.refs_4_.refs_10_
  77.8 2.2 %collective-permute-start.8 = (bf16[176,2240]{1,0:T(8,128)(2,1)}, bf16[176,2240]{1,0:T(8,128)(2,1)}, u32[]{:S(2)}, u32[]{:S(2)}) collective-permute-start(bf16[176,2240]{1,0:T(8,128)(2,1)} %collective-permute-done.6.refs_3_.refs_9_), channel_id=1, source_target_pairs={{0,2},{3,1},{4,6},{7,5},{8,10},{11,9},{12,14},{15,13},{16,18},{19,... | collective-permute-start | bytes 2365448 | tf_op jit(solution)/shard_map/wcy1/ppermute | solution.py:258
  80.0 3.6 %collective-permute-done.10.refs_7_.refs_13_ = bf16[176,2240]{1,0:T(8,128)(2,1)} collective-permute-done((bf16[176,2240]{1,0:T(8,128)(2,1)}, bf16[176,2240]{1,0:T(8,128)(2,1)}, u32[]{:S(2)}, u32[]{:S(2)}) %collective-permute-start.10) | collective-permute-done | bytes 788512 | tf_op jit(solution)/shard_map/wy2/ppermute | solution.py:267
  83.6 2.2 %collective-permute-start.12 = (bf16[176,2240]{1,0:T(8,128)(2,1)}, bf16[176,2240]{1,0:T(8,128)(2,1)}, u32[]{:S(2)}, u32[]{:S(2)}) collective-permute-start(bf16[176,2240]{1,0:T(8,128)(2,1)} %collective-permute-done.10.refs_7_.refs_13_), channel_id=1, source_target_pairs={{0,2},{3,1},{4,6},{7,5},{8,10},{11,9},{12,14},{15,13},{16,18},{19,... | collective-permute-start | bytes 2365448 | tf_op jit(solution)/shard_map/wcy2/ppermute | solution.py:258
  85.8 6.5 %collective-permute-done.14.refs_11_.refs_17_ = bf16[176,2240]{1,0:T(8,128)(2,1)} collective-permute-done((bf16[176,2240]{1,0:T(8,128)(2,1)}, bf16[176,2240]{1,0:T(8,128)(2,1)}, u32[]{:S(2)}, u32[]{:S(2)}) %collective-permute-start.14) | collective-permute-done | bytes 788512 | tf_op jit(solution)/shard_map/wy3/ppermute | solution.py:267
  92.3 2.2 %collective-permute-start.16 = (bf16[176,2240]{1,0:T(8,128)(2,1)}, bf16[176,2240]{1,0:T(8,128)(2,1)}, u32[]{:S(2)}, u32[]{:S(2)}) collective-permute-start(bf16[176,2240]{1,0:T(8,128)(2,1)} %collective-permute-done.14.refs_11_.refs_17_), channel_id=1, source_target_pairs={{0,2},{3,1},{4,6},{7,5},{8,10},{11,9},{12,14},{15,13},{16,18},{19,... | collective-permute-start | bytes 2365448 | tf_op jit(solution)/shard_map/wcy3/ppermute | solution.py:258
  94.6 0.7 pad_maximum_fusion.refs_1_
  95.2 2.1 %copy.12.refs_5_ = bf16[128,2240]{1,0:T(8,128)(2,1)} copy(bf16[128,2240]{0,1:T(8,128)(2,1)} %copy-done.6) | data formatting | bytes 1146880 | tf_op jit(solution)/shard_map/cot1/ppermute | solution.py:329
  97.3 6.4 %conv.1 = (bf16[4,2,128,352]{3,2,1,0:T(8,128)(2,1)}, f32[4,2,128,352]{3,2,1,0:T(8,128)}, f32[4,2,128,352]{3,2,1,0:T(8,128)}) custom-call(s32[5]{0:T(128)} %stack.23.s_ref, bf16[2,4,2,64,352]{4,3,2,1,0:T(8,128)(2,1)} %get-tuple-element.14.own, bf16[2,4,2,64,352]{4,3,2,1,0:T(8,128)(2,1)} %collective-permute-done.refs_0_, ...), custom_call_target="tpu_custom_call" | custom-call | tf_op jit(solution)/shard_map/conv/pallas_call | solution.py:338
  103.8 0.0 collective-permute-done.11.refs_8_.refs_14_
  103.8 0.0 collective-permute-done.8.refs_5_.refs_11_
  103.8 0.0 collective-permute-done.12.refs_9_.refs_15_
  103.8 0.0 collective-permute-done.15.refs_12_.refs_18_
  103.8 0.8 copy-done.2
  104.7 0.3 copy-done.3
  104.9 14.3 %grad.1 = (bf16[2,4,2,64,352]{4,3,2,1,0:T(8,128)(2,1)}, bf16[2,4,2,64,352]{4,3,2,1,0:T(8,128)(2,1)}, f32[2,4,16,352]{3,2,1,0:T(8,128)}) custom-call(s32[5]{0:T(128)} %stack.23.s_ref, bf16[2,4,2,64,352]{4,3,2,1,0:T(8,128)(2,1)} %get-tuple-element.14.own, bf16[2,4,2,64,352]{4,3,2,1,0:T(8,128)(2,1)} %collective-permute-done.refs_0_, ...), custom_call_target="tpu_custom_call" | custom-call | tf_op jit(solution)/shard_map/grad/pallas_call | solution.py:373
  119.2 4.8 %all-to-all-start = ((f32[8,16,352]{2,1,0:T(8,128)}), f32[8,16,352]{2,1,0:T(8,128)S(1)}, u32[]{:S(2)}, u32[]{:S(2)}) async-start(f32[8,16,352]{2,1,0:T(8,128)} %bitcast.23), calls=%async_computation | async-start | bytes 393216 | tf_op jit(solution)/shard_map/all_to_all | solution.py:404
  124.0 7.2 %project.1 = (f32[128,2240]{1,0:T(8,128)}, bf16[128,2240]{1,0:T(8,128)(2,1)}) custom-call(s32[5]{0:T(128)} %stack.23.s_ref, bf16[4,2,128,352]{3,2,1,0:T(8,128)(2,1)} %get-tuple-element.16.glu, bf16[2,176,2240]{2,1,0:T(8,128)(2,1)} %bitcast.15, bf16[2,176,2240]{2,1,0:T(8,128)(2,1)} %bitcast.17, bf16[176,2240]{1,0:T(8,128)(2,1)} %collective-permute-done.5.refs_2_.refs_8_, ...), custom_call_target="tpu_custom_call" | custom-call | tf_op jit(solution)/shard_map/project/pallas_call | solution.py:357
  131.2 0.0 copy-start.4
  131.2 1.5 copy.9
  132.7 1.4 collective-permute-start.17
  134.1 0.0 all-to-all-done
  134.1 0.7 collective-permute-start.20
  134.8 1.4 collective-permute-start.19
  136.2 12.9 %collective-permute-done.20 = f32[16,352]{1,0:T(8,128)S(1)} collective-permute-done((f32[16,352]{1,0:T(8,128)S(1)}, f32[16,352]{1,0:T(8,128)S(1)}, u32[]{:S(2)}, u32[]{:S(2)}) %collective-permute-start.20) | collective-permute-done | bytes 22560 | tf_op jit(solution)/shard_map/tg/ppermute | solution.py:329
  149.1 0.7 fusion.3
  149.8 0.7 slice_maximum_fusion
  150.5 1.3 copy.10
  151.8 0.9 add_convert_fusion
  152.7 12.8 %collective-permute-done.19.refs_1_ = bf16[2,4,2,64,352]{4,3,2,1,0:T(8,128)(2,1)S(1)} collective-permute-done((bf16[2,4,2,64,352]{4,3,2,1,0:T(8,128)(2,1)}, bf16[2,4,2,64,352]{4,3,2,1,0:T(8,128)(2,1)S(1)}, u32[]{:S(2)}, u32[]{:S(2)}) %collective-permute-start.19) | collective-permute-done | bytes 720928 | tf_op jit(solution)/shard_map/dh1/ppermute | solution.py:329
  165.5 0.9 copy-done.5
  166.4 3.2 %unpack.1 = bf16[128,5632]{1,0:T(8,128)(2,1)} custom-call(s32[5]{0:T(128)} %stack.23.s_ref, bf16[2,4,2,64,352]{4,3,2,1,0:T(8,128)(2,1)} %get-tuple-element.21.refs_0_, bf16[2,4,2,64,352]{4,3,2,1,0:T(8,128)(2,1)} %copy-done.5), custom_call_target="tpu_custom_call" | custom-call | tf_op jit(solution)/shard_map/unpack/pallas_call | solution.py:393
  (21 shorter events, 0.1 us)
Async XLA Ops:
  0.6 8.5 %copy-start = (bf16[352,2240]{1,0:T(8,128)(2,1)S(1)}, bf16[352,2240]{1,0:T(8,128)(2,1)}, u32[]{:S(2)}) copy-start(bf16[352,2240]{1,0:T(8,128)(2,1)} %param.8) | copy-start | bytes 4730884
  0.6 8.2 %copy-start.8 = (bf16[704]{0:T(1024)(128)(2,1)S(1)}, bf16[704]{0:T(1024)(128)(2,1)}, u32[]{:S(2)}) copy-start(bf16[704]{0:T(1024)(128)(2,1)} %param.7) | copy-start | bytes 4228
  0.7 8.3 %copy-start.7 = (bf16[9,704]{1,0:T(8,128)(2,1)S(1)}, bf16[9,704]{1,0:T(8,128)(2,1)}, u32[]{:S(2)}) copy-start(bf16[9,704]{1,0:T(8,128)(2,1)} %param.6) | copy-start | bytes 38020
  2.9 25.3 %collective-permute-start.9 = (bf16[176,2240]{1,0:T(8,128)(2,1)}, bf16[176,2240]{1,0:T(8,128)(2,1)}, u32[]{:S(2)}, u32[]{:S(2)}) collective-permute-start(bf16[176,2240]{1,0:T(8,128)(2,1)} %constant_dynamic-slice_fusion), channel_id=1, source_target_pairs={{0,8},{3,11},{4,12},{7,15},{8,0},{11,3},{12,4},{15,7},{16,24},{19,... | collective-permute-start | bytes 2365448 | tf_op jit(solution)/shard_map/wz2/ppermute | solution.py:258
  9.1 22.0 %collective-permute-start.1 = (bf16[1,16,352]{2,1,0:T(8,128)(2,1)S(1)}, bf16[1,16,352]{2,1,0:T(8,128)(2,1)S(1)}, u32[]{:S(2)}, u32[]{:S(2)}) collective-permute-start(bf16[1,16,352]{2,1,0:T(8,128)(2,1)S(1)} %fusion.2), channel_id=1, source_target_pairs={{0,2},{2,0},{4,6},{6,4},{8,10},{10,8},{12,14},{14,12},{1,3},{3,1},... | collective-permute-start | bytes 33800 | tf_op jit(solution)/shard_map/tap1/ppermute | solution.py:309
  9.1 65.9 %collective-permute-start.4 = (bf16[352,2240]{1,0:T(8,128)(2,1)S(1)}, bf16[352,2240]{1,0:T(8,128)(2,1)S(1)}, u32[]{:S(2)}, u32[]{:S(2)}) collective-permute-start(bf16[352,2240]{1,0:T(8,128)(2,1)S(1)} %copy-done), channel_id=1, source_target_pairs={{0,2},{3,1},{4,6},{7,5},{8,10},{11,9},{12,14},{15,13},{16,18},{19,... | collective-permute-start | bytes 4730888 | tf_op jit(solution)/shard_map/wc0/ppermute | solution.py:258
  11.6 36.7 %collective-permute-start.5 = (bf16[176,2240]{1,0:T(8,128)(2,1)}, bf16[176,2240]{1,0:T(8,128)(2,1)}, u32[]{:S(2)}, u32[]{:S(2)}) collective-permute-start(bf16[176,2240]{1,0:T(8,128)(2,1)} %constant_dynamic-slice_fusion), channel_id=1, source_target_pairs={{0,4},{3,7},{4,0},{7,3},{8,12},{11,15},{12,8},{15,11},{16,20},{19,... | collective-permute-start | bytes 2365448 | tf_op jit(solution)/shard_map/wz1/ppermute | solution.py:258
  28.2 44.4 %collective-permute-start.13 = (bf16[176,2240]{1,0:T(8,128)(2,1)}, bf16[176,2240]{1,0:T(8,128)(2,1)}, u32[]{:S(2)}, u32[]{:S(2)}) collective-permute-start(bf16[176,2240]{1,0:T(8,128)(2,1)} %collective-permute-done.9.refs_6_.refs_12_), channel_id=1, source_target_pairs={{0,4},{3,7},{4,0},{7,3},{8,12},{11,15},{12,8},{15,11},{16,20},{19,... | collective-permute-start | bytes 2365448 | tf_op jit(solution)/shard_map/wz3/ppermute | solution.py:258
  31.0 12.3 %collective-permute-start.2 = (bf16[2,16,352]{2,1,0:T(8,128)(2,1)S(1)}, bf16[2,16,352]{2,1,0:T(8,128)(2,1)S(1)}, u32[]{:S(2)}, u32[]{:S(2)}) collective-permute-start(bf16[2,16,352]{2,1,0:T(8,128)(2,1)S(1)} %pad_maximum_fusion.2), channel_id=1, source_target_pairs={{0,4},{2,6},{4,0},{6,2},{8,12},{10,14},{12,8},{14,10},{1,5},{3,7},... | collective-permute-start | bytes 67592 | tf_op jit(solution)/shard_map/tap2/ppermute | solution.py:309
  36.8 32.4 %collective-permute-start = (bf16[2,4,2,64,352]{4,3,2,1,0:T(8,128)(2,1)}, bf16[2,4,2,64,352]{4,3,2,1,0:T(8,128)(2,1)}, u32[]{:S(2)}, u32[]{:S(2)}) collective-permute-start(bf16[2,4,2,64,352]{4,3,2,1,0:T(8,128)(2,1)} %get-tuple-element.15), channel_id=1, source_target_pairs={{0,1},{1,0},{2,3},{3,2},{4,5},{5,4},{6,7},{7,6},{8,9},{9,8},{10,11... | collective-permute-start | bytes 2162696 | tf_op jit(solution)/shard_map/hid1/ppermute | solution.py:329
  43.3 5.1 %collective-permute-start.3 = (bf16[4,16,352]{2,1,0:T(8,128)(2,1)S(1)}, bf16[4,16,352]{2,1,0:T(8,128)(2,1)S(1)}, u32[]{:S(2)}, u32[]{:S(2)}) collective-permute-start(bf16[4,16,352]{2,1,0:T(8,128)(2,1)S(1)} %pad_maximum_fusion.1), channel_id=1, source_target_pairs={{0,8},{2,10},{4,12},{6,14},{8,0},{10,2},{12,4},{14,6},{1,9},{3,11}... | collective-permute-start | bytes 135176 | tf_op jit(solution)/shard_map/tap4/ppermute | solution.py:309
  48.4 18.5 %collective-permute-start.18 = (bf16[128,2240]{0,1:T(8,128)(2,1)}, bf16[128,2240]{0,1:T(8,128)(2,1)S(1)}, u32[]{:S(2)}, u32[]{:S(2)}) collective-permute-start(bf16[128,2240]{0,1:T(8,128)(2,1)} %copy.11), channel_id=1, source_target_pairs={{0,1},{1,0},{2,3},{3,2},{4,5},{5,4},{6,7},{7,6},{8,9},{9,8},{10,11... | collective-permute-start | bytes 1720328 | tf_op jit(solution)/shard_map/cot1/ppermute | solution.py:329
  48.4 28.0 %collective-permute-start.6 = (bf16[176,2240]{1,0:T(8,128)(2,1)}, bf16[176,2240]{1,0:T(8,128)(2,1)}, u32[]{:S(2)}, u32[]{:S(2)}) collective-permute-start(bf16[176,2240]{1,0:T(8,128)(2,1)} %collective-permute-done.5.refs_2_.refs_8_), channel_id=1, source_target_pairs={{0,16},{3,19},{4,20},{7,23},{8,24},{11,27},{12,28},{15,31},{16,0},... | collective-permute-start | bytes 2365448 | tf_op jit(solution)/shard_map/wy1/ppermute | solution.py:267
  66.9 9.5 %copy-start.6 = (bf16[128,2240]{0,1:T(8,128)(2,1)}, bf16[128,2240]{0,1:T(8,128)(2,1)S(1)}, u32[]{:S(2)}) copy-start(bf16[128,2240]{0,1:T(8,128)(2,1)S(1)} %collective-permute-done.18) | copy-start | bytes 1720324
  66.9 10.8 %collective-permute-start.7 = (bf16[176,2240]{1,0:T(8,128)(2,1)}, bf16[176,2240]{1,0:T(8,128)(2,1)}, u32[]{:S(2)}, u32[]{:S(2)}) collective-permute-start(bf16[176,2240]{1,0:T(8,128)(2,1)} %collective-permute-done.5.refs_2_.refs_8_), channel_id=1, source_target_pairs={{0,2},{3,1},{4,6},{7,5},{8,10},{11,9},{12,14},{15,13},{16,18},{19,... | collective-permute-start | bytes 2365448 | tf_op jit(solution)/shard_map/wca1/ppermute | solution.py:258
  69.2 14.5 %collective-permute-start.10 = (bf16[176,2240]{1,0:T(8,128)(2,1)}, bf16[176,2240]{1,0:T(8,128)(2,1)}, u32[]{:S(2)}, u32[]{:S(2)}) collective-permute-start(bf16[176,2240]{1,0:T(8,128)(2,1)} %collective-permute-done.9.refs_6_.refs_12_), channel_id=1, source_target_pairs={{0,16},{3,19},{4,20},{7,23},{8,24},{11,27},{12,28},{15,31},{16,0},... | collective-permute-start | bytes 2365448 | tf_op jit(solution)/shard_map/wy2/ppermute | solution.py:267
  72.6 19.7 %collective-permute-start.14 = (bf16[176,2240]{1,0:T(8,128)(2,1)}, bf16[176,2240]{1,0:T(8,128)(2,1)}, u32[]{:S(2)}, u32[]{:S(2)}) collective-permute-start(bf16[176,2240]{1,0:T(8,128)(2,1)} %collective-permute-done.13.refs_10_.refs_16_), channel_id=1, source_target_pairs={{0,16},{3,19},{4,20},{7,23},{8,24},{11,27},{12,28},{15,31},{16,0},... | collective-permute-start | bytes 2365448 | tf_op jit(solution)/shard_map/wy3/ppermute | solution.py:267
  75.0 28.7 %copy-start.1 = (bf16[352,2240]{1,0:T(8,128)(2,1)}, bf16[352,2240]{1,0:T(8,128)(2,1)S(1)}, u32[]{:S(2)}) copy-start(bf16[352,2240]{1,0:T(8,128)(2,1)S(1)} %collective-permute-done.4) | copy-start | bytes 4730884
  75.1 28.7 %collective-permute-start.11 = (bf16[176,2240]{1,0:T(8,128)(2,1)}, bf16[176,2240]{1,0:T(8,128)(2,1)S(1)}, u32[]{:S(2)}, u32[]{:S(2)}) collective-permute-start(bf16[176,2240]{1,0:T(8,128)(2,1)} %collective-permute-done.9.refs_6_.refs_12_), channel_id=1, source_target_pairs={{0,2},{3,1},{4,6},{7,5},{8,10},{11,9},{12,14},{15,13},{16,18},{19,... | collective-permute-start | bytes 2365448 | tf_op jit(solution)/shard_map/wca2/ppermute | solution.py:258
  76.4 27.4 %collective-permute-start.15 = (bf16[176,2240]{1,0:T(8,128)(2,1)}, bf16[176,2240]{1,0:T(8,128)(2,1)S(1)}, u32[]{:S(2)}, u32[]{:S(2)}) collective-permute-start(bf16[176,2240]{1,0:T(8,128)(2,1)} %collective-permute-done.13.refs_10_.refs_16_), channel_id=1, source_target_pairs={{0,2},{3,1},{4,6},{7,5},{8,10},{11,9},{12,14},{15,13},{16,18},{19,... | collective-permute-start | bytes 2365448 | tf_op jit(solution)/shard_map/wca3/ppermute | solution.py:258
  77.8 26.0 %collective-permute-start.8 = (bf16[176,2240]{1,0:T(8,128)(2,1)}, bf16[176,2240]{1,0:T(8,128)(2,1)}, u32[]{:S(2)}, u32[]{:S(2)}) collective-permute-start(bf16[176,2240]{1,0:T(8,128)(2,1)} %collective-permute-done.6.refs_3_.refs_9_), channel_id=1, source_target_pairs={{0,2},{3,1},{4,6},{7,5},{8,10},{11,9},{12,14},{15,13},{16,18},{19,... | collective-permute-start | bytes 2365448 | tf_op jit(solution)/shard_map/wcy1/ppermute | solution.py:258
  83.6 20.2 %collective-permute-start.12 = (bf16[176,2240]{1,0:T(8,128)(2,1)}, bf16[176,2240]{1,0:T(8,128)(2,1)}, u32[]{:S(2)}, u32[]{:S(2)}) collective-permute-start(bf16[176,2240]{1,0:T(8,128)(2,1)} %collective-permute-done.10.refs_7_.refs_13_), channel_id=1, source_target_pairs={{0,2},{3,1},{4,6},{7,5},{8,10},{11,9},{12,14},{15,13},{16,18},{19,... | collective-permute-start | bytes 2365448 | tf_op jit(solution)/shard_map/wcy2/ppermute | solution.py:258
  92.3 11.5 %collective-permute-start.16 = (bf16[176,2240]{1,0:T(8,128)(2,1)}, bf16[176,2240]{1,0:T(8,128)(2,1)}, u32[]{:S(2)}, u32[]{:S(2)}) collective-permute-start(bf16[176,2240]{1,0:T(8,128)(2,1)} %collective-permute-done.14.refs_11_.refs_17_), channel_id=1, source_target_pairs={{0,2},{3,1},{4,6},{7,5},{8,10},{11,9},{12,14},{15,13},{16,18},{19,... | collective-permute-start | bytes 2365448 | tf_op jit(solution)/shard_map/wcy3/ppermute | solution.py:258
  103.8 0.9 copy-start.2
  103.8 1.1 copy-start.3
  119.2 14.9 %all-to-all-start = ((f32[8,16,352]{2,1,0:T(8,128)}), f32[8,16,352]{2,1,0:T(8,128)S(1)}, u32[]{:S(2)}, u32[]{:S(2)}) async-start(f32[8,16,352]{2,1,0:T(8,128)} %bitcast.23), calls=%async_computation | async-start | bytes 393216 | tf_op jit(solution)/shard_map/all_to_all | solution.py:404
  131.2 20.6 %copy-start.4 = (f32[128,2240]{1,0:T(8,128)S(1)}, f32[128,2240]{1,0:T(8,128)}, u32[]{:S(2)}) copy-start(f32[128,2240]{1,0:T(8,128)} %get-tuple-element.17) | copy-start | bytes 3440644
  132.7 17.8 %collective-permute-start.17 = (bf16[128,2240]{0,1:T(8,128)(2,1)S(1)}, bf16[128,2240]{0,1:T(8,128)(2,1)}, u32[]{:S(2)}, u32[]{:S(2)}) collective-permute-start(bf16[128,2240]{0,1:T(8,128)(2,1)S(1)} %copy.9), channel_id=1, source_target_pairs={{0,1},{1,0},{2,3},{3,2},{4,5},{5,4},{6,7},{7,6},{8,9},{9,8},{10,11... | collective-permute-start | bytes 1720328 | tf_op jit(solution)/shard_map/bo1/ppermute | solution.py:329
  134.1 15.0 %collective-permute-start.20 = (f32[16,352]{1,0:T(8,128)S(1)}, f32[16,352]{1,0:T(8,128)S(1)}, u32[]{:S(2)}, u32[]{:S(2)}) collective-permute-start(f32[16,352]{1,0:T(8,128)S(1)} %reduce_sum.9), channel_id=1, source_target_pairs={{0,1},{1,0},{2,3},{3,2},{4,5},{5,4},{6,7},{7,6},{8,9},{9,8},{10,11... | collective-permute-start | bytes 67592 | tf_op jit(solution)/shard_map/tg/ppermute | solution.py:329
  134.8 30.6 %collective-permute-start.19 = (bf16[2,4,2,64,352]{4,3,2,1,0:T(8,128)(2,1)}, bf16[2,4,2,64,352]{4,3,2,1,0:T(8,128)(2,1)S(1)}, u32[]{:S(2)}, u32[]{:S(2)}) collective-permute-start(bf16[2,4,2,64,352]{4,3,2,1,0:T(8,128)(2,1)} %get-tuple-element.22), channel_id=1, source_target_pairs={{0,1},{1,0},{2,3},{3,2},{4,5},{5,4},{6,7},{7,6},{8,9},{9,8},{10,11... | collective-permute-start | bytes 2162696 | tf_op jit(solution)/shard_map/dh1/ppermute | solution.py:329
  165.5 0.9 copy-start.5

commit v2 on v1

v2 whole, which is shorter than its diff:
```python
import functools

import jax
import jax.numpy as jnp
from jax import lax
from jax.experimental import pallas as pl
from jax.experimental.pallas import tpu as pltpu
from jax.sharding import PartitionSpec as P


F32 = jnp.float32
BF16 = jnp.bfloat16
LANES = 128


def up(value, step):
    return -(-value // step) * step


def pack_kernel(n, jb, blk, s_ref, x_ref, *outs):
    b = s_ref[0]
    rows, cols = outs[0].shape[2:4]
    chans = x_ref.shape[1]
    for vg in range(2):
        for jz in range(jb):
            for t in range(n):
                start = ((vg * jb + jz) * n + t) * blk
                low = start // LANES * LANES
                high = min(up(start + blk, LANES), chans)
                wide = x_ref[:, low:high].astype(F32)
                if start != low:
                    wide = pltpu.roll(wide, high - low - (start - low), 1)
                piece = wide[:, :blk].astype(BF16).reshape(rows, cols, blk)
                for k in range(n):

                    @pl.when(lax.rem(b + k, n) == t)
                    def _():
                        outs[k][vg, jz] = piece


def place_rows(n, rl, b, xs, own, received):
    for vg in range(2):
        for i in range(rl):
            xs[vg, b * rl + i] = own[vg, 0, i].astype(F32)
            for k in range(1, n):
                src = lax.rem(b - k + n, n)
                xs[vg, src * rl + i] = received[k - 1][vg, 0, i].astype(F32)


def shifted(row):
    cols = row.shape[0]
    at = lax.broadcasted_iota(jnp.int32, row.shape, 0)
    prev = jnp.where(at == 0, 0.0, pltpu.roll(row, 1, 0))
    nxt = jnp.where(at == cols - 1, 0.0, pltpu.roll(row, cols - 1, 0))
    return prev, row, nxt


def lane_tiles(blk):
    return [pl.ds(low, min(LANES, blk - low)) for low in range(0, blk, LANES)]


def conv_kernel(n, jb, rl, s_ref, own, *refs):
    received, (taps, glu, silu, slope, xs, pres) = refs[: n - 1], refs[n - 1 :]
    b, tap_mask = s_ref[0], s_ref[1]
    jz = pl.program_id(0)
    place_rows(n, rl, b, xs, own, received)
    total = n * rl
    cols, blk = own.shape[3:]
    for lanes in lane_tiles(blk):
        for vg in range(2):
            w = taps[(vg * jb + jz) ^ tap_mask, :, lanes].astype(F32)
            acc = [None] * total
            for r in range(total):
                parts = shifted(xs[vg, r, :, lanes])
                for i in range(3):
                    to = r + 1 - i
                    if 0 <= to < total:
                        term = sum(w[3 * i + j : 3 * i + j + 1] * parts[j] for j in range(3))
                        acc[to] = term + w[9:10] if acc[to] is None else acc[to] + term
                done = [r - 1] if r < total - 1 else [r - 1, r]
                for at in done:
                    if at < 0:
                        continue
                    if vg == 0:
                        pres[at] = acc[at] if acc[at].shape[1] == LANES else jnp.pad(
                            acc[at], ((0, 0), (0, LANES - acc[at].shape[1]))
                        )
                        continue
                    values, gate = pres[at][:, : acc[at].shape[1]], acc[at]
                    rel = lax.rem(at // rl - b + n, n)
                    sigma = jax.nn.sigmoid(gate)
                    act = gate * sigma
                    spot = pl.ds(at % rl * cols, cols)
                    glu[0, rel, spot, lanes] = (values * act).astype(BF16)
                    silu[0, rel, spot, lanes] = act
                    slope[0, rel, spot, lanes] = values * (sigma * (1.0 + gate * (1.0 - sigma)))


def move_weights(action, s_ref, copy, at, w_refs, w_buf, sems):
    def run(source):
        for src, slot in source(s_ref, w_refs):
            where = w_buf.at[at] if slot is None else w_buf.at[at, slot]
            getattr(pltpu.make_async_copy(src, where, sems.at[at]), action)()

    main, other = copy
    if other is None:
        run(main)
        return

    @pl.when(s_ref[2] == 1)
    def _():
        run(main)

    @pl.when(s_ref[2] == 0)
    def _():
        run(other)


def out_kernel(n, blocks, copies, n_w, first, last, s_ref, glu, *refs):
    before, refs = (None, refs) if first else (refs[0], refs[1:])
    w_refs, refs = refs[:n_w], refs[n_w:]
    outs, (w_buf, sems) = refs[:-2], refs[-2:]
    acc, outs = (outs[-1], outs[:-1]) if last else (outs[0], ())
    for at in range(len(blocks)):
        move_weights("start", s_ref, copies[at], at, w_refs, w_buf, sems)
    tokens, blk = glu.shape[2:]
    for at, k in enumerate(blocks):
        move_weights("wait", s_ref, copies[at], at, w_refs, w_buf, sems)
        part = jnp.dot(
            glu[s_ref[3] ^ k].reshape(n * tokens, blk),
            w_buf[at].reshape(blk, w_buf.shape[3]),
            preferred_element_type=F32,
        )
        if at == 0:
            acc[...] = part if before is None else before[...] + part
        else:
            acc[...] += part
    for k, out in enumerate(outs):
        out[...] = acc[k * tokens : (k + 1) * tokens, :].astype(out.dtype)


def grad_kernel(n, jb, rl, first_k, copies, n_w, aliased, s_ref, own, *refs):
    received, refs = refs[: n - 1], refs[n - 1 :]
    (taps, silu, slope), refs = refs[:3], refs[3:]
    cots, refs = refs[:n], refs[n:]
    w_refs, refs = refs[:n_w], refs[n_w + aliased :]
    outs, (tap_grad, xs, dp, dh, cot_all, w_buf, sems, cot_sems) = refs[:n], refs[n:]
    b, tap_mask = s_ref[0], s_ref[1]
    step = pl.program_id(0)
    jz = s_ref[3] ^ (step + first_k)
    tokens, blk = silu.shape[2:]
    cols = tokens // rl
    total = n * rl

    def move_cots(action):
        for k in range(n):
            where = cot_all.at[pl.ds(k * tokens, tokens)]
            getattr(pltpu.make_async_copy(cots[k], where, cot_sems.at[k]), action)()

    @pl.when(step == 0)
    def _():
        move_cots("start")
        for at in range(len(copies)):
            move_weights("start", s_ref, copies[at], at, w_refs, w_buf, sems)

    place_rows(n, rl, b, xs, own, received)

    @pl.when(step == 0)
    def _():
        move_cots("wait")

    for at in range(len(copies)):
        @pl.when(step == at)
        def _():
            move_weights("wait", s_ref, copies[at], at, w_refs, w_buf, sems)

    d_glu = lax.dot_general(
        cot_all[...],
        w_buf[step].reshape(blk, w_buf.shape[3]),
        (((1,), (1,)), ((), ())),
        preferred_element_type=F32,
    ).reshape(n, tokens, blk)
    dp[0] = (d_glu * silu[0]).astype(BF16).astype(F32).reshape(n, rl, cols, blk)
    dp[1] = (d_glu * slope[0]).astype(BF16).astype(F32).reshape(n, rl, cols, blk)

    def fold(value):
        return jnp.sum(value.reshape(cols // 8, 8, value.shape[1]), axis=0)

    for vg in range(2):
        for lanes in lane_tiles(blk):
            w = taps[(vg * jb + jz) ^ tap_mask, :, lanes].astype(F32)
            acc = [None] * total
            sums = [None] * 10
            for r in range(total):
                row = dp[vg, lax.rem(r // rl - b + n, n), r % rl, :, lanes]
                seen = shifted(row)
                part = fold(row)
                sums[9] = part if sums[9] is None else sums[9] + part
                for i in range(3):
                    to = r - 1 + i
                    if not 0 <= to < total:
                        continue
                    x = xs[vg, to, :, lanes]
                    term = sum(w[3 * i + j : 3 * i + j + 1] * seen[2 - j] for j in range(3))
                    acc[to] = term if acc[to] is None else acc[to] + term
                    for j in range(3):
                        part = fold(x * seen[2 - j])
                        tap = 3 * i + j
                        sums[tap] = part if sums[tap] is None else sums[tap] + part
                for to in [r - 1] if r < total - 1 else [r - 1, r]:
                    if to >= 0:
                        rel = lax.rem(to // rl - b + n, n)
                        dh[rel, vg, to % rl, :, lanes] = acc[to].astype(BF16)
            tap_grad[vg, 0, :10, lanes] = jnp.concatenate(
                [jnp.sum(v, axis=0, keepdims=True) for v in sums], axis=0
            )
    for k in range(n):
        for vg in range(2):
            outs[k][vg, 0] = dh[k, vg]


def unpack_kernel(n, jb, blk, sizes, s_ref, *refs):
    ins, out, held = refs[:-2], refs[-2], refs[-1]
    b = s_ref[0]
    rl, cols = ins[0].shape[2:4]
    done = 0
    for c, size in enumerate(sizes):
        for k in range(n):
            for at in range(size):
                held[lax.rem(b - k + n, n), :, s_ref[3] ^ (done + at)] = ins[c * n + k][:, at]
        done += size
    for vg in range(2):
        for jz in range(jb):
            for t in range(n):
                start = ((vg * jb + jz) * n + t) * blk
                out[:, start : start + blk] = held[t, vg, jz].reshape(rl * cols, blk)


def unit(hidden_in, tap_weights, tap_bias, w_out, cotangent):
    groups, shards, n = (lax.axis_size(a) for a in ("groups", "fsdp", "band"))
    images, rl, cols, chans = hidden_in.shape
    blk = w_out.shape[0]
    jb = shards // n
    feats = w_out.shape[1]
    tokens = rl * cols
    g, f, b = (lax.axis_index(a) for a in ("groups", "fsdp", "band"))
    fast = n == 2 and groups == 2 and shards % 4 == 0 and shards & (shards - 1) == 0 and blk % 32 == 0
    assert images == 1 and shards % n == 0

    tap_block = jnp.concatenate(
        [tap_weights, tap_bias[None], jnp.zeros((6, tap_bias.shape[0]), BF16)], axis=0
    )
    if fast:
        scalars = jnp.stack([b, f, jnp.where(f % 2 == b, 1, 0), f // n, g]).astype(jnp.int32)
    else:
        scalars = jnp.stack([b, 0 * f, 0 * f + 1, 0 * f, g]).astype(jnp.int32)

    if fast:
        every = ("groups", "fsdp", "band")
        zr = jb

        def across(x, flip):
            pairs = [
                (s * n + t, (s ^ flip) * n + t)
                for s in range(shards) for t in range(n) if flip == 1 or s % 2 == t
            ]
            return lax.ppermute(x, ("fsdp", "band"), pairs)

        def other_group(x):
            size = shards * n
            pairs = [
                (p * size + s * n + t, (1 - p) * size + s * n + t)
                for p in range(2) for s in range(shards) for t in range(n) if s % 2 == t
            ]
            return lax.ppermute(x, every, pairs)

        half = lax.dynamic_slice_in_dim(w_out, g * (blk // 2), blk // 2, 0)
        mine = {0: half}
        order = []
        bit = zr // 2
        while bit:
            order.append(bit)
            bit //= 2
        for bit in order:
            for k in list(mine):
                mine[k ^ bit] = across(mine[k], 2 * bit)
        w_parts = []
        for k in range(zr):
            if k == 0:
                w_parts.append(([w.reshape(2, blk // 2, feats) for w in (w_out, across(w_out, 1))], False))
            else:
                a, y = mine[k], other_group(mine[k])
                w_parts.append(([a, y, across(a, 1), across(y, 1)], True))
        parts = 2
    else:
        w_all = lax.all_gather(w_out, "fsdp", axis=0, tiled=True).reshape(jb, n, 1, blk, feats)
        w_args = [lax.dynamic_index_in_dim(w_all, b, 1, keepdims=False)]
        copies = [(lambda s, w, k=k: [(w[0].at[k], None)], None) for k in range(jb)]
        parts = 1

    if fast:
        tap_all = lax.dynamic_slice_in_dim(tap_block, b * blk, blk, 1)[None]
        step = 1
        while step < shards:
            other = lax.ppermute(tap_all, "fsdp", [(i, i ^ step) for i in range(shards)])
            tap_all = jnp.concatenate([tap_all, other], axis=0)
            step *= 2
    else:
        tap_all = lax.all_gather(tap_block, "fsdp", axis=1, tiled=True)
        tap_all = tap_all.reshape(16, 2 * jb, n, blk)
        tap_all = lax.dynamic_index_in_dim(tap_all, b, 2, keepdims=False).transpose(1, 0, 2)

    vmem = pl.BlockSpec(memory_space=pltpu.VMEM)
    smem = pl.BlockSpec(memory_space=pltpu.SMEM)
    part_shape = (2, jb, rl, cols, blk)
    packed = pl.pallas_call(
        functools.partial(pack_kernel, n, jb, blk),
        out_shape=[jax.ShapeDtypeStruct(part_shape, BF16)] * n,
        in_specs=[smem, vmem],
        out_specs=[vmem] * n,
        name="pack",
    )(scalars, hidden_in.reshape(tokens, chans))

    def turn(x, k):
        return lax.ppermute(x, "band", [(i, (i + k) % n) for i in range(n)])

    hid_in = [turn(packed[k], k) for k in range(1, n)]
    cots = [cotangent] + [turn(cotangent, n - k) for k in range(1, n)]
    cots = [c.reshape(tokens, feats) for c in cots]

    part_spec = pl.BlockSpec((2, 1, rl, cols, blk), lambda j, s: (0, j, 0, 0, 0))
    tap_spec = pl.BlockSpec((2 * jb, 16, blk), lambda j, s: (0, 0, 0))
    act_spec = pl.BlockSpec((1, n, tokens, blk), lambda j, s: (j, 0, 0, 0))
    act_shape = (jb, n, tokens, blk)
    glu, silu, slope = pl.pallas_call(
        functools.partial(conv_kernel, n, jb, rl),
        grid_spec=pltpu.PrefetchScalarGridSpec(
            num_scalar_prefetch=1,
            grid=(jb,),
            in_specs=[part_spec] * n + [tap_spec],
            out_specs=[act_spec] * 3,
            scratch_shapes=[
                pltpu.VMEM((2, n * rl, cols, blk), F32),
                pltpu.VMEM((n * rl, cols, LANES), F32),
            ],
        ),
        out_shape=[
            jax.ShapeDtypeStruct(act_shape, BF16),
            jax.ShapeDtypeStruct(act_shape, F32),
            jax.ShapeDtypeStruct(act_shape, F32),
        ],
        name="conv",
    )(scalars, packed[0], *hid_in, tap_all)

    any_spec = pl.BlockSpec(memory_space=pl.ANY)
    chunks, done = [], 0
    for size in CHUNKS if fast and sum(CHUNKS) == jb else (jb,):
        chunks.append(range(done, done + size))
        done += size

    def weights_of(blocks):
        if not fast:
            return w_args, copies
        args, moves = [], []
        for k in blocks:
            arrays, halves = w_parts[k]
            base = len(args)
            args += arrays
            if halves:
                moves.append((
                    lambda s, w, i=base: [(w[i], s[4]), (w[i + 1], 1 - s[4])],
                    lambda s, w, i=base + 2: [(w[i], s[4]), (w[i + 1], 1 - s[4])],
                ))
            else:
                moves.append((
                    lambda s, w, i=base: [(w[i], None)],
                    lambda s, w, i=base + 1: [(w[i], None)],
                ))
        return args, moves

    partial = None
    for c, blocks in enumerate(chunks):
        args, moves = weights_of(blocks)
        first, last = c == 0, c == len(chunks) - 1
        shapes = [jax.ShapeDtypeStruct((tokens, feats), F32 if k == 0 else BF16) for k in range(n)]
        total_shape = jax.ShapeDtypeStruct((n * tokens, feats), F32)
        scratch = [
            pltpu.VMEM((len(blocks), parts, blk // parts, feats), BF16),
            pltpu.SemaphoreType.DMA((len(blocks),)),
        ]
        if last:
            scratch = [pltpu.VMEM((n * tokens, feats), F32)] + scratch
        partial = pl.pallas_call(
            functools.partial(out_kernel, n, blocks, moves, len(args), first, last),
            in_specs=[smem] + [vmem] * (1 if first else 2) + [any_spec] * len(args),
            out_specs=[vmem] * n if last else vmem,
            out_shape=shapes if last else total_shape,
            scratch_shapes=scratch,
        )(scalars, glu, *([] if first else [partial]), *args)
    partial = [p.reshape(cotangent.shape) for p in partial]
    block_out = partial[0]
    for k in range(1, n):
        block_out = block_out + turn(partial[k], k).astype(F32)
    block_out = block_out.astype(BF16)

    tap_grad, d_parts = None, []
    for blocks in chunks:
        args, moves = weights_of(blocks)
        at = lambda j, s, lo=blocks[0]: s[3] ^ (j + lo)
        part_at = pl.BlockSpec((2, 1, rl, cols, blk), lambda j, s, at=at: (0, at(j, s), 0, 0, 0))
        act_at = pl.BlockSpec((1, n, tokens, blk), lambda j, s, at=at: (at(j, s), 0, 0, 0))
        aliased = 0 if tap_grad is None else 1
        outs = pl.pallas_call(
            functools.partial(grad_kernel, n, jb, rl, blocks[0], moves, len(args), aliased),
            grid_spec=pltpu.PrefetchScalarGridSpec(
                num_scalar_prefetch=1,
                grid=(len(blocks),),
                in_specs=[part_at] * n + [tap_spec, act_at, act_at] + [any_spec] * (n + len(args) + aliased),
                out_specs=[part_spec] * n
                + [pl.BlockSpec((2, 1, 16, blk), lambda j, s, at=at: (0, at(j, s), 0, 0))],
                scratch_shapes=[
                    pltpu.VMEM((2, n * rl, cols, blk), F32),
                    pltpu.VMEM((2, n, rl, cols, blk), F32),
                    pltpu.VMEM((n, 2, rl, cols, blk), BF16),
                    pltpu.VMEM((n * tokens, feats), BF16),
                    pltpu.VMEM((len(blocks), parts, blk // parts, feats), BF16),
                    pltpu.SemaphoreType.DMA((len(blocks),)),
                    pltpu.SemaphoreType.DMA((n,)),
                ],
            ),
            out_shape=[jax.ShapeDtypeStruct((2, len(blocks), rl, cols, blk), BF16)] * n
            + [jax.ShapeDtypeStruct((2, jb, 16, blk), F32)],
            input_output_aliases={4 + 2 * n + len(args): n} if aliased else {},
        )(
            scalars, packed[0], *hid_in, tap_all, silu, slope, *cots, *args,
            *([tap_grad] if aliased else []),
        )
        tap_grad = outs[n]
        d_parts += [outs[0]] + [turn(outs[k], k) for k in range(1, n)]
    d_hidden = pl.pallas_call(
        functools.partial(unpack_kernel, n, jb, blk, [len(c) for c in chunks]),
        in_specs=[smem] + [vmem] * len(d_parts),
        out_specs=vmem,
        out_shape=jax.ShapeDtypeStruct((tokens, chans), BF16),
        scratch_shapes=[pltpu.VMEM((n,) + part_shape, BF16)],
        name="unpack",
    )(scalars, *d_parts)

    tap_grad = tap_grad.reshape(2 * jb, 16, blk)
    if fast:
        pieces = lax.all_to_all(tap_grad, "fsdp", 0, 0, tiled=True)
        mine_sum = jnp.sum(pieces, axis=0)
        theirs = turn(mine_sum, 1)
        first = jnp.where(b == 0, mine_sum, theirs)
        second = jnp.where(b == 0, theirs, mine_sum)
        share = jnp.concatenate([first, second], axis=1)
    else:
        spread = jnp.where(
            (jnp.arange(n) == b)[None, None, :, None], tap_grad.transpose(1, 0, 2)[:, :, None, :], 0.0
        ).reshape(16, chans)
        share = lax.psum(spread, "band")
        share = lax.psum_scatter(share, "fsdp", scatter_dimension=1, tiled=True)
    return (
        block_out,
        d_hidden.reshape(hidden_in.shape),
        share[:9],
        share[9],
    )


CHUNKS = (3, 1)


def solution(mesh):
    placed = (
        P(("groups", "fsdp"), "band", None, None),
        P(None, "fsdp"),
        P("fsdp"),
        P("fsdp", None),
        P(("groups", "fsdp"), "band", None, None),
    )
    return jax.shard_map(
        unit,
        mesh=mesh,
        in_specs=placed,
        out_specs=(
            P(("groups", "fsdp"), "band", None, None),
            P(("groups", "fsdp"), "band", None, None),
            P("groups", "fsdp"),
            P(("groups", "fsdp")),
        ),
        check_vma=False,
    )
```

time: 170 us -> 146 us (0.86)
  starting transfers between devices: 47.9 us -> 33.8 us
  waiting for transfers between devices: 70.7 us -> 59 us
  Pallas kernels: 35 us -> 43.4 us
  local copies, waits for them, and re-layouts: 11.9 us -> 4.57 us
    ppermute x10, waiting for transfers between devices: 13.1 us -> 0.03 us  [across(): return lax.ppermute(x, ('fsdp', 'band'), pairs)]
    ppermute x10, starting transfers between devices: 26.3 us -> 14.9 us  [across(): return lax.ppermute(x, ('fsdp', 'band'), pairs)]
    ppermute x5 -> x6, waiting for transfers between devices: 40.4 us -> 30.3 us  [turn(): return lax.ppermute(x, 'band', [(i, (i + k) % n) for i in range(n)])]
    pallas_call x5 -> x7, Pallas kernels: 35 us -> 43.4 us  [the longest x2 18.3 us: unit(): pl.pallas_call(functools.partial(grad_kernel, n, jb, rl, blocks[0], moves...]
    ppermute x3, waiting for transfers between devices: 7.04 us -> 13.3 us  [unit(): lax.ppermute(tap_all, 'fsdp', [(i, i ^ step) for i in range(shards)])]
    ppermute x3, waiting for transfers between devices: 10.1 us -> 15.3 us  [other_group(): return lax.ppermute(x, every, pairs)]
    ppermute x2 -> x0, local copies, waits for them, and re-layouts: 3.41 us -> none  [turn(): return lax.ppermute(x, 'band', [(i, (i + k) % n) for i in range(n)])]
    reshape x1 -> x0, local copies, waits for them, and re-layouts: 2.11 us -> none  [body(): cot = cotangent.reshape(tokens, feats)]
  transfers between devices with their start and end apart: 22 -> 23, of which waited for: 8 -> 5; matrix products, arithmetic and copies ran while one was open for 6% -> 2% of each run, Pallas kernels for 10% -> 30%
where the time goes in v2:
time: 146 us; the launch traced here: 145 us
  waiting for transfers between devices  59 us (40%)
  Pallas kernels  43.4 us (30%)
  starting transfers between devices  33.8 us (23%)
  local copies, waits for them, and re-layouts  4.57 us (3%)
  other arithmetic  3.1 us (2%)
    ppermute x6, waiting for transfers between devices, turn(): return lax.ppermute(x, 'band', [(i, (i + k) % n) for i in range(n)])  30.3 us
    pallas_call x2, Pallas kernels, unit(): pl.pallas_call(functools.partial(grad_kernel, n, jb, rl, blocks[0], moves...  18.3 us
    ppermute x3, waiting for transfers between devices, other_group(): return lax.ppermute(x, every, pairs)  15.3 us
    ppermute x10, starting transfers between devices, across(): return lax.ppermute(x, ('fsdp', 'band'), pairs)  14.9 us
    ppermute x3, waiting for transfers between devices, unit(): lax.ppermute(tap_all, 'fsdp', [(i, i ^ step) for i in range(shards)])  13.3 us
    pallas_call x2, Pallas kernels, unit(): pl.pallas_call(functools.partial(out_kernel, n, blocks, moves, len(args),...  11.9 us
    ppermute x3, starting transfers between devices, other_group(): return lax.ppermute(x, every, pairs)  9.25 us
    pallas_call x1, Pallas kernels, unit(): pl.pallas_call(functools.partial(conv_kernel, n, jb, rl), grid_spec=pltpu...  6.14 us
  transfers between devices with their start and end apart: 23, of which 5 were waited for; matrix products, arithmetic and copies ran while one was open for 2% of the time, Pallas kernels for 30%

profile of v2, /device:TPU:0, one launch (start us, length us, event | category | flops | bytes accessed | tf_op | source)
XLA Modules:
  0.0 144.8 jit_solution(6884447902940574188)
XLA Ops:
  0.7 0.0 copy-start
  0.7 2.2 %constant_dynamic-slice_fusion = bf16[176,2240]{1,0:T(8,128)(2,1)} fusion(bf16[352,2240]{1,0:T(8,128)(2,1)} %param.8, s32[]{:T(128)S(6)} %select_n.37), kind=kLoop, calls=%fused_computation.14 | loop fusion | bytes 1576964 | tf_op jit(solution)/shard_map/dynamic_slice | solution.py:277
  2.9 6.0 %collective-permute-start.9 = (bf16[176,2240]{1,0:T(8,128)(2,1)}, bf16[176,2240]{1,0:T(8,128)(2,1)S(1)}, u32[]{:S(2)}, u32[]{:S(2)}) collective-permute-start(bf16[176,2240]{1,0:T(8,128)(2,1)} %constant_dynamic-slice_fusion), channel_id=1, source_target_pairs={{0,8},{3,11},{4,12},{7,15},{8,0},{11,3},{12,4},{15,7},{16,24},{19,... | collective-permute-start | bytes 2365448 | tf_op jit(solution)/shard_map/ppermute | solution.py:267
  8.9 0.1 pad.13.clone
  9.0 0.1 fusion.2
  9.1 0.1 collective-permute-start.1
  9.1 3.5 %collective-permute-start.5 = (bf16[176,2240]{1,0:T(8,128)(2,1)}, bf16[176,2240]{1,0:T(8,128)(2,1)}, u32[]{:S(2)}, u32[]{:S(2)}) collective-permute-start(bf16[176,2240]{1,0:T(8,128)(2,1)} %constant_dynamic-slice_fusion), channel_id=1, source_target_pairs={{0,4},{3,7},{4,0},{7,3},{8,12},{11,15},{12,8},{15,11},{16,20},{19,... | collective-permute-start | bytes 2365448 | tf_op jit(solution)/shard_map/ppermute | solution.py:267
  12.6 0.0 collective-permute-done.1
  12.7 0.5 collective-permute-start.2
  13.2 0.7 stack.23.s_ref
  13.9 3.9 %pack.1 = (bf16[2,4,2,64,352]{4,3,2,1,0:T(8,128)(2,1)}, bf16[2,4,2,64,352]{4,3,2,1,0:T(8,128)(2,1)}) custom-call(s32[5]{0:T(128)} %stack.23.s_ref, bf16[128,5632]{1,0:T(8,128)(2,1)} %bitcast.22), custom_call_target="tpu_custom_call" | custom-call | tf_op jit(solution)/shard_map/pack/pallas_call | solution.py:316
  17.8 0.2 collective-permute-start
  18.0 13.3 %collective-permute-done.2 = bf16[2,16,352]{2,1,0:T(8,128)(2,1)S(1)} collective-permute-done((bf16[2,16,352]{2,1,0:T(8,128)(2,1)S(1)}, bf16[2,16,352]{2,1,0:T(8,128)(2,1)S(1)}, u32[]{:S(2)}, u32[]{:S(2)}) %collective-permute-start.2) | collective-permute-done | bytes 22560 | tf_op jit(solution)/shard_map/ppermute | solution.py:305
  31.3 1.0 collective-permute-start.3
  32.4 0.0 collective-permute-done.9.refs_6_.refs_12_
  32.4 3.4 %collective-permute-start.10 = (bf16[176,2240]{1,0:T(8,128)(2,1)S(1)}, bf16[176,2240]{1,0:T(8,128)(2,1)}, u32[]{:S(2)}, u32[]{:S(2)}) collective-permute-start(bf16[176,2240]{1,0:T(8,128)(2,1)S(1)} %collective-permute-done.9.refs_6_.refs_12_), channel_id=1, source_target_pairs={{0,16},{3,19},{4,20},{7,23},{8,24},{11,27},{12,28},{15,31},{16,0},... | collective-permute-start | bytes 2365448 | tf_op jit(solution)/shard_map/ppermute | solution.py:275
  35.8 4.4 %collective-permute-start.13 = (bf16[176,2240]{1,0:T(8,128)(2,1)S(1)}, bf16[176,2240]{1,0:T(8,128)(2,1)}, u32[]{:S(2)}, u32[]{:S(2)}) collective-permute-start(bf16[176,2240]{1,0:T(8,128)(2,1)S(1)} %collective-permute-done.9.refs_6_.refs_12_), channel_id=1, source_target_pairs={{0,4},{3,7},{4,0},{7,3},{8,12},{11,15},{12,8},{15,11},{16,20},{19,... | collective-permute-start | bytes 2365448 | tf_op jit(solution)/shard_map/ppermute | solution.py:267
  40.2 0.0 collective-permute-done.3
  40.2 0.1 collective-permute-start.18
  40.3 13.3 %collective-permute-done.18 = bf16[1,2,64,2240]{3,2,1,0:T(8,128)(2,1)S(1)} collective-permute-done((bf16[1,2,64,2240]{3,2,1,0:T(8,128)(2,1)}, bf16[1,2,64,2240]{3,2,1,0:T(8,128)(2,1)S(1)}, u32[]{:S(2)}, u32[]{:S(2)}) %collective-permute-start.18) | collective-permute-done | bytes 573472 | tf_op jit(solution)/shard_map/ppermute | solution.py:325
  53.6 0.0 collective-permute-start.4
  53.6 0.0 collective-permute-done.5.refs_2_.refs_8_
  53.6 2.4 %collective-permute-start.6 = (bf16[176,2240]{1,0:T(8,128)(2,1)}, bf16[176,2240]{1,0:T(8,128)(2,1)}, u32[]{:S(2)}, u32[]{:S(2)}) collective-permute-start(bf16[176,2240]{1,0:T(8,128)(2,1)} %collective-permute-done.5.refs_2_.refs_8_), channel_id=1, source_target_pairs={{0,16},{3,19},{4,20},{7,23},{8,24},{11,27},{12,28},{15,31},{16,0},... | collective-permute-start | bytes 2365448 | tf_op jit(solution)/shard_map/ppermute | solution.py:275
  56.1 0.0 collective-permute-done.refs_0_
  56.1 0.1 collective-permute-start.11
  56.2 0.0 collective-permute-done.10.refs_7_.refs_13_
  56.2 0.5 collective-permute-start.7
  56.7 0.0 collective-permute-done.13.refs_1_.refs_6_
  56.7 3.4 %collective-permute-start.14 = (bf16[176,2240]{1,0:T(8,128)(2,1)}, bf16[176,2240]{1,0:T(8,128)(2,1)}, u32[]{:S(2)}, u32[]{:S(2)}) collective-permute-start(bf16[176,2240]{1,0:T(8,128)(2,1)} %collective-permute-done.13.refs_1_.refs_6_), channel_id=1, source_target_pairs={{0,16},{3,19},{4,20},{7,23},{8,24},{11,27},{12,28},{15,31},{16,0},... | collective-permute-start | bytes 2365448 | tf_op jit(solution)/shard_map/ppermute | solution.py:275
  60.1 8.0 %collective-permute-done.6.refs_3_.refs_9_ = bf16[176,2240]{1,0:T(8,128)(2,1)} collective-permute-done((bf16[176,2240]{1,0:T(8,128)(2,1)}, bf16[176,2240]{1,0:T(8,128)(2,1)}, u32[]{:S(2)}, u32[]{:S(2)}) %collective-permute-start.6) | collective-permute-done | bytes 788512 | tf_op jit(solution)/shard_map/ppermute | solution.py:275
  68.1 0.0 collective-permute-start.12
  68.1 0.0 collective-permute-done.11.refs_8_.refs_14_
  68.1 0.9 copy-done.3
  69.0 0.5 collective-permute-start.8
  69.5 0.0 collective-permute-done.7.refs_4_.refs_10_
  69.5 0.0 collective-permute-start.15
  69.5 7.3 %collective-permute-done.14.refs_2_.refs_7_ = bf16[176,2240]{1,0:T(8,128)(2,1)} collective-permute-done((bf16[176,2240]{1,0:T(8,128)(2,1)}, bf16[176,2240]{1,0:T(8,128)(2,1)}, u32[]{:S(2)}, u32[]{:S(2)}) %collective-permute-start.14) | collective-permute-done | bytes 788512 | tf_op jit(solution)/shard_map/ppermute | solution.py:275
  76.8 0.0 collective-permute-start.16
  76.8 0.7 pad_maximum_fusion.refs_1_
  77.5 6.1 %conv.1 = (bf16[4,2,128,352]{3,2,1,0:T(8,128)(2,1)}, f32[4,2,128,352]{3,2,1,0:T(8,128)}, f32[4,2,128,352]{3,2,1,0:T(8,128)}) custom-call(s32[5]{0:T(128)} %stack.23.s_ref, bf16[2,4,2,64,352]{4,3,2,1,0:T(8,128)(2,1)} %get-tuple-element.17.own, bf16[2,4,2,64,352]{4,3,2,1,0:T(8,128)(2,1)} %copy-done.1, bf16[8,16,352]{2,1,0:T(8,128)(2,1)} %pad_maximum_fusion.refs_1_), custom_call_target="tpu_custom_call" | custom-call | tf_op jit(solution)/shard_map/conv/pallas_call | solution.py:335
  83.6 0.0 collective-permute-done.4
  83.6 0.0 collective-permute-done.12.refs_9_.refs_15_
  83.6 0.0 collective-permute-done.8.refs_5_.refs_11_
  83.6 11.8 %shard_map.86 = (bf16[2,3,2,64,352]{4,3,2,1,0:T(8,128)(2,1)}, bf16[2,3,2,64,352]{4,3,2,1,0:T(8,128)(2,1)}, f32[2,4,16,352]{3,2,1,0:T(8,128)}) custom-call(s32[5]{0:T(128)} %stack.23.s_ref, bf16[2,4,2,64,352]{4,3,2,1,0:T(8,128)(2,1)} %get-tuple-element.17.own, bf16[2,4,2,64,352]{4,3,2,1,0:T(8,128)(2,1)} %copy-done.1, ...), custom_call_target="tpu_custom_call" | custom-call | tf_op jit(solution)/shard_map/pallas_call | solution.py:413
  95.5 0.9 collective-permute-start.19
  96.4 0.0 collective-permute-done.15.refs_3_.refs_8_
  96.4 0.0 collective-permute-done.16.refs_4_.refs_9_
  96.4 6.5 %shard_map.87 = (bf16[2,1,2,64,352]{4,3,2,1,0:T(8,128)(2,1)}, bf16[2,1,2,64,352]{4,3,2,1,0:T(8,128)(2,1)}, f32[2,4,16,352]{3,2,1,0:T(8,128)}) custom-call(s32[5]{0:T(128)} %stack.23.s_ref, bf16[2,4,2,64,352]{4,3,2,1,0:T(8,128)(2,1)} %get-tuple-element.17.own, bf16[2,4,2,64,352]{4,3,2,1,0:T(8,128)(2,1)} %copy-done.1, ...), custom_call_target="tpu_custom_call", output_to_operand_aliasing={{2}: (12, {})} | custom-call | tf_op jit(solution)/shard_map/pallas_call | solution.py:413
  102.9 3.4 %all-to-all-start = ((f32[8,16,352]{2,1,0:T(8,128)}), f32[8,16,352]{2,1,0:T(8,128)S(1)}, u32[]{:S(2)}, u32[]{:S(2)}) async-start(f32[8,16,352]{2,1,0:T(8,128)} %bitcast.25), calls=%async_computation | async-start | bytes 393216 | tf_op jit(solution)/shard_map/all_to_all | solution.py:451
  106.3 6.6 %shard_map.84.refs_0_ = f32[256,2240]{1,0:T(8,128)} custom-call(s32[5]{0:T(128)} %stack.23.s_ref, bf16[4,2,128,352]{3,2,1,0:T(8,128)(2,1)} %get-tuple-element.19.glu, bf16[2,176,2240]{2,1,0:T(8,128)(2,1)} %bitcast.17, bf16[2,176,2240]{2,1,0:T(8,128)(2,1)} %bitcast.8.refs_1_.refs_7_, bf16[176,2240]{1,0:T(8,128)(2,1)} %collective-permute-done.5.refs_2_.refs_8_, ...), custom_call_target="tpu_custom_call" | custom-call | tf_op jit(solution)/shard_map/pallas_call | solution.py:393
  112.9 5.3 %shard_map.85 = (f32[128,2240]{1,0:T(8,128)}, bf16[128,2240]{1,0:T(8,128)(2,1)}) custom-call(s32[5]{0:T(128)} %stack.23.s_ref, bf16[4,2,128,352]{3,2,1,0:T(8,128)(2,1)} %get-tuple-element.19.glu, f32[256,2240]{1,0:T(8,128)} %shard_map.84.refs_0_, bf16[176,2240]{1,0:T(8,128)(2,1)} %collective-permute-done.13.refs_1_.refs_6_, ...), custom_call_target="tpu_custom_call" | custom-call | tf_op jit(solution)/shard_map/pallas_call | solution.py:393
  118.2 1.2 collective-permute-start.17
  119.5 0.9 collective-permute-start.20
  120.3 0.0 all-to-all-done
  120.4 1.2 collective-permute-start.21
  121.6 0.0 collective-permute-done.19.refs_1_
  121.6 17.0 %collective-permute-done.20.refs_3_ = bf16[2,1,2,64,352]{4,3,2,1,0:T(8,128)(2,1)S(1)} collective-permute-done((bf16[2,1,2,64,352]{4,3,2,1,0:T(8,128)(2,1)S(1)}, bf16[2,1,2,64,352]{4,3,2,1,0:T(8,128)(2,1)S(1)}, u32[]{:S(2)}, u32[]{:S(2)}) %collective-permute-start.20) | collective-permute-done | bytes 180256 | tf_op jit(solution)/shard_map/ppermute | solution.py:325
  138.6 0.7 copy-done.7
  139.3 3.2 %unpack.1 = bf16[128,5632]{1,0:T(8,128)(2,1)} custom-call(s32[5]{0:T(128)} %stack.23.s_ref, bf16[2,3,2,64,352]{4,3,2,1,0:T(8,128)(2,1)} %get-tuple-element.24.refs_0_, bf16[2,3,2,64,352]{4,3,2,1,0:T(8,128)(2,1)} %copy-done.6, bf16[2,1,2,64,352]{4,3,2,1,0:T(8,128)(2,1)} %get-tuple-element.27.refs_2_, bf16[2,1,2,64,352]{4,3,2,1,0:T(8,128)(2,1)} %copy-done.7), custom_call_target="tpu_custom_call" | custom-call | tf_op jit(solution)/shard_map/unpack/pallas_call | solution.py:440
  142.5 0.0 collective-permute-done.21
  142.5 0.7 fusion.3
  143.2 0.7 slice_maximum_fusion
  143.9 0.0 collective-permute-done.17
  143.9 0.9 add_convert_fusion
  (25 shorter events, 0.1 us)
Async XLA Ops:
  0.6 8.2 %copy-start.9 = (bf16[704]{0:T(1024)(128)(2,1)S(1)}, bf16[704]{0:T(1024)(128)(2,1)}, u32[]{:S(2)}) copy-start(bf16[704]{0:T(1024)(128)(2,1)} %param.7) | copy-start | bytes 4228
  0.6 8.3 %copy-start.8 = (bf16[9,704]{1,0:T(8,128)(2,1)S(1)}, bf16[9,704]{1,0:T(8,128)(2,1)}, u32[]{:S(2)}) copy-start(bf16[9,704]{1,0:T(8,128)(2,1)} %param.6) | copy-start | bytes 38020
  0.7 53.0 %copy-start = (bf16[352,2240]{1,0:T(8,128)(2,1)S(1)}, bf16[352,2240]{1,0:T(8,128)(2,1)}, u32[]{:S(2)}) copy-start(bf16[352,2240]{1,0:T(8,128)(2,1)} %param.8) | copy-start | bytes 4730884
  2.9 29.5 %collective-permute-start.9 = (bf16[176,2240]{1,0:T(8,128)(2,1)}, bf16[176,2240]{1,0:T(8,128)(2,1)S(1)}, u32[]{:S(2)}, u32[]{:S(2)}) collective-permute-start(bf16[176,2240]{1,0:T(8,128)(2,1)} %constant_dynamic-slice_fusion), channel_id=1, source_target_pairs={{0,8},{3,11},{4,12},{7,15},{8,0},{11,3},{12,4},{15,7},{16,24},{19,... | collective-permute-start | bytes 2365448 | tf_op jit(solution)/shard_map/ppermute | solution.py:267
  9.1 3.6 %collective-permute-start.1 = (bf16[1,16,352]{2,1,0:T(8,128)(2,1)S(1)}, bf16[1,16,352]{2,1,0:T(8,128)(2,1)S(1)}, u32[]{:S(2)}, u32[]{:S(2)}) collective-permute-start(bf16[1,16,352]{2,1,0:T(8,128)(2,1)S(1)} %fusion.2), channel_id=1, source_target_pairs={{0,2},{2,0},{4,6},{6,4},{8,10},{10,8},{12,14},{14,12},{1,3},{3,1},... | collective-permute-start | bytes 33800 | tf_op jit(solution)/shard_map/ppermute | solution.py:305
  9.1 44.5 %collective-permute-start.5 = (bf16[176,2240]{1,0:T(8,128)(2,1)}, bf16[176,2240]{1,0:T(8,128)(2,1)}, u32[]{:S(2)}, u32[]{:S(2)}) collective-permute-start(bf16[176,2240]{1,0:T(8,128)(2,1)} %constant_dynamic-slice_fusion), channel_id=1, source_target_pairs={{0,4},{3,7},{4,0},{7,3},{8,12},{11,15},{12,8},{15,11},{16,20},{19,... | collective-permute-start | bytes 2365448 | tf_op jit(solution)/shard_map/ppermute | solution.py:267
  12.7 18.7 %collective-permute-start.2 = (bf16[2,16,352]{2,1,0:T(8,128)(2,1)S(1)}, bf16[2,16,352]{2,1,0:T(8,128)(2,1)S(1)}, u32[]{:S(2)}, u32[]{:S(2)}) collective-permute-start(bf16[2,16,352]{2,1,0:T(8,128)(2,1)S(1)} %pad_maximum_fusion.2), channel_id=1, source_target_pairs={{0,4},{2,6},{4,0},{6,2},{8,12},{10,14},{12,8},{14,10},{1,5},{3,7},... | collective-permute-start | bytes 67592 | tf_op jit(solution)/shard_map/ppermute | solution.py:305
  17.8 38.3 %collective-permute-start = (bf16[2,4,2,64,352]{4,3,2,1,0:T(8,128)(2,1)}, bf16[2,4,2,64,352]{4,3,2,1,0:T(8,128)(2,1)S(1)}, u32[]{:S(2)}, u32[]{:S(2)}) collective-permute-start(bf16[2,4,2,64,352]{4,3,2,1,0:T(8,128)(2,1)} %get-tuple-element.18), channel_id=1, source_target_pairs={{0,1},{1,0},{2,3},{3,2},{4,5},{5,4},{6,7},{7,6},{8,9},{9,8},{10,11... | collective-permute-start | bytes 2162696 | tf_op jit(solution)/shard_map/ppermute | solution.py:325
  31.3 8.9 %collective-permute-start.3 = (bf16[4,16,352]{2,1,0:T(8,128)(2,1)S(1)}, bf16[4,16,352]{2,1,0:T(8,128)(2,1)S(1)}, u32[]{:S(2)}, u32[]{:S(2)}) collective-permute-start(bf16[4,16,352]{2,1,0:T(8,128)(2,1)S(1)} %pad_maximum_fusion.1), channel_id=1, source_target_pairs={{0,8},{2,10},{4,12},{6,14},{8,0},{10,2},{12,4},{14,6},{1,9},{3,11}... | collective-permute-start | bytes 135176 | tf_op jit(solution)/shard_map/ppermute | solution.py:305
  32.4 51.2 %copy-start.2 = (bf16[176,2240]{1,0:T(8,128)(2,1)}, bf16[176,2240]{1,0:T(8,128)(2,1)S(1)}, u32[]{:S(2)}) copy-start(bf16[176,2240]{1,0:T(8,128)(2,1)S(1)} %collective-permute-done.9.refs_6_.refs_12_) | copy-start | bytes 2365444
  32.4 23.8 %collective-permute-start.10 = (bf16[176,2240]{1,0:T(8,128)(2,1)S(1)}, bf16[176,2240]{1,0:T(8,128)(2,1)}, u32[]{:S(2)}, u32[]{:S(2)}) collective-permute-start(bf16[176,2240]{1,0:T(8,128)(2,1)S(1)} %collective-permute-done.9.refs_6_.refs_12_), channel_id=1, source_target_pairs={{0,16},{3,19},{4,20},{7,23},{8,24},{11,27},{12,28},{15,31},{16,0},... | collective-permute-start | bytes 2365448 | tf_op jit(solution)/shard_map/ppermute | solution.py:275
  35.8 20.9 %collective-permute-start.13 = (bf16[176,2240]{1,0:T(8,128)(2,1)S(1)}, bf16[176,2240]{1,0:T(8,128)(2,1)}, u32[]{:S(2)}, u32[]{:S(2)}) collective-permute-start(bf16[176,2240]{1,0:T(8,128)(2,1)S(1)} %collective-permute-done.9.refs_6_.refs_12_), channel_id=1, source_target_pairs={{0,4},{3,7},{4,0},{7,3},{8,12},{11,15},{12,8},{15,11},{16,20},{19,... | collective-permute-start | bytes 2365448 | tf_op jit(solution)/shard_map/ppermute | solution.py:267
  40.2 13.4 %collective-permute-start.18 = (bf16[1,2,64,2240]{3,2,1,0:T(8,128)(2,1)}, bf16[1,2,64,2240]{3,2,1,0:T(8,128)(2,1)S(1)}, u32[]{:S(2)}, u32[]{:S(2)}) collective-permute-start(bf16[1,2,64,2240]{3,2,1,0:T(8,128)(2,1)} %param.9), channel_id=1, source_target_pairs={{0,1},{1,0},{2,3},{3,2},{4,5},{5,4},{6,7},{7,6},{8,9},{9,8},{10,11... | collective-permute-start | bytes 1720328 | tf_op jit(solution)/shard_map/ppermute | solution.py:325
  53.6 2.4 %copy-start.4 = (bf16[1,2,64,2240]{3,2,1,0:T(8,128)(2,1)}, bf16[1,2,64,2240]{3,2,1,0:T(8,128)(2,1)S(1)}, u32[]{:S(2)}) copy-start(bf16[1,2,64,2240]{3,2,1,0:T(8,128)(2,1)S(1)} %collective-permute-done.18) | copy-start | bytes 1720324
  53.6 30.0 %collective-permute-start.4 = (bf16[352,2240]{1,0:T(8,128)(2,1)S(1)}, bf16[352,2240]{1,0:T(8,128)(2,1)}, u32[]{:S(2)}, u32[]{:S(2)}) collective-permute-start(bf16[352,2240]{1,0:T(8,128)(2,1)S(1)} %copy-done), channel_id=1, source_target_pairs={{0,2},{1,3},{2,0},{3,1},{4,6},{5,7},{6,4},{7,5},{8,10},{9,11},{10,... | collective-permute-start | bytes 4730888 | tf_op jit(solution)/shard_map/ppermute | solution.py:267
  53.6 14.5 %collective-permute-start.6 = (bf16[176,2240]{1,0:T(8,128)(2,1)}, bf16[176,2240]{1,0:T(8,128)(2,1)}, u32[]{:S(2)}, u32[]{:S(2)}) collective-permute-start(bf16[176,2240]{1,0:T(8,128)(2,1)} %collective-permute-done.5.refs_2_.refs_8_), channel_id=1, source_target_pairs={{0,16},{3,19},{4,20},{7,23},{8,24},{11,27},{12,28},{15,31},{16,0},... | collective-permute-start | bytes 2365448 | tf_op jit(solution)/shard_map/ppermute | solution.py:275
  56.1 21.4 %copy-start.1 = (bf16[2,4,2,64,352]{4,3,2,1,0:T(8,128)(2,1)}, bf16[2,4,2,64,352]{4,3,2,1,0:T(8,128)(2,1)S(1)}, u32[]{:S(2)}) copy-start(bf16[2,4,2,64,352]{4,3,2,1,0:T(8,128)(2,1)S(1)} %collective-permute-done.refs_0_) | copy-start | bytes 2162692
  56.1 12.0 %collective-permute-start.11 = (bf16[176,2240]{1,0:T(8,128)(2,1)S(1)}, bf16[176,2240]{1,0:T(8,128)(2,1)S(1)}, u32[]{:S(2)}, u32[]{:S(2)}) collective-permute-start(bf16[176,2240]{1,0:T(8,128)(2,1)S(1)} %collective-permute-done.9.refs_6_.refs_12_), channel_id=1, source_target_pairs={{0,2},{1,3},{2,0},{3,1},{4,6},{5,7},{6,4},{7,5},{8,10},{9,11},{10,... | collective-permute-start | bytes 2365448 | tf_op jit(solution)/shard_map/ppermute | solution.py:267
  56.2 13.3 %collective-permute-start.7 = (bf16[176,2240]{1,0:T(8,128)(2,1)}, bf16[176,2240]{1,0:T(8,128)(2,1)}, u32[]{:S(2)}, u32[]{:S(2)}) collective-permute-start(bf16[176,2240]{1,0:T(8,128)(2,1)} %collective-permute-done.5.refs_2_.refs_8_), channel_id=1, source_target_pairs={{0,2},{1,3},{2,0},{3,1},{4,6},{5,7},{6,4},{7,5},{8,10},{9,11},{10,... | collective-permute-start | bytes 2365448 | tf_op jit(solution)/shard_map/ppermute | solution.py:267
  56.7 20.1 %collective-permute-start.14 = (bf16[176,2240]{1,0:T(8,128)(2,1)}, bf16[176,2240]{1,0:T(8,128)(2,1)}, u32[]{:S(2)}, u32[]{:S(2)}) collective-permute-start(bf16[176,2240]{1,0:T(8,128)(2,1)} %collective-permute-done.13.refs_1_.refs_6_), channel_id=1, source_target_pairs={{0,16},{3,19},{4,20},{7,23},{8,24},{11,27},{12,28},{15,31},{16,0},... | collective-permute-start | bytes 2365448 | tf_op jit(solution)/shard_map/ppermute | solution.py:275
  68.1 15.5 %collective-permute-start.12 = (bf16[176,2240]{1,0:T(8,128)(2,1)}, bf16[176,2240]{1,0:T(8,128)(2,1)}, u32[]{:S(2)}, u32[]{:S(2)}) collective-permute-start(bf16[176,2240]{1,0:T(8,128)(2,1)} %collective-permute-done.10.refs_7_.refs_13_), channel_id=1, source_target_pairs={{0,2},{1,3},{2,0},{3,1},{4,6},{5,7},{6,4},{7,5},{8,10},{9,11},{10,... | collective-permute-start | bytes 2365448 | tf_op jit(solution)/shard_map/ppermute | solution.py:267
  68.1 0.9 copy-start.3
  69.0 14.6 %collective-permute-start.8 = (bf16[176,2240]{1,0:T(8,128)(2,1)}, bf16[176,2240]{1,0:T(8,128)(2,1)}, u32[]{:S(2)}, u32[]{:S(2)}) collective-permute-start(bf16[176,2240]{1,0:T(8,128)(2,1)} %collective-permute-done.6.refs_3_.refs_9_), channel_id=1, source_target_pairs={{0,2},{1,3},{2,0},{3,1},{4,6},{5,7},{6,4},{7,5},{8,10},{9,11},{10,... | collective-permute-start | bytes 2365448 | tf_op jit(solution)/shard_map/ppermute | solution.py:267
  69.5 26.9 %collective-permute-start.15 = (bf16[176,2240]{1,0:T(8,128)(2,1)}, bf16[176,2240]{1,0:T(8,128)(2,1)}, u32[]{:S(2)}, u32[]{:S(2)}) collective-permute-start(bf16[176,2240]{1,0:T(8,128)(2,1)} %collective-permute-done.13.refs_1_.refs_6_), channel_id=1, source_target_pairs={{0,2},{1,3},{2,0},{3,1},{4,6},{5,7},{6,4},{7,5},{8,10},{9,11},{10,... | collective-permute-start | bytes 2365448 | tf_op jit(solution)/shard_map/ppermute | solution.py:267
  76.8 19.6 %collective-permute-start.16 = (bf16[176,2240]{1,0:T(8,128)(2,1)}, bf16[176,2240]{1,0:T(8,128)(2,1)}, u32[]{:S(2)}, u32[]{:S(2)}) collective-permute-start(bf16[176,2240]{1,0:T(8,128)(2,1)} %collective-permute-done.14.refs_2_.refs_7_), channel_id=1, source_target_pairs={{0,2},{1,3},{2,0},{3,1},{4,6},{5,7},{6,4},{7,5},{8,10},{9,11},{10,... | collective-permute-start | bytes 2365448 | tf_op jit(solution)/shard_map/ppermute | solution.py:267
  95.5 26.1 %collective-permute-start.19 = (bf16[2,3,2,64,352]{4,3,2,1,0:T(8,128)(2,1)}, bf16[2,3,2,64,352]{4,3,2,1,0:T(8,128)(2,1)S(1)}, u32[]{:S(2)}, u32[]{:S(2)}) collective-permute-start(bf16[2,3,2,64,352]{4,3,2,1,0:T(8,128)(2,1)} %get-tuple-element.25), channel_id=1, source_target_pairs={{0,1},{1,0},{2,3},{3,2},{4,5},{5,4},{6,7},{7,6},{8,9},{9,8},{10,11... | collective-permute-start | bytes 1622024 | tf_op jit(solution)/shard_map/ppermute | solution.py:325
  102.9 17.4 %all-to-all-start = ((f32[8,16,352]{2,1,0:T(8,128)}), f32[8,16,352]{2,1,0:T(8,128)S(1)}, u32[]{:S(2)}, u32[]{:S(2)}) async-start(f32[8,16,352]{2,1,0:T(8,128)} %bitcast.25), calls=%async_computation | async-start | bytes 393216 | tf_op jit(solution)/shard_map/all_to_all | solution.py:451
  112.9 6.6 %copy-start.10 = (bf16[2,1,2,64,352]{4,3,2,1,0:T(8,128)(2,1)S(1)}, bf16[2,1,2,64,352]{4,3,2,1,0:T(8,128)(2,1)}, u32[]{:S(2)}) copy-start(bf16[2,1,2,64,352]{4,3,2,1,0:T(8,128)(2,1)} %get-tuple-element.28) | copy-start | bytes 540676
  118.2 25.6 %collective-permute-start.17 = (bf16[1,2,64,2240]{3,2,1,0:T(8,128)(2,1)}, bf16[1,2,64,2240]{3,2,1,0:T(8,128)(2,1)S(1)}, u32[]{:S(2)}, u32[]{:S(2)}) collective-permute-start(bf16[1,2,64,2240]{3,2,1,0:T(8,128)(2,1)} %bitcast.26), channel_id=1, source_target_pairs={{0,1},{1,0},{2,3},{3,2},{4,5},{5,4},{6,7},{7,6},{8,9},{9,8},{10,11... | collective-permute-start | bytes 1720328 | tf_op jit(solution)/shard_map/ppermute | solution.py:325
  119.5 19.1 %collective-permute-start.20 = (bf16[2,1,2,64,352]{4,3,2,1,0:T(8,128)(2,1)S(1)}, bf16[2,1,2,64,352]{4,3,2,1,0:T(8,128)(2,1)S(1)}, u32[]{:S(2)}, u32[]{:S(2)}) collective-permute-start(bf16[2,1,2,64,352]{4,3,2,1,0:T(8,128)(2,1)S(1)} %copy-done.10), channel_id=1, source_target_pairs={{0,1},{1,0},{2,3},{3,2},{4,5},{5,4},{6,7},{7,6},{8,9},{9,8},{10,11... | collective-permute-start | bytes 540680 | tf_op jit(solution)/shard_map/ppermute | solution.py:325
  120.4 22.1 %collective-permute-start.21 = (f32[16,352]{1,0:T(8,128)S(1)}, f32[16,352]{1,0:T(8,128)S(1)}, u32[]{:S(2)}, u32[]{:S(2)}) collective-permute-start(f32[16,352]{1,0:T(8,128)S(1)} %reduce_sum.9), channel_id=1, source_target_pairs={{0,1},{1,0},{2,3},{3,2},{4,5},{5,4},{6,7},{7,6},{8,9},{9,8},{10,11... | collective-permute-start | bytes 67592 | tf_op jit(solution)/shard_map/ppermute | solution.py:325
  121.6 17.0 %copy-start.6 = (bf16[2,3,2,64,352]{4,3,2,1,0:T(8,128)(2,1)}, bf16[2,3,2,64,352]{4,3,2,1,0:T(8,128)(2,1)S(1)}, u32[]{:S(2)}) copy-start(bf16[2,3,2,64,352]{4,3,2,1,0:T(8,128)(2,1)S(1)} %collective-permute-done.19.refs_1_) | copy-start | bytes 1622020
  138.6 0.7 copy-start.7
  139.3 4.6 %copy-start.5 = (f32[128,2240]{1,0:T(8,128)S(1)}, f32[128,2240]{1,0:T(8,128)}, u32[]{:S(2)}) copy-start(f32[128,2240]{1,0:T(8,128)} %get-tuple-element.20) | copy-start | bytes 3440644

commit v3 on v2

--- a/solution.py
+++ b/solution.py
@@ -19,7 +19,6 @@
 
 def pack_kernel(n, jb, blk, s_ref, x_ref, *outs):
     b = s_ref[0]
-    rows, cols = outs[0].shape[2:4]
     chans = x_ref.shape[1]
     for vg in range(2):
         for jz in range(jb):
@@ -30,12 +29,12 @@
                 wide = x_ref[:, low:high].astype(F32)
                 if start != low:
                     wide = pltpu.roll(wide, high - low - (start - low), 1)
-                piece = wide[:, :blk].astype(BF16).reshape(rows, cols, blk)
+                piece = wide[:, :blk].astype(BF16)
                 for k in range(n):
 
                     @pl.when(lax.rem(b + k, n) == t)
                     def _():
-                        outs[k][vg, jz] = piece
+                        outs[k][vg, jz, 0] = piece
 
 
 def place_rows(n, rl, b, xs, own, received):
@@ -116,30 +115,27 @@
         run(other)
 
 
-def out_kernel(n, blocks, copies, n_w, first, last, s_ref, glu, *refs):
-    before, refs = (None, refs) if first else (refs[0], refs[1:])
-    w_refs, refs = refs[:n_w], refs[n_w:]
-    outs, (w_buf, sems) = refs[:-2], refs[-2:]
-    acc, outs = (outs[-1], outs[:-1]) if last else (outs[0], ())
-    for at in range(len(blocks)):
-        move_weights("start", s_ref, copies[at], at, w_refs, w_buf, sems)
+def out_kernel(n, copies, n_w, s_ref, glu, *refs):
+    w_refs, outs, (acc, w_buf, sems) = refs[:n_w], refs[n_w:-3], refs[-3:]
+    for k, copy in enumerate(copies):
+        move_weights("start", s_ref, copy, k, w_refs, w_buf, sems)
     tokens, blk = glu.shape[2:]
-    for at, k in enumerate(blocks):
-        move_weights("wait", s_ref, copies[at], at, w_refs, w_buf, sems)
+    for k, copy in enumerate(copies):
+        move_weights("wait", s_ref, copy, k, w_refs, w_buf, sems)
         part = jnp.dot(
             glu[s_ref[3] ^ k].reshape(n * tokens, blk),
-            w_buf[at].reshape(blk, w_buf.shape[3]),
+            w_buf[k].reshape(blk, w_buf.shape[3]),
             preferred_element_type=F32,
         )
-        if at == 0:
-            acc[...] = part if before is None else before[...] + part
+        if k == 0:
+            acc[...] = part
         else:
             acc[...] += part
     for k, out in enumerate(outs):
         out[...] = acc[k * tokens : (k + 1) * tokens, :].astype(out.dtype)
 
 
-def grad_kernel(n, jb, rl, first_k, copies, n_w, aliased, s_ref, own, *refs):
+def grad_kernel(n, jb, rl, blocks, copies, n_w, aliased, s_ref, own, *refs):
     received, refs = refs[: n - 1], refs[n - 1 :]
     (taps, silu, slope), refs = refs[:3], refs[3:]
     cots, refs = refs[:n], refs[n:]
@@ -147,7 +143,7 @@
     outs, (tap_grad, xs, dp, dh, cot_all, w_buf, sems, cot_sems) = refs[:n], refs[n:]
     b, tap_mask = s_ref[0], s_ref[1]
     step = pl.program_id(0)
-    jz = s_ref[3] ^ (step + first_k)
+    jz = s_ref[3] ^ (step * blocks.step + blocks.start)
     tokens, blk = silu.shape[2:]
     cols = tokens // rl
     total = n * rl
@@ -219,21 +215,18 @@
             outs[k][vg, 0] = dh[k, vg]
 
 
-def unpack_kernel(n, jb, blk, sizes, s_ref, *refs):
+def unpack_kernel(n, jb, blk, chunks, s_ref, *refs):
     ins, out, held = refs[:-2], refs[-2], refs[-1]
     b = s_ref[0]
-    rl, cols = ins[0].shape[2:4]
-    done = 0
-    for c, size in enumerate(sizes):
+    for c, blocks in enumerate(chunks):
         for k in range(n):
-            for at in range(size):
-                held[lax.rem(b - k + n, n), :, s_ref[3] ^ (done + at)] = ins[c * n + k][:, at]
-        done += size
+            for at, kz in enumerate(blocks):
+                held[lax.rem(b - k + n, n), :, s_ref[3] ^ kz] = ins[c * n + k][:, at, 0]
     for vg in range(2):
         for jz in range(jb):
             for t in range(n):
                 start = ((vg * jb + jz) * n + t) * blk
-                out[:, start : start + blk] = held[t, vg, jz].reshape(rl * cols, blk)
+                out[:, start : start + blk] = held[t, vg, jz]
 
 
 def unit(hidden_in, tap_weights, tap_bias, w_out, cotangent):
@@ -251,9 +244,25 @@
         [tap_weights, tap_bias[None], jnp.zeros((6, tap_bias.shape[0]), BF16)], axis=0
     )
     if fast:
-        scalars = jnp.stack([b, f, jnp.where(f % 2 == b, 1, 0), f // n, g]).astype(jnp.int32)
+        scalars = jnp.stack([b, f // 2 * 2 + 1 - b, jnp.where(f % 2 == b, 1, 0), f // n, g]).astype(jnp.int32)
     else:
-        scalars = jnp.stack([b, 0 * f, 0 * f + 1, 0 * f, g]).astype(jnp.int32)
+        scalars = jnp.stack([b, 0 * f, 0 * f + 1, 0 * f, 0 * g]).astype(jnp.int32)
+
+    vmem = pl.BlockSpec(memory_space=pltpu.VMEM)
+    smem = pl.BlockSpec(memory_space=pltpu.SMEM)
+    any_spec = pl.BlockSpec(memory_space=pl.ANY)
+    part_shape = (2, jb, rl, cols, blk)
+    packed = pl.pallas_call(
+        functools.partial(pack_kernel, n, jb, blk),
+        grid_spec=pltpu.PrefetchScalarGridSpec(
+            num_scalar_prefetch=1,
+            grid=(rl,),
+            in_specs=[pl.BlockSpec((cols, chans), lambda i, s: (i, 0))],
+            out_specs=[pl.BlockSpec((2, jb, 1, cols, blk), lambda i, s: (0, 0, i, 0, 0))] * n,
+        ),
+        out_shape=[jax.ShapeDtypeStruct(part_shape, BF16)] * n,
+        name="pack",
+    )(scalars, hidden_in.reshape(tokens, chans))
 
     if fast:
         every = ("groups", "fsdp", "band")
@@ -274,8 +283,7 @@
             ]
             return lax.ppermute(x, every, pairs)
 
-        half = lax.dynamic_slice_in_dim(w_out, g * (blk // 2), blk // 2, 0)
-        mine = {0: half}
+        mine = {0: lax.dynamic_slice_in_dim(w_out, g * (blk // 2), blk // 2, 0)}
         order = []
         bit = zr // 2
         while bit:
@@ -287,7 +295,8 @@
         w_parts = []
         for k in range(zr):
             if k == 0:
-                w_parts.append(([w.reshape(2, blk // 2, feats) for w in (w_out, across(w_out, 1))], False))
+                pair = [w_out, across(w_out, 1)]
+                w_parts.append(([w.reshape(2, blk // 2, feats) for w in pair], False))
             else:
                 a, y = mine[k], other_group(mine[k])
                 w_parts.append(([a, y, across(a, 1), across(y, 1)], True))
@@ -299,27 +308,20 @@
         parts = 1
 
     if fast:
-        tap_all = lax.dynamic_slice_in_dim(tap_block, b * blk, blk, 1)[None]
-        step = 1
-        while step < shards:
-            other = lax.ppermute(tap_all, "fsdp", [(i, i ^ step) for i in range(shards)])
-            tap_all = jnp.concatenate([tap_all, other], axis=0)
-            step *= 2
+        tap_own = lax.dynamic_slice_in_dim(tap_block, b * blk, blk, 1)
+        tap_pair = jnp.stack([tap_own, across(tap_own, 1)])
+        tap_all = [tap_pair]
+        for k in range(1, zr):
+            pairs = [
+                (s * n + t, (s ^ 2 * k) * n + t) for s in range(shards) for t in range(n) if s % 2 != t
+            ]
+            tap_all.append(lax.ppermute(tap_pair, ("fsdp", "band"), pairs))
+        tap_all = jnp.concatenate(tap_all, axis=0)
+        tap_all = jnp.where(f % 2 == b, across(tap_all, 1), tap_all)
     else:
         tap_all = lax.all_gather(tap_block, "fsdp", axis=1, tiled=True)
         tap_all = tap_all.reshape(16, 2 * jb, n, blk)
         tap_all = lax.dynamic_index_in_dim(tap_all, b, 2, keepdims=False).transpose(1, 0, 2)
-
-    vmem = pl.BlockSpec(memory_space=pltpu.VMEM)
-    smem = pl.BlockSpec(memory_space=pltpu.SMEM)
-    part_shape = (2, jb, rl, cols, blk)
-    packed = pl.pallas_call(
-        functools.partial(pack_kernel, n, jb, blk),
-        out_shape=[jax.ShapeDtypeStruct(part_shape, BF16)] * n,
-        in_specs=[smem, vmem],
-        out_specs=[vmem] * n,
-        name="pack",
-    )(scalars, hidden_in.reshape(tokens, chans))
 
     def turn(x, k):
         return lax.ppermute(x, "band", [(i, (i + k) % n) for i in range(n)])
@@ -352,11 +354,7 @@
         name="conv",
     )(scalars, packed[0], *hid_in, tap_all)
 
-    any_spec = pl.BlockSpec(memory_space=pl.ANY)
-    chunks, done = [], 0
-    for size in CHUNKS if fast and sum(CHUNKS) == jb else (jb,):
-        chunks.append(range(done, done + size))
-        done += size
+    chunks = [range(jb - 1), range(jb - 1, jb)] if fast else [range(jb)]
 
     def weights_of(blocks):
         if not fast:
@@ -378,40 +376,35 @@
                 ))
         return args, moves
 
-    partial = None
-    for c, blocks in enumerate(chunks):
-        args, moves = weights_of(blocks)
-        first, last = c == 0, c == len(chunks) - 1
-        shapes = [jax.ShapeDtypeStruct((tokens, feats), F32 if k == 0 else BF16) for k in range(n)]
-        total_shape = jax.ShapeDtypeStruct((n * tokens, feats), F32)
-        scratch = [
-            pltpu.VMEM((len(blocks), parts, blk // parts, feats), BF16),
-            pltpu.SemaphoreType.DMA((len(blocks),)),
-        ]
-        if last:
-            scratch = [pltpu.VMEM((n * tokens, feats), F32)] + scratch
-        partial = pl.pallas_call(
-            functools.partial(out_kernel, n, blocks, moves, len(args), first, last),
-            in_specs=[smem] + [vmem] * (1 if first else 2) + [any_spec] * len(args),
-            out_specs=[vmem] * n if last else vmem,
-            out_shape=shapes if last else total_shape,
-            scratch_shapes=scratch,
-        )(scalars, glu, *([] if first else [partial]), *args)
+    args, moves = weights_of(range(jb))
+    partial = pl.pallas_call(
+        functools.partial(out_kernel, n, moves, len(args)),
+        in_specs=[smem, vmem] + [any_spec] * len(args),
+        out_specs=[vmem] * n,
+        out_shape=[jax.ShapeDtypeStruct((tokens, feats), F32 if k == 0 else BF16) for k in range(n)],
+        scratch_shapes=[
+            pltpu.VMEM((n * tokens, feats), F32),
+            pltpu.VMEM((jb, parts, blk // parts, feats), BF16),
+            pltpu.SemaphoreType.DMA((jb,)),
+        ],
+        name="project",
+    )(scalars, glu, *args)
     partial = [p.reshape(cotangent.shape) for p in partial]
     block_out = partial[0]
-    for k in range(1, n):
-        block_out = block_out + turn(partial[k], k).astype(F32)
+    others = [turn(partial[k], k) for k in range(1, n)]
+    for other in others:
+        block_out = block_out + other.astype(F32)
     block_out = block_out.astype(BF16)
 
     tap_grad, d_parts = None, []
     for blocks in chunks:
         args, moves = weights_of(blocks)
-        at = lambda j, s, lo=blocks[0]: s[3] ^ (j + lo)
+        at = lambda j, s, c=blocks: s[3] ^ (j * c.step + c.start)
         part_at = pl.BlockSpec((2, 1, rl, cols, blk), lambda j, s, at=at: (0, at(j, s), 0, 0, 0))
         act_at = pl.BlockSpec((1, n, tokens, blk), lambda j, s, at=at: (at(j, s), 0, 0, 0))
         aliased = 0 if tap_grad is None else 1
         outs = pl.pallas_call(
-            functools.partial(grad_kernel, n, jb, rl, blocks[0], moves, len(args), aliased),
+            functools.partial(grad_kernel, n, jb, rl, blocks, moves, len(args), aliased),
             grid_spec=pltpu.PrefetchScalarGridSpec(
                 num_scalar_prefetch=1,
                 grid=(len(blocks),),
@@ -438,11 +431,17 @@
         tap_grad = outs[n]
         d_parts += [outs[0]] + [turn(outs[k], k) for k in range(1, n)]
     d_hidden = pl.pallas_call(
-        functools.partial(unpack_kernel, n, jb, blk, [len(c) for c in chunks]),
-        in_specs=[smem] + [vmem] * len(d_parts),
-        out_specs=vmem,
+        functools.partial(unpack_kernel, n, jb, blk, chunks),
+        grid_spec=pltpu.PrefetchScalarGridSpec(
+            num_scalar_prefetch=1,
+            grid=(rl,),
+            in_specs=[
+                pl.BlockSpec((2, p.shape[1], 1, cols, blk), lambda i, s: (0, 0, i, 0, 0)) for p in d_parts
+            ],
+            out_specs=pl.BlockSpec((cols, chans), lambda i, s: (i, 0)),
+            scratch_shapes=[pltpu.VMEM((n, 2, jb, cols, blk), BF16)],
+        ),
         out_shape=jax.ShapeDtypeStruct((tokens, chans), BF16),
-        scratch_shapes=[pltpu.VMEM((n,) + part_shape, BF16)],
         name="unpack",
     )(scalars, *d_parts)
 
@@ -468,9 +467,6 @@
     )
 
 
-CHUNKS = (3, 1)
-
-
 def solution(mesh):
     placed = (
         P(("groups", "fsdp"), "band", None, None),

time: 146 us -> 144 us (0.986)
  starting transfers between devices: 33.8 us -> 45 us
  waiting for transfers between devices: 59 us -> 49.2 us
  Pallas kernels: 43.4 us -> 40.1 us
    ppermute x3, waiting for transfers between devices: 13.3 us -> 0.01 us  [unit(): tap_all.append(lax.ppermute(tap_pair, ('fsdp', 'band'), pairs))]
    ppermute x10 -> x12, starting transfers between devices: 14.9 us -> 22.1 us  [across(): return lax.ppermute(x, ('fsdp', 'band'), pairs)]
    ppermute x10 -> x12, waiting for transfers between devices: 0.03 us -> 5.78 us  [across(): return lax.ppermute(x, ('fsdp', 'band'), pairs)]
    ppermute x3, waiting for transfers between devices: 15.3 us -> 9.92 us  [other_group(): return lax.ppermute(x, every, pairs)]
    pallas_call x6 -> x5, Pallas kernels: 37.3 us -> 34 us  [the longest x2 18.2 us: unit(): pl.pallas_call(functools.partial(grad_kernel, n, jb, rl, blocks, moves, l...]
    ppermute x6, waiting for transfers between devices: 30.3 us -> 33.5 us  [turn(): return lax.ppermute(x, 'band', [(i, (i + k) % n) for i in range(n)])]
    ppermute x6, starting transfers between devices: 4.56 us -> 6.34 us  [turn(): return lax.ppermute(x, 'band', [(i, (i + k) % n) for i in range(n)])]
  transfers between devices with their start and end apart: 23 -> 25, of which waited for: 5 -> 5; matrix products, arithmetic and copies ran while one was open for 2% -> 2% of each run, Pallas kernels for 30% -> 28%
where the time goes in v3:
time: 144 us; the launch traced here: 143 us
  waiting for transfers between devices  49.2 us (34%)
  starting transfers between devices  45 us (31%)
  Pallas kernels  40.1 us (28%)
  local copies, waits for them, and re-layouts  4.78 us (3%)
  other arithmetic  3.07 us (2%)
    ppermute x6, waiting for transfers between devices, turn(): return lax.ppermute(x, 'band', [(i, (i + k) % n) for i in range(n)])  33.5 us
    ppermute x12, starting transfers between devices, across(): return lax.ppermute(x, ('fsdp', 'band'), pairs)  22.1 us
    pallas_call x2, Pallas kernels, unit(): pl.pallas_call(functools.partial(grad_kernel, n, jb, rl, blocks, moves, l...  18.2 us
    ppermute x3, starting transfers between devices, other_group(): return lax.ppermute(x, every, pairs)  10.3 us
    ppermute x3, waiting for transfers between devices, other_group(): return lax.ppermute(x, every, pairs)  9.92 us
    pallas_call x1, Pallas kernels, unit(): pl.pallas_call(functools.partial(out_kernel, n, moves, len(args)), in_spe...  7.31 us
    ppermute x6, starting transfers between devices, turn(): return lax.ppermute(x, 'band', [(i, (i + k) % n) for i in range(n)])  6.34 us
    pallas_call x1, Pallas kernels, unit(): pl.pallas_call(functools.partial(conv_kernel, n, jb, rl), grid_spec=pltpu...  6.14 us
  transfers between devices with their start and end apart: 25, of which 5 were waited for; matrix products, arithmetic and copies ran while one was open for 2% of the time, Pallas kernels for 28%

profile of v3, /device:TPU:0, one launch (start us, length us, event | category | flops | bytes accessed | tf_op | source)
XLA Modules:
  0.0 143.1 jit_solution(12117240450612331162)
XLA Ops:
  0.6 0.0 copy-start
  0.7 2.2 %constant_dynamic-slice_fusion = bf16[176,2240]{1,0:T(8,128)(2,1)} fusion(bf16[352,2240]{1,0:T(8,128)(2,1)} %param.8, s32[]{:T(128)S(6)} %select_n.50), kind=kLoop, calls=%fused_computation.17 | loop fusion | bytes 1576964 | tf_op jit(solution)/shard_map/dynamic_slice | solution.py:286
  2.9 6.0 %collective-permute-start.11 = (bf16[176,2240]{1,0:T(8,128)(2,1)}, bf16[176,2240]{1,0:T(8,128)(2,1)S(1)}, u32[]{:S(2)}, u32[]{:S(2)}) collective-permute-start(bf16[176,2240]{1,0:T(8,128)(2,1)} %constant_dynamic-slice_fusion), channel_id=1, source_target_pairs={{0,8},{3,11},{4,12},{7,15},{8,0},{11,3},{12,4},{15,7},{16,24},{19,... | collective-permute-start | bytes 2365448 | tf_op jit(solution)/shard_map/ppermute | solution.py:276
  8.9 0.1 pad.6.clone
  9.0 0.1 constant_dynamic-update-slice_fusion.4
  9.1 0.1 collective-permute-start.1
  9.1 0.5 collective-permute-start.6
  9.6 3.5 %collective-permute-start.7 = (bf16[176,2240]{1,0:T(8,128)(2,1)}, bf16[176,2240]{1,0:T(8,128)(2,1)}, u32[]{:S(2)}, u32[]{:S(2)}) collective-permute-start(bf16[176,2240]{1,0:T(8,128)(2,1)} %constant_dynamic-slice_fusion), channel_id=1, source_target_pairs={{0,4},{3,7},{4,0},{7,3},{8,12},{11,15},{12,8},{15,11},{16,20},{19,... | collective-permute-start | bytes 2365448 | tf_op jit(solution)/shard_map/ppermute | solution.py:276
  13.1 0.0 collective-permute-done.1
  13.1 0.7 collective-permute-start.2
  13.8 0.7 collective-permute-start.3
  14.5 0.0 collective-permute-done.2
  14.5 0.7 collective-permute-start.4
  15.2 0.0 collective-permute-done.3
  15.2 0.0 collective-permute-done.4
  15.2 8.0 %collective-permute-start.5 = (bf16[8,16,352]{2,1,0:T(8,128)(2,1)S(1)}, bf16[8,16,352]{2,1,0:T(8,128)(2,1)S(1)}, u32[]{:S(2)}, u32[]{:S(2)}) collective-permute-start(bf16[8,16,352]{2,1,0:T(8,128)(2,1)S(1)} %constant_dynamic-update-slice_fusion), channel_id=1, source_target_pairs={{0,2},{1,3},{2,0},{3,1},{4,6},{5,7},{6,4},{7,5},{8,10},{9,11},{10,... | collective-permute-start | bytes 270344 | tf_op jit(solution)/shard_map/ppermute | solution.py:276
  23.3 5.8 %collective-permute-done.11.refs_6_.refs_12_ = bf16[176,2240]{1,0:T(8,128)(2,1)S(1)} collective-permute-done((bf16[176,2240]{1,0:T(8,128)(2,1)}, bf16[176,2240]{1,0:T(8,128)(2,1)S(1)}, u32[]{:S(2)}, u32[]{:S(2)}) %collective-permute-start.11) | collective-permute-done | bytes 788512 | tf_op jit(solution)/shard_map/ppermute | solution.py:276
  29.0 3.0 %collective-permute-start.15 = (bf16[176,2240]{1,0:T(8,128)(2,1)S(1)}, bf16[176,2240]{1,0:T(8,128)(2,1)}, u32[]{:S(2)}, u32[]{:S(2)}) collective-permute-start(bf16[176,2240]{1,0:T(8,128)(2,1)S(1)} %collective-permute-done.11.refs_6_.refs_12_), channel_id=1, source_target_pairs={{0,4},{3,7},{4,0},{7,3},{8,12},{11,15},{12,8},{15,11},{16,20},{19,... | collective-permute-start | bytes 2365448 | tf_op jit(solution)/shard_map/ppermute | solution.py:276
  32.0 0.1 collective-permute-start.20
  32.1 0.6 stack.32.s_ref
  32.7 4.9 %pack.1 = (bf16[2,4,2,64,352]{4,3,2,1,0:T(8,128)(2,1)}, bf16[2,4,2,64,352]{4,3,2,1,0:T(8,128)(2,1)}) custom-call(s32[5]{0:T(128)} %stack.32.s_ref, bf16[128,5632]{1,0:T(8,128)(2,1)} %bitcast.22), custom_call_target="tpu_custom_call" | custom-call | tf_op jit(solution)/shard_map/pack/pallas_call | solution.py:255
  37.7 0.0 collective-permute-done.5
  37.7 2.0 %collective-permute-start = (bf16[2,4,2,64,352]{4,3,2,1,0:T(8,128)(2,1)}, bf16[2,4,2,64,352]{4,3,2,1,0:T(8,128)(2,1)S(1)}, u32[]{:S(2)}, u32[]{:S(2)}) collective-permute-start(bf16[2,4,2,64,352]{4,3,2,1,0:T(8,128)(2,1)} %get-tuple-element.18), channel_id=1, source_target_pairs={{0,1},{1,0},{2,3},{3,2},{4,5},{5,4},{6,7},{7,6},{8,9},{9,8},{10,11... | collective-permute-start | bytes 2162696 | tf_op jit(solution)/shard_map/ppermute | solution.py:327
  39.7 0.0 collective-permute-done.7.refs_2_.refs_8_
  39.7 3.4 %collective-permute-start.8 = (bf16[176,2240]{1,0:T(8,128)(2,1)}, bf16[176,2240]{1,0:T(8,128)(2,1)}, u32[]{:S(2)}, u32[]{:S(2)}) collective-permute-start(bf16[176,2240]{1,0:T(8,128)(2,1)} %collective-permute-done.7.refs_2_.refs_8_), channel_id=1, source_target_pairs={{0,16},{3,19},{4,20},{7,23},{8,24},{11,27},{12,28},{15,31},{16,0},... | collective-permute-start | bytes 2365448 | tf_op jit(solution)/shard_map/ppermute | solution.py:284
  43.1 5.5 %collective-permute-done.20 = bf16[1,2,64,2240]{3,2,1,0:T(8,128)(2,1)} collective-permute-done((bf16[1,2,64,2240]{3,2,1,0:T(8,128)(2,1)}, bf16[1,2,64,2240]{3,2,1,0:T(8,128)(2,1)}, u32[]{:S(2)}, u32[]{:S(2)}) %collective-permute-start.20) | collective-permute-done | bytes 573472 | tf_op jit(solution)/shard_map/ppermute | solution.py:327
  48.6 3.4 %collective-permute-start.12 = (bf16[176,2240]{1,0:T(8,128)(2,1)S(1)}, bf16[176,2240]{1,0:T(8,128)(2,1)}, u32[]{:S(2)}, u32[]{:S(2)}) collective-permute-start(bf16[176,2240]{1,0:T(8,128)(2,1)S(1)} %collective-permute-done.11.refs_6_.refs_12_), channel_id=1, source_target_pairs={{0,16},{3,19},{4,20},{7,23},{8,24},{11,27},{12,28},{15,31},{16,0},... | collective-permute-start | bytes 2365448 | tf_op jit(solution)/shard_map/ppermute | solution.py:284
  52.0 10.9 %collective-permute-done.refs_0_ = bf16[2,4,2,64,352]{4,3,2,1,0:T(8,128)(2,1)S(1)} collective-permute-done((bf16[2,4,2,64,352]{4,3,2,1,0:T(8,128)(2,1)}, bf16[2,4,2,64,352]{4,3,2,1,0:T(8,128)(2,1)S(1)}, u32[]{:S(2)}, u32[]{:S(2)}) %collective-permute-start) | collective-permute-done | bytes 720928 | tf_op jit(solution)/shard_map/ppermute | solution.py:327
  62.9 0.0 collective-permute-start.9
  62.9 0.0 collective-permute-done.15.refs_10_.refs_6_
  62.9 3.4 %collective-permute-start.16 = (bf16[176,2240]{1,0:T(8,128)(2,1)}, bf16[176,2240]{1,0:T(8,128)(2,1)}, u32[]{:S(2)}, u32[]{:S(2)}) collective-permute-start(bf16[176,2240]{1,0:T(8,128)(2,1)} %collective-permute-done.15.refs_10_.refs_6_), channel_id=1, source_target_pairs={{0,16},{3,19},{4,20},{7,23},{8,24},{11,27},{12,28},{15,31},{16,0},... | collective-permute-start | bytes 2365448 | tf_op jit(solution)/shard_map/ppermute | solution.py:284
  66.3 0.0 collective-permute-done.6
  66.3 0.1 collective-permute-start.13
  66.4 0.5 collective-permute-start.10
  66.9 0.0 collective-permute-done.12.refs_7_.refs_13_
  66.9 0.1 collective-permute-start.14
  67.0 0.0 collective-permute-done.9.refs_4_.refs_10_
  67.0 0.4 collective-permute-start.17
  67.4 9.9 %collective-permute-done.16.refs_11_.refs_7_ = bf16[176,2240]{1,0:T(8,128)(2,1)} collective-permute-done((bf16[176,2240]{1,0:T(8,128)(2,1)}, bf16[176,2240]{1,0:T(8,128)(2,1)}, u32[]{:S(2)}, u32[]{:S(2)}) %collective-permute-start.16) | collective-permute-done | bytes 788512 | tf_op jit(solution)/shard_map/ppermute | solution.py:284
  77.4 0.7 broadcast_select_fusion.refs_1_
  78.0 6.1 %conv.1 = (bf16[4,2,128,352]{3,2,1,0:T(8,128)(2,1)}, f32[4,2,128,352]{3,2,1,0:T(8,128)}, f32[4,2,128,352]{3,2,1,0:T(8,128)}) custom-call(s32[5]{0:T(128)} %stack.32.s_ref, bf16[2,4,2,64,352]{4,3,2,1,0:T(8,128)(2,1)} %get-tuple-element.17.own, bf16[2,4,2,64,352]{4,3,2,1,0:T(8,128)(2,1)} %copy-done.1, bf16[8,16,352]{2,1,0:T(8,128)(2,1)} %broadcast_select_fusion.refs_1_), custom_call_target="tpu_custom_call" | custom-call | tf_op jit(solution)/shard_map/conv/pallas_call | solution.py:337
  84.2 0.0 collective-permute-done.10.refs_5_.refs_11_
  84.2 0.0 copy-start.4
  84.2 0.9 copy-done.3
  85.1 0.3 copy-done.4
  85.3 11.8 %shard_map.84 = (bf16[2,3,2,64,352]{4,3,2,1,0:T(8,128)(2,1)}, bf16[2,3,2,64,352]{4,3,2,1,0:T(8,128)(2,1)}, f32[2,4,16,352]{3,2,1,0:T(8,128)}) custom-call(s32[5]{0:T(128)} %stack.32.s_ref, bf16[2,4,2,64,352]{4,3,2,1,0:T(8,128)(2,1)} %get-tuple-element.17.own, bf16[2,4,2,64,352]{4,3,2,1,0:T(8,128)(2,1)} %copy-done.1, ...), custom_call_target="tpu_custom_call" | custom-call | tf_op jit(solution)/shard_map/pallas_call | solution.py:406
  97.1 0.9 collective-permute-start.21
  98.1 0.0 collective-permute-done.17.refs_12_.refs_8_
  98.1 0.0 collective-permute-done.18.refs_13_.refs_9_
  98.1 6.5 %shard_map.85 = (bf16[2,1,2,64,352]{4,3,2,1,0:T(8,128)(2,1)}, bf16[2,1,2,64,352]{4,3,2,1,0:T(8,128)(2,1)}, f32[2,4,16,352]{3,2,1,0:T(8,128)}) custom-call(s32[5]{0:T(128)} %stack.32.s_ref, bf16[2,4,2,64,352]{4,3,2,1,0:T(8,128)(2,1)} %get-tuple-element.17.own, bf16[2,4,2,64,352]{4,3,2,1,0:T(8,128)(2,1)} %copy-done.1, ...), custom_call_target="tpu_custom_call", output_to_operand_aliasing={{2}: (12, {})} | custom-call | tf_op jit(solution)/shard_map/pallas_call | solution.py:406
  104.5 4.3 %all-to-all-start = ((f32[8,16,352]{2,1,0:T(8,128)}), f32[8,16,352]{2,1,0:T(8,128)S(1)}, u32[]{:S(2)}, u32[]{:S(2)}) async-start(f32[8,16,352]{2,1,0:T(8,128)} %bitcast.25), calls=%async_computation | async-start | bytes 393216 | tf_op jit(solution)/shard_map/all_to_all | solution.py:450
  108.9 7.3 %project.1 = (f32[128,2240]{1,0:T(8,128)}, bf16[128,2240]{1,0:T(8,128)(2,1)}) custom-call(s32[5]{0:T(128)} %stack.32.s_ref, bf16[4,2,128,352]{3,2,1,0:T(8,128)(2,1)} %get-tuple-element.19.glu, bf16[2,176,2240]{2,1,0:T(8,128)(2,1)} %bitcast.19, bf16[2,176,2240]{2,1,0:T(8,128)(2,1)} %bitcast.9.refs_1_.refs_7_, ...), custom_call_target="tpu_custom_call" | custom-call | tf_op jit(solution)/shard_map/project/pallas_call | solution.py:380
  116.2 1.2 collective-permute-start.19
  117.4 0.9 collective-permute-start.22
  118.3 0.0 all-to-all-done
  118.3 1.2 collective-permute-start.23
  119.5 0.0 collective-permute-done.21.refs_1_
  119.5 17.1 %collective-permute-done.22.refs_3_ = bf16[2,1,2,64,352]{4,3,2,1,0:T(8,128)(2,1)S(1)} collective-permute-done((bf16[2,1,2,64,352]{4,3,2,1,0:T(8,128)(2,1)S(1)}, bf16[2,1,2,64,352]{4,3,2,1,0:T(8,128)(2,1)S(1)}, u32[]{:S(2)}, u32[]{:S(2)}) %collective-permute-start.22) | collective-permute-done | bytes 180256 | tf_op jit(solution)/shard_map/ppermute | solution.py:327
  136.7 0.7 copy-done.7
  137.3 3.5 %unpack.1 = bf16[128,5632]{1,0:T(8,128)(2,1)} custom-call(s32[5]{0:T(128)} %stack.32.s_ref, bf16[2,3,2,64,352]{4,3,2,1,0:T(8,128)(2,1)} %get-tuple-element.24.refs_0_, bf16[2,3,2,64,352]{4,3,2,1,0:T(8,128)(2,1)} %copy-done.6, bf16[2,1,2,64,352]{4,3,2,1,0:T(8,128)(2,1)} %get-tuple-element.27.refs_2_, bf16[2,1,2,64,352]{4,3,2,1,0:T(8,128)(2,1)} %copy-done.7), custom_call_target="tpu_custom_call" | custom-call | tf_op jit(solution)/shard_map/unpack/pallas_call | solution.py:433
  140.8 0.7 fusion.2
  141.5 0.7 slice_maximum_fusion
  142.2 0.0 collective-permute-done.19
  142.2 0.9 add_convert_fusion
  (31 shorter events, 0.1 us)
Async XLA Ops:
  0.6 8.5 %copy-start = (bf16[352,2240]{1,0:T(8,128)(2,1)S(1)}, bf16[352,2240]{1,0:T(8,128)(2,1)}, u32[]{:S(2)}) copy-start(bf16[352,2240]{1,0:T(8,128)(2,1)} %param.8) | copy-start | bytes 4730884
  0.6 8.2 %copy-start.9 = (bf16[704]{0:T(1024)(128)(2,1)S(1)}, bf16[704]{0:T(1024)(128)(2,1)}, u32[]{:S(2)}) copy-start(bf16[704]{0:T(1024)(128)(2,1)} %param.7) | copy-start | bytes 4228
  0.7 8.3 %copy-start.8 = (bf16[9,704]{1,0:T(8,128)(2,1)S(1)}, bf16[9,704]{1,0:T(8,128)(2,1)}, u32[]{:S(2)}) copy-start(bf16[9,704]{1,0:T(8,128)(2,1)} %param.6) | copy-start | bytes 38020
  2.9 26.1 %collective-permute-start.11 = (bf16[176,2240]{1,0:T(8,128)(2,1)}, bf16[176,2240]{1,0:T(8,128)(2,1)S(1)}, u32[]{:S(2)}, u32[]{:S(2)}) collective-permute-start(bf16[176,2240]{1,0:T(8,128)(2,1)} %constant_dynamic-slice_fusion), channel_id=1, source_target_pairs={{0,8},{3,11},{4,12},{7,15},{8,0},{11,3},{12,4},{15,7},{16,24},{19,... | collective-permute-start | bytes 2365448 | tf_op jit(solution)/shard_map/ppermute | solution.py:276
  9.1 4.1 %collective-permute-start.1 = (bf16[16,352]{1,0:T(8,128)(2,1)S(1)}, bf16[16,352]{1,0:T(8,128)(2,1)S(1)}, u32[]{:S(2)}, u32[]{:S(2)}) collective-permute-start(bf16[16,352]{1,0:T(8,128)(2,1)S(1)} %get-tuple-element.31), channel_id=1, source_target_pairs={{0,2},{1,3},{2,0},{3,1},{4,6},{5,7},{6,4},{7,5},{8,10},{9,11},{10,... | collective-permute-start | bytes 33800 | tf_op jit(solution)/shard_map/ppermute | solution.py:276
  9.1 57.2 %collective-permute-start.6 = (bf16[352,2240]{1,0:T(8,128)(2,1)S(1)}, bf16[352,2240]{1,0:T(8,128)(2,1)}, u32[]{:S(2)}, u32[]{:S(2)}) collective-permute-start(bf16[352,2240]{1,0:T(8,128)(2,1)S(1)} %copy-done), channel_id=1, source_target_pairs={{0,2},{1,3},{2,0},{3,1},{4,6},{5,7},{6,4},{7,5},{8,10},{9,11},{10,... | collective-permute-start | bytes 4730888 | tf_op jit(solution)/shard_map/ppermute | solution.py:276
  9.6 30.0 %collective-permute-start.7 = (bf16[176,2240]{1,0:T(8,128)(2,1)}, bf16[176,2240]{1,0:T(8,128)(2,1)}, u32[]{:S(2)}, u32[]{:S(2)}) collective-permute-start(bf16[176,2240]{1,0:T(8,128)(2,1)} %constant_dynamic-slice_fusion), channel_id=1, source_target_pairs={{0,4},{3,7},{4,0},{7,3},{8,12},{11,15},{12,8},{15,11},{16,20},{19,... | collective-permute-start | bytes 2365448 | tf_op jit(solution)/shard_map/ppermute | solution.py:276
  13.1 1.4 collective-permute-start.2
  13.8 1.4 collective-permute-start.3
  14.5 0.7 collective-permute-start.4
  15.2 22.4 %collective-permute-start.5 = (bf16[8,16,352]{2,1,0:T(8,128)(2,1)S(1)}, bf16[8,16,352]{2,1,0:T(8,128)(2,1)S(1)}, u32[]{:S(2)}, u32[]{:S(2)}) collective-permute-start(bf16[8,16,352]{2,1,0:T(8,128)(2,1)S(1)} %constant_dynamic-update-slice_fusion), channel_id=1, source_target_pairs={{0,2},{1,3},{2,0},{3,1},{4,6},{5,7},{6,4},{7,5},{8,10},{9,11},{10,... | collective-permute-start | bytes 270344 | tf_op jit(solution)/shard_map/ppermute | solution.py:276
  29.0 55.1 %copy-start.2 = (bf16[176,2240]{1,0:T(8,128)(2,1)}, bf16[176,2240]{1,0:T(8,128)(2,1)S(1)}, u32[]{:S(2)}) copy-start(bf16[176,2240]{1,0:T(8,128)(2,1)S(1)} %collective-permute-done.11.refs_6_.refs_12_) | copy-start | bytes 2365444
  29.0 33.9 %collective-permute-start.15 = (bf16[176,2240]{1,0:T(8,128)(2,1)S(1)}, bf16[176,2240]{1,0:T(8,128)(2,1)}, u32[]{:S(2)}, u32[]{:S(2)}) collective-permute-start(bf16[176,2240]{1,0:T(8,128)(2,1)S(1)} %collective-permute-done.11.refs_6_.refs_12_), channel_id=1, source_target_pairs={{0,4},{3,7},{4,0},{7,3},{8,12},{11,15},{12,8},{15,11},{16,20},{19,... | collective-permute-start | bytes 2365448 | tf_op jit(solution)/shard_map/ppermute | solution.py:276
  32.0 16.6 %collective-permute-start.20 = (bf16[1,2,64,2240]{3,2,1,0:T(8,128)(2,1)}, bf16[1,2,64,2240]{3,2,1,0:T(8,128)(2,1)}, u32[]{:S(2)}, u32[]{:S(2)}) collective-permute-start(bf16[1,2,64,2240]{3,2,1,0:T(8,128)(2,1)} %param.9), channel_id=1, source_target_pairs={{0,1},{1,0},{2,3},{3,2},{4,5},{5,4},{6,7},{7,6},{8,9},{9,8},{10,11... | collective-permute-start | bytes 1720328 | tf_op jit(solution)/shard_map/ppermute | solution.py:327
  37.7 25.2 %collective-permute-start = (bf16[2,4,2,64,352]{4,3,2,1,0:T(8,128)(2,1)}, bf16[2,4,2,64,352]{4,3,2,1,0:T(8,128)(2,1)S(1)}, u32[]{:S(2)}, u32[]{:S(2)}) collective-permute-start(bf16[2,4,2,64,352]{4,3,2,1,0:T(8,128)(2,1)} %get-tuple-element.18), channel_id=1, source_target_pairs={{0,1},{1,0},{2,3},{3,2},{4,5},{5,4},{6,7},{7,6},{8,9},{9,8},{10,11... | collective-permute-start | bytes 2162696 | tf_op jit(solution)/shard_map/ppermute | solution.py:327
  39.7 26.8 %collective-permute-start.8 = (bf16[176,2240]{1,0:T(8,128)(2,1)}, bf16[176,2240]{1,0:T(8,128)(2,1)}, u32[]{:S(2)}, u32[]{:S(2)}) collective-permute-start(bf16[176,2240]{1,0:T(8,128)(2,1)} %collective-permute-done.7.refs_2_.refs_8_), channel_id=1, source_target_pairs={{0,16},{3,19},{4,20},{7,23},{8,24},{11,27},{12,28},{15,31},{16,0},... | collective-permute-start | bytes 2365448 | tf_op jit(solution)/shard_map/ppermute | solution.py:284
  48.6 18.3 %collective-permute-start.12 = (bf16[176,2240]{1,0:T(8,128)(2,1)S(1)}, bf16[176,2240]{1,0:T(8,128)(2,1)}, u32[]{:S(2)}, u32[]{:S(2)}) collective-permute-start(bf16[176,2240]{1,0:T(8,128)(2,1)S(1)} %collective-permute-done.11.refs_6_.refs_12_), channel_id=1, source_target_pairs={{0,16},{3,19},{4,20},{7,23},{8,24},{11,27},{12,28},{15,31},{16,0},... | collective-permute-start | bytes 2365448 | tf_op jit(solution)/shard_map/ppermute | solution.py:284
  62.9 15.1 %copy-start.1 = (bf16[2,4,2,64,352]{4,3,2,1,0:T(8,128)(2,1)}, bf16[2,4,2,64,352]{4,3,2,1,0:T(8,128)(2,1)S(1)}, u32[]{:S(2)}) copy-start(bf16[2,4,2,64,352]{4,3,2,1,0:T(8,128)(2,1)S(1)} %collective-permute-done.refs_0_) | copy-start | bytes 2162692
  62.9 4.1 %collective-permute-start.9 = (bf16[176,2240]{1,0:T(8,128)(2,1)}, bf16[176,2240]{1,0:T(8,128)(2,1)}, u32[]{:S(2)}, u32[]{:S(2)}) collective-permute-start(bf16[176,2240]{1,0:T(8,128)(2,1)} %collective-permute-done.7.refs_2_.refs_8_), channel_id=1, source_target_pairs={{0,2},{1,3},{2,0},{3,1},{4,6},{5,7},{6,4},{7,5},{8,10},{9,11},{10,... | collective-permute-start | bytes 2365448 | tf_op jit(solution)/shard_map/ppermute | solution.py:276
  62.9 14.5 %collective-permute-start.16 = (bf16[176,2240]{1,0:T(8,128)(2,1)}, bf16[176,2240]{1,0:T(8,128)(2,1)}, u32[]{:S(2)}, u32[]{:S(2)}) collective-permute-start(bf16[176,2240]{1,0:T(8,128)(2,1)} %collective-permute-done.15.refs_10_.refs_6_), channel_id=1, source_target_pairs={{0,16},{3,19},{4,20},{7,23},{8,24},{11,27},{12,28},{15,31},{16,0},... | collective-permute-start | bytes 2365448 | tf_op jit(solution)/shard_map/ppermute | solution.py:284
  66.3 17.8 %collective-permute-start.13 = (bf16[176,2240]{1,0:T(8,128)(2,1)S(1)}, bf16[176,2240]{1,0:T(8,128)(2,1)S(1)}, u32[]{:S(2)}, u32[]{:S(2)}) collective-permute-start(bf16[176,2240]{1,0:T(8,128)(2,1)S(1)} %collective-permute-done.11.refs_6_.refs_12_), channel_id=1, source_target_pairs={{0,2},{1,3},{2,0},{3,1},{4,6},{5,7},{6,4},{7,5},{8,10},{9,11},{10,... | collective-permute-start | bytes 2365448 | tf_op jit(solution)/shard_map/ppermute | solution.py:276
  66.4 17.7 %collective-permute-start.10 = (bf16[176,2240]{1,0:T(8,128)(2,1)}, bf16[176,2240]{1,0:T(8,128)(2,1)S(1)}, u32[]{:S(2)}, u32[]{:S(2)}) collective-permute-start(bf16[176,2240]{1,0:T(8,128)(2,1)} %collective-permute-done.8.refs_3_.refs_9_), channel_id=1, source_target_pairs={{0,2},{1,3},{2,0},{3,1},{4,6},{5,7},{6,4},{7,5},{8,10},{9,11},{10,... | collective-permute-start | bytes 2365448 | tf_op jit(solution)/shard_map/ppermute | solution.py:276
  66.9 17.3 %collective-permute-start.14 = (bf16[176,2240]{1,0:T(8,128)(2,1)}, bf16[176,2240]{1,0:T(8,128)(2,1)}, u32[]{:S(2)}, u32[]{:S(2)}) collective-permute-start(bf16[176,2240]{1,0:T(8,128)(2,1)} %collective-permute-done.12.refs_7_.refs_13_), channel_id=1, source_target_pairs={{0,2},{1,3},{2,0},{3,1},{4,6},{5,7},{6,4},{7,5},{8,10},{9,11},{10,... | collective-permute-start | bytes 2365448 | tf_op jit(solution)/shard_map/ppermute | solution.py:276
  67.0 31.1 %collective-permute-start.17 = (bf16[176,2240]{1,0:T(8,128)(2,1)}, bf16[176,2240]{1,0:T(8,128)(2,1)}, u32[]{:S(2)}, u32[]{:S(2)}) collective-permute-start(bf16[176,2240]{1,0:T(8,128)(2,1)} %collective-permute-done.15.refs_10_.refs_6_), channel_id=1, source_target_pairs={{0,2},{1,3},{2,0},{3,1},{4,6},{5,7},{6,4},{7,5},{8,10},{9,11},{10,... | collective-permute-start | bytes 2365448 | tf_op jit(solution)/shard_map/ppermute | solution.py:276
  77.4 20.7 %collective-permute-start.18 = (bf16[176,2240]{1,0:T(8,128)(2,1)}, bf16[176,2240]{1,0:T(8,128)(2,1)}, u32[]{:S(2)}, u32[]{:S(2)}) collective-permute-start(bf16[176,2240]{1,0:T(8,128)(2,1)} %collective-permute-done.16.refs_11_.refs_7_), channel_id=1, source_target_pairs={{0,2},{1,3},{2,0},{3,1},{4,6},{5,7},{6,4},{7,5},{8,10},{9,11},{10,... | collective-permute-start | bytes 2365448 | tf_op jit(solution)/shard_map/ppermute | solution.py:276
  84.2 0.9 copy-start.3
  84.2 1.1 copy-start.4
  97.1 22.4 %collective-permute-start.21 = (bf16[2,3,2,64,352]{4,3,2,1,0:T(8,128)(2,1)}, bf16[2,3,2,64,352]{4,3,2,1,0:T(8,128)(2,1)S(1)}, u32[]{:S(2)}, u32[]{:S(2)}) collective-permute-start(bf16[2,3,2,64,352]{4,3,2,1,0:T(8,128)(2,1)} %get-tuple-element.25), channel_id=1, source_target_pairs={{0,1},{1,0},{2,3},{3,2},{4,5},{5,4},{6,7},{7,6},{8,9},{9,8},{10,11... | collective-permute-start | bytes 1622024 | tf_op jit(solution)/shard_map/ppermute | solution.py:327
  104.5 13.7 %all-to-all-start = ((f32[8,16,352]{2,1,0:T(8,128)}), f32[8,16,352]{2,1,0:T(8,128)S(1)}, u32[]{:S(2)}, u32[]{:S(2)}) async-start(f32[8,16,352]{2,1,0:T(8,128)} %bitcast.25), calls=%async_computation | async-start | bytes 393216 | tf_op jit(solution)/shard_map/all_to_all | solution.py:450
  108.8 8.6 %copy-start.10 = (bf16[2,1,2,64,352]{4,3,2,1,0:T(8,128)(2,1)S(1)}, bf16[2,1,2,64,352]{4,3,2,1,0:T(8,128)(2,1)}, u32[]{:S(2)}) copy-start(bf16[2,1,2,64,352]{4,3,2,1,0:T(8,128)(2,1)} %get-tuple-element.28) | copy-start | bytes 540676
  116.2 26.0 %collective-permute-start.19 = (bf16[1,2,64,2240]{3,2,1,0:T(8,128)(2,1)}, bf16[1,2,64,2240]{3,2,1,0:T(8,128)(2,1)S(1)}, u32[]{:S(2)}, u32[]{:S(2)}) collective-permute-start(bf16[1,2,64,2240]{3,2,1,0:T(8,128)(2,1)} %bitcast.28), channel_id=1, source_target_pairs={{0,1},{1,0},{2,3},{3,2},{4,5},{5,4},{6,7},{7,6},{8,9},{9,8},{10,11... | collective-permute-start | bytes 1720328 | tf_op jit(solution)/shard_map/ppermute | solution.py:327
  117.4 19.2 %collective-permute-start.22 = (bf16[2,1,2,64,352]{4,3,2,1,0:T(8,128)(2,1)S(1)}, bf16[2,1,2,64,352]{4,3,2,1,0:T(8,128)(2,1)S(1)}, u32[]{:S(2)}, u32[]{:S(2)}) collective-permute-start(bf16[2,1,2,64,352]{4,3,2,1,0:T(8,128)(2,1)S(1)} %copy-done.10), channel_id=1, source_target_pairs={{0,1},{1,0},{2,3},{3,2},{4,5},{5,4},{6,7},{7,6},{8,9},{9,8},{10,11... | collective-permute-start | bytes 540680 | tf_op jit(solution)/shard_map/ppermute | solution.py:327
  118.3 22.5 %collective-permute-start.23 = (f32[16,352]{1,0:T(8,128)S(1)}, f32[16,352]{1,0:T(8,128)S(1)}, u32[]{:S(2)}, u32[]{:S(2)}) collective-permute-start(f32[16,352]{1,0:T(8,128)S(1)} %reduce_sum.9), channel_id=1, source_target_pairs={{0,1},{1,0},{2,3},{3,2},{4,5},{5,4},{6,7},{7,6},{8,9},{9,8},{10,11... | collective-permute-start | bytes 67592 | tf_op jit(solution)/shard_map/ppermute | solution.py:327
  119.5 17.1 %copy-start.6 = (bf16[2,3,2,64,352]{4,3,2,1,0:T(8,128)(2,1)}, bf16[2,3,2,64,352]{4,3,2,1,0:T(8,128)(2,1)S(1)}, u32[]{:S(2)}) copy-start(bf16[2,3,2,64,352]{4,3,2,1,0:T(8,128)(2,1)S(1)} %collective-permute-done.21.refs_1_) | copy-start | bytes 1622020
  136.7 0.7 copy-start.7
  137.3 4.9 %copy-start.5 = (f32[128,2240]{1,0:T(8,128)S(1)}, f32[128,2240]{1,0:T(8,128)}, u32[]{:S(2)}) copy-start(f32[128,2240]{1,0:T(8,128)} %get-tuple-element.20) | copy-start | bytes 3440644

commit v4 on v3

--- a/solution.py
+++ b/solution.py
@@ -17,7 +17,8 @@
     return -(-value // step) * step
 
 
-def pack_kernel(n, jb, blk, s_ref, x_ref, *outs):
+def pack_kernel(n, jb, blk, s_ref, x_ref, *refs):
+    outs, held = refs[:-1], refs[-1]
     b = s_ref[0]
     chans = x_ref.shape[1]
     for vg in range(2):
@@ -29,12 +30,9 @@
                 wide = x_ref[:, low:high].astype(F32)
                 if start != low:
                     wide = pltpu.roll(wide, high - low - (start - low), 1)
-                piece = wide[:, :blk].astype(BF16)
-                for k in range(n):
-
-                    @pl.when(lax.rem(b + k, n) == t)
-                    def _():
-                        outs[k][vg, jz, 0] = piece
+                held[lax.rem(t - b + n, n), vg, jz] = wide[:, :blk].astype(BF16)
+    for k in range(n):
+        outs[k][:, :, 0] = held[k]
 
 
 def place_rows(n, rl, b, xs, own, received):
@@ -215,9 +213,17 @@
             outs[k][vg, 0] = dh[k, vg]
 
 
-def unpack_kernel(n, jb, blk, chunks, s_ref, *refs):
+def unpack_kernel(n, jb, blk, chunks, sums, s_ref, *refs):
+    b = s_ref[0]
+    if sums:
+        (mine, theirs), refs = refs[:2], refs[2:]
+        taps, bias, held = refs[-3:]
+        refs = refs[:-3] + (held,)
+        for half in range(n):
+            part = jnp.where(b == half, mine[...], theirs[...])
+            taps[:, half * blk : (half + 1) * blk] = part[:9]
+            bias[half * blk : (half + 1) * blk] = part[9]
     ins, out, held = refs[:-2], refs[-2], refs[-1]
-    b = s_ref[0]
     for c, blocks in enumerate(chunks):
         for k in range(n):
             for at, kz in enumerate(blocks):
@@ -259,6 +265,7 @@
             grid=(rl,),
             in_specs=[pl.BlockSpec((cols, chans), lambda i, s: (i, 0))],
             out_specs=[pl.BlockSpec((2, jb, 1, cols, blk), lambda i, s: (0, 0, i, 0, 0))] * n,
+            scratch_shapes=[pltpu.VMEM((n, 2, jb, cols, blk), BF16)],
         ),
         out_shape=[jax.ShapeDtypeStruct(part_shape, BF16)] * n,
         name="pack",
@@ -354,7 +361,7 @@
         name="conv",
     )(scalars, packed[0], *hid_in, tap_all)
 
-    chunks = [range(jb - 1), range(jb - 1, jb)] if fast else [range(jb)]
+    chunks = CHUNKS if fast and jb == 4 else [range(jb)]
 
     def weights_of(blocks):
         if not fast:
@@ -390,8 +397,8 @@
         name="project",
     )(scalars, glu, *args)
     partial = [p.reshape(cotangent.shape) for p in partial]
+    others = [turn(partial[k], k) for k in range(1, n)]
     block_out = partial[0]
-    others = [turn(partial[k], k) for k in range(1, n)]
     for other in others:
         block_out = block_out + other.astype(F32)
     block_out = block_out.astype(BF16)
@@ -430,41 +437,46 @@
         )
         tap_grad = outs[n]
         d_parts += [outs[0]] + [turn(outs[k], k) for k in range(1, n)]
-    d_hidden = pl.pallas_call(
-        functools.partial(unpack_kernel, n, jb, blk, chunks),
-        grid_spec=pltpu.PrefetchScalarGridSpec(
-            num_scalar_prefetch=1,
-            grid=(rl,),
-            in_specs=[
-                pl.BlockSpec((2, p.shape[1], 1, cols, blk), lambda i, s: (0, 0, i, 0, 0)) for p in d_parts
-            ],
-            out_specs=pl.BlockSpec((cols, chans), lambda i, s: (i, 0)),
-            scratch_shapes=[pltpu.VMEM((n, 2, jb, cols, blk), BF16)],
-        ),
-        out_shape=jax.ShapeDtypeStruct((tokens, chans), BF16),
-        name="unpack",
-    )(scalars, *d_parts)
-
     tap_grad = tap_grad.reshape(2 * jb, 16, blk)
     if fast:
         pieces = lax.all_to_all(tap_grad, "fsdp", 0, 0, tiled=True)
         mine_sum = jnp.sum(pieces, axis=0)
-        theirs = turn(mine_sum, 1)
-        first = jnp.where(b == 0, mine_sum, theirs)
-        second = jnp.where(b == 0, theirs, mine_sum)
-        share = jnp.concatenate([first, second], axis=1)
+        sums = [mine_sum, turn(mine_sum, 1)]
     else:
+        sums = []
         spread = jnp.where(
             (jnp.arange(n) == b)[None, None, :, None], tap_grad.transpose(1, 0, 2)[:, :, None, :], 0.0
         ).reshape(16, chans)
         share = lax.psum(spread, "band")
         share = lax.psum_scatter(share, "fsdp", scatter_dimension=1, tiled=True)
+
+    whole = lambda shape: pl.BlockSpec(shape, lambda i, s: (0, 0))
+    row_specs = [pl.BlockSpec((2, p.shape[1], 1, cols, blk), lambda i, s: (0, 0, i, 0, 0)) for p in d_parts]
+    outs = pl.pallas_call(
+        functools.partial(unpack_kernel, n, jb, blk, chunks, len(sums)),
+        grid_spec=pltpu.PrefetchScalarGridSpec(
+            num_scalar_prefetch=1,
+            grid=(rl,),
+            in_specs=[whole((16, blk))] * len(sums) + row_specs,
+            out_specs=[pl.BlockSpec((cols, chans), lambda i, s: (i, 0))]
+            + ([whole((9, n * blk)), pl.BlockSpec((n * blk,), lambda i, s: (0,))] if sums else []),
+            scratch_shapes=[pltpu.VMEM((n, 2, jb, cols, blk), BF16)],
+        ),
+        out_shape=[jax.ShapeDtypeStruct((tokens, chans), BF16)]
+        + ([jax.ShapeDtypeStruct(shape, F32) for shape in ((9, n * blk), (n * blk,))] if sums else []),
+        name="unpack",
+    )(scalars, *sums, *d_parts)
+    d_hidden = outs[0]
+    d_taps, d_bias = (outs[1], outs[2]) if sums else (share[:9], share[9])
     return (
         block_out,
         d_hidden.reshape(hidden_in.shape),
-        share[:9],
-        share[9],
+        d_taps,
+        d_bias,
     )
+
+
+CHUNKS = [range(0, 2), range(2, 4)]
 
 
 def solution(mesh):

time: 144 us -> 146 us (1.014)
  blocking collectives: 0 us -> 11.8 us
  waiting for transfers between devices: 49.2 us -> 39.2 us
  starting transfers between devices: 45 us -> 48.5 us
  Pallas kernels: 40.1 us -> 38.6 us
    ppermute x6, waiting for transfers between devices: 33.5 us -> 2.09 us  [turn(): return lax.ppermute(x, 'band', [(i, (i + k) % n) for i in range(n)])]
    all_to_all x0 -> x1, blocking collectives: none -> 11.8 us  [unit(): pieces = lax.all_to_all(tap_grad, 'fsdp', 0, 0, tiled=True)]
    ppermute x3, waiting for transfers between devices: 9.92 us -> 21.6 us  [other_group(): return lax.ppermute(x, every, pairs)]
    ppermute x12, waiting for transfers between devices: 5.78 us -> 15.5 us  [across(): return lax.ppermute(x, ('fsdp', 'band'), pairs)]
    ppermute x12, starting transfers between devices: 22.1 us -> 29.2 us  [across(): return lax.ppermute(x, ('fsdp', 'band'), pairs)]
    all_to_all x1 -> x0, starting transfers between devices: 4.32 us -> none  [unit(): pieces = lax.all_to_all(tap_grad, 'fsdp', 0, 0, tiled=True)]
    pallas_call x1, Pallas kernels: 4.93 us -> 3.34 us  [unit(): pl.pallas_call(functools.partial(pack_kernel, n, jb, blk), grid_spec=pltp...]
    ppermute x6, starting transfers between devices: 6.34 us -> 7.84 us  [turn(): return lax.ppermute(x, 'band', [(i, (i + k) % n) for i in range(n)])]
  transfers between devices with their start and end apart: 25 -> 24, of which waited for: 5 -> 5; matrix products, arithmetic and copies ran while one was open for 2% -> 1% of each run, Pallas kernels for 28% -> 27%
where the time goes in v4:
time: 146 us
  starting transfers between devices  48.5 us (33%)
  waiting for transfers between devices  39.2 us (27%)
  Pallas kernels  38.6 us (26%)
  blocking collectives  11.8 us (8%)
  local copies, waits for them, and re-layouts  4.66 us (3%)
  other arithmetic  1.68 us (1%)
    ppermute x12, starting transfers between devices, across(): return lax.ppermute(x, ('fsdp', 'band'), pairs)  29.2 us
    ppermute x3, waiting for transfers between devices, other_group(): return lax.ppermute(x, every, pairs)  21.6 us
    pallas_call x2, Pallas kernels, unit(): pl.pallas_call(functools.partial(grad_kernel, n, jb, rl, blocks, moves, l...  18.4 us
    ppermute x12, waiting for transfers between devices, across(): return lax.ppermute(x, ('fsdp', 'band'), pairs)  15.5 us
    all_to_all x1, blocking collectives, unit(): pieces = lax.all_to_all(tap_grad, 'fsdp', 0, 0, tiled=True)  11.8 us
    ppermute x3, starting transfers between devices, other_group(): return lax.ppermute(x, every, pairs)  9.53 us
    ppermute x6, starting transfers between devices, turn(): return lax.ppermute(x, 'band', [(i, (i + k) % n) for i in range(n)])  7.84 us
    pallas_call x1, Pallas kernels, unit(): pl.pallas_call(functools.partial(out_kernel, n, moves, len(args)), in_spe...  7.27 us
  transfers between devices with their start and end apart: 24, of which 5 were waited for; matrix products, arithmetic and copies ran while one was open for 1% of the time, Pallas kernels for 27%

profile of v4, /device:TPU:0, one launch (start us, length us, event | category | flops | bytes accessed | tf_op | source)
XLA Modules:
  0.0 145.5 jit_solution(13912923323429049841)
XLA Ops:
  0.6 0.0 copy-start
  0.7 2.2 %constant_dynamic-slice_fusion = bf16[176,2240]{1,0:T(8,128)(2,1)} fusion(bf16[352,2240]{1,0:T(8,128)(2,1)} %param.8, s32[]{:T(128)S(6)} %select_n.38), kind=kLoop, calls=%fused_computation.12 | loop fusion | bytes 1576964 | tf_op jit(solution)/shard_map/dynamic_slice | solution.py:293
  2.9 6.0 %collective-permute-start.11 = (bf16[176,2240]{1,0:T(8,128)(2,1)}, bf16[176,2240]{1,0:T(8,128)(2,1)S(1)}, u32[]{:S(2)}, u32[]{:S(2)}) collective-permute-start(bf16[176,2240]{1,0:T(8,128)(2,1)} %constant_dynamic-slice_fusion), channel_id=1, source_target_pairs={{0,8},{3,11},{4,12},{7,15},{8,0},{11,3},{12,4},{15,7},{16,24},{19,... | collective-permute-start | bytes 2365448 | tf_op jit(solution)/shard_map/ppermute | solution.py:283
  8.8 0.1 collective-permute-start.6
  8.9 3.5 %collective-permute-start.7 = (bf16[176,2240]{1,0:T(8,128)(2,1)}, bf16[176,2240]{1,0:T(8,128)(2,1)}, u32[]{:S(2)}, u32[]{:S(2)}) collective-permute-start(bf16[176,2240]{1,0:T(8,128)(2,1)} %constant_dynamic-slice_fusion), channel_id=1, source_target_pairs={{0,4},{3,7},{4,0},{7,3},{8,12},{11,15},{12,8},{15,11},{16,20},{19,... | collective-permute-start | bytes 2365448 | tf_op jit(solution)/shard_map/ppermute | solution.py:283
  12.5 0.1 pad.4.clone
  12.5 15.5 %collective-permute-done.11.refs_6_ = bf16[176,2240]{1,0:T(8,128)(2,1)S(1)} collective-permute-done((bf16[176,2240]{1,0:T(8,128)(2,1)}, bf16[176,2240]{1,0:T(8,128)(2,1)S(1)}, u32[]{:S(2)}, u32[]{:S(2)}) %collective-permute-start.11) | collective-permute-done | bytes 788512 | tf_op jit(solution)/shard_map/ppermute | solution.py:283
  28.1 2.9 %collective-permute-start.15 = (bf16[176,2240]{1,0:T(8,128)(2,1)S(1)}, bf16[176,2240]{1,0:T(8,128)(2,1)}, u32[]{:S(2)}, u32[]{:S(2)}) collective-permute-start(bf16[176,2240]{1,0:T(8,128)(2,1)S(1)} %collective-permute-done.11.refs_6_), channel_id=1, source_target_pairs={{0,4},{3,7},{4,0},{7,3},{8,12},{11,15},{12,8},{15,11},{16,20},{19,... | collective-permute-start | bytes 2365448 | tf_op jit(solution)/shard_map/ppermute | solution.py:283
  31.0 0.1 constant_dynamic-update-slice_fusion.4
  31.1 0.1 collective-permute-start.1
  31.2 0.6 stack.32.s_ref
  31.8 3.3 %pack.1 = (bf16[2,4,2,64,352]{4,3,2,1,0:T(8,128)(2,1)}, bf16[2,4,2,64,352]{4,3,2,1,0:T(8,128)(2,1)}) custom-call(s32[5]{0:T(128)} %stack.32.s_ref, bf16[128,5632]{1,0:T(8,128)(2,1)} %bitcast.22), custom_call_target="tpu_custom_call" | custom-call | tf_op jit(solution)/shard_map/pack/pallas_call | solution.py:261
  35.2 0.2 collective-permute-start
  35.3 0.0 collective-permute-done.1
  35.3 0.7 collective-permute-start.2
  36.0 0.0 collective-permute-done.2
  36.0 0.7 collective-permute-start.3
  36.7 0.0 collective-permute-done.3
  36.7 0.7 collective-permute-start.4
  37.4 0.0 collective-permute-done.4
  37.4 16.0 %collective-permute-start.5 = (bf16[8,16,352]{2,1,0:T(8,128)(2,1)S(1)}, bf16[8,16,352]{2,1,0:T(8,128)(2,1)S(1)}, u32[]{:S(2)}, u32[]{:S(2)}) collective-permute-start(bf16[8,16,352]{2,1,0:T(8,128)(2,1)S(1)} %constant_dynamic-update-slice_fusion), channel_id=1, source_target_pairs={{0,2},{1,3},{2,0},{3,1},{4,6},{5,7},{6,4},{7,5},{8,10},{9,11},{10,... | collective-permute-start | bytes 270344 | tf_op jit(solution)/shard_map/ppermute | solution.py:283
  53.4 0.0 collective-permute-done.7.refs_2_.refs_8_
  53.4 3.7 %collective-permute-start.8 = (bf16[176,2240]{1,0:T(8,128)(2,1)}, bf16[176,2240]{1,0:T(8,128)(2,1)}, u32[]{:S(2)}, u32[]{:S(2)}) collective-permute-start(bf16[176,2240]{1,0:T(8,128)(2,1)} %collective-permute-done.7.refs_2_.refs_8_), channel_id=1, source_target_pairs={{0,16},{3,19},{4,20},{7,23},{8,24},{11,27},{12,28},{15,31},{16,0},... | collective-permute-start | bytes 2365448 | tf_op jit(solution)/shard_map/ppermute | solution.py:291
  57.1 0.0 collective-permute-done.5
  57.1 0.1 collective-permute-start.9
  57.2 0.0 collective-permute-done.refs_0_
  57.2 2.2 %collective-permute-start.12 = (bf16[176,2240]{1,0:T(8,128)(2,1)S(1)}, bf16[176,2240]{1,0:T(8,128)(2,1)}, u32[]{:S(2)}, u32[]{:S(2)}) collective-permute-start(bf16[176,2240]{1,0:T(8,128)(2,1)S(1)} %collective-permute-done.11.refs_6_), channel_id=1, source_target_pairs={{0,16},{3,19},{4,20},{7,23},{8,24},{11,27},{12,28},{15,31},{16,0},... | collective-permute-start | bytes 2365448 | tf_op jit(solution)/shard_map/ppermute | solution.py:291
  59.4 0.0 collective-permute-done.15.refs_10_
  59.4 3.7 %collective-permute-start.16 = (bf16[176,2240]{1,0:T(8,128)(2,1)}, bf16[176,2240]{1,0:T(8,128)(2,1)}, u32[]{:S(2)}, u32[]{:S(2)}) collective-permute-start(bf16[176,2240]{1,0:T(8,128)(2,1)} %collective-permute-done.15.refs_10_), channel_id=1, source_target_pairs={{0,16},{3,19},{4,20},{7,23},{8,24},{11,27},{12,28},{15,31},{16,0},... | collective-permute-start | bytes 2365448 | tf_op jit(solution)/shard_map/ppermute | solution.py:291
  63.1 0.0 collective-permute-done.6
  63.1 0.1 collective-permute-start.13
  63.2 4.7 %collective-permute-done.8.refs_3_.refs_9_ = bf16[176,2240]{1,0:T(8,128)(2,1)} collective-permute-done((bf16[176,2240]{1,0:T(8,128)(2,1)}, bf16[176,2240]{1,0:T(8,128)(2,1)}, u32[]{:S(2)}, u32[]{:S(2)}) %collective-permute-start.8) | collective-permute-done | bytes 788512 | tf_op jit(solution)/shard_map/ppermute | solution.py:291
  67.9 0.0 collective-permute-start.17
  67.9 0.0 collective-permute-done.9.refs_4_.refs_10_
  67.9 0.5 collective-permute-start.10
  68.4 8.2 %collective-permute-done.12.refs_7_ = bf16[176,2240]{1,0:T(8,128)(2,1)} collective-permute-done((bf16[176,2240]{1,0:T(8,128)(2,1)S(1)}, bf16[176,2240]{1,0:T(8,128)(2,1)}, u32[]{:S(2)}, u32[]{:S(2)}) %collective-permute-start.12) | collective-permute-done | bytes 788512 | tf_op jit(solution)/shard_map/ppermute | solution.py:291
  76.6 0.0 collective-permute-start.14
  76.6 8.7 %collective-permute-done.16.refs_11_ = bf16[176,2240]{1,0:T(8,128)(2,1)} collective-permute-done((bf16[176,2240]{1,0:T(8,128)(2,1)}, bf16[176,2240]{1,0:T(8,128)(2,1)}, u32[]{:S(2)}, u32[]{:S(2)}) %collective-permute-start.16) | collective-permute-done | bytes 788512 | tf_op jit(solution)/shard_map/ppermute | solution.py:291
  85.3 0.0 collective-permute-start.18
  85.3 0.0 collective-permute-done.13.refs_8_
  85.3 3.7 %collective-permute-start.20 = (bf16[1,2,64,2240]{3,2,1,0:T(8,128)(2,1)}, bf16[1,2,64,2240]{3,2,1,0:T(8,128)(2,1)}, u32[]{:S(2)}, u32[]{:S(2)}) collective-permute-start(bf16[1,2,64,2240]{3,2,1,0:T(8,128)(2,1)} %param.9), channel_id=1, source_target_pairs={{0,1},{1,0},{2,3},{3,2},{4,5},{5,4},{6,7},{7,6},{8,9},{9,8},{10,11... | collective-permute-start | bytes 1720328 | tf_op jit(solution)/shard_map/ppermute | solution.py:334
  89.0 0.6 broadcast_select_fusion.refs_1_
  89.7 6.1 %conv.1 = (bf16[4,2,128,352]{3,2,1,0:T(8,128)(2,1)}, f32[4,2,128,352]{3,2,1,0:T(8,128)}, f32[4,2,128,352]{3,2,1,0:T(8,128)}) custom-call(s32[5]{0:T(128)} %stack.32.s_ref, bf16[2,4,2,64,352]{4,3,2,1,0:T(8,128)(2,1)} %get-tuple-element.20.own, bf16[2,4,2,64,352]{4,3,2,1,0:T(8,128)(2,1)} %copy-done.1, bf16[8,16,352]{2,1,0:T(8,128)(2,1)} %broadcast_select_fusion.refs_1_), custom_call_target="tpu_custom_call" | custom-call | tf_op jit(solution)/shard_map/conv/pallas_call | solution.py:344
  95.8 0.0 collective-permute-done.10.refs_5_.refs_11_
  95.8 0.0 collective-permute-done.14.refs_9_
  95.8 0.0 collective-permute-done.17.refs_12_
  95.8 0.0 collective-permute-done.18.refs_13_
  95.8 0.9 copy-done.5
  96.8 7.3 %project.1 = (f32[128,2240]{1,0:T(8,128)}, bf16[128,2240]{1,0:T(8,128)(2,1)}) custom-call(s32[5]{0:T(128)} %stack.32.s_ref, bf16[4,2,128,352]{3,2,1,0:T(8,128)(2,1)} %get-tuple-element.22.glu, bf16[2,176,2240]{2,1,0:T(8,128)(2,1)} %bitcast.18, bf16[2,176,2240]{2,1,0:T(8,128)(2,1)} %bitcast.9.refs_1_.refs_7_, ...), custom_call_target="tpu_custom_call" | custom-call | tf_op jit(solution)/shard_map/project/pallas_call | solution.py:387
  104.0 0.2 collective-permute-start.19
  104.3 9.2 %shard_map.84 = (bf16[2,2,2,64,352]{4,3,2,1,0:T(8,128)(2,1)}, bf16[2,2,2,64,352]{4,3,2,1,0:T(8,128)(2,1)}, f32[2,4,16,352]{3,2,1,0:T(8,128)}) custom-call(s32[5]{0:T(128)} %stack.32.s_ref, bf16[2,4,2,64,352]{4,3,2,1,0:T(8,128)(2,1)} %get-tuple-element.20.own, bf16[2,4,2,64,352]{4,3,2,1,0:T(8,128)(2,1)} %copy-done.1, ...), custom_call_target="tpu_custom_call" | custom-call | tf_op jit(solution)/shard_map/pallas_call | solution.py:413
  113.4 1.7 %collective-permute-start.22 = (bf16[2,2,2,64,352]{4,3,2,1,0:T(8,128)(2,1)}, bf16[2,2,2,64,352]{4,3,2,1,0:T(8,128)(2,1)S(1)}, u32[]{:S(2)}, u32[]{:S(2)}) collective-permute-start(bf16[2,2,2,64,352]{4,3,2,1,0:T(8,128)(2,1)} %get-tuple-element.30), channel_id=1, source_target_pairs={{0,1},{1,0},{2,3},{3,2},{4,5},{5,4},{6,7},{7,6},{8,9},{9,8},{10,11... | collective-permute-start | bytes 1081352 | tf_op jit(solution)/shard_map/ppermute | solution.py:334
  115.2 9.2 %shard_map.85 = (bf16[2,2,2,64,352]{4,3,2,1,0:T(8,128)(2,1)}, bf16[2,2,2,64,352]{4,3,2,1,0:T(8,128)(2,1)}, f32[2,4,16,352]{3,2,1,0:T(8,128)}) custom-call(s32[5]{0:T(128)} %stack.32.s_ref, bf16[2,4,2,64,352]{4,3,2,1,0:T(8,128)(2,1)} %get-tuple-element.20.own, bf16[2,4,2,64,352]{4,3,2,1,0:T(8,128)(2,1)} %copy-done.1, ...), custom_call_target="tpu_custom_call", output_to_operand_aliasing={{2}: (16, {})} | custom-call | tf_op jit(solution)/shard_map/pallas_call | solution.py:413
  124.4 0.2 collective-permute-start.23
  124.6 11.8 %all_to_all.5 = f32[8,16,352]{2,1,0:T(8,128)S(1)} all-to-all(f32[8,16,352]{2,1,0:T(8,128)} %bitcast.24), channel_id=1, replica_groups=mesh['groups'=2,'fsdp'=8,'band'=2] {'fsdp'}, dimensions={0} | all-to-all | bytes 360448 | tf_op jit(solution)/shard_map/all_to_all | solution.py:442
  136.4 1.8 %collective-permute-start.21 = (f32[16,352]{1,0:T(8,128)S(1)}, f32[16,352]{1,0:T(8,128)S(1)}, u32[]{:S(2)}, u32[]{:S(2)}) collective-permute-start(f32[16,352]{1,0:T(8,128)S(1)} %reduce_sum.9.refs_0_), channel_id=1, source_target_pairs={{0,1},{1,0},{2,3},{3,2},{4,5},{5,4},{6,7},{7,6},{8,9},{9,8},{10,11... | collective-permute-start | bytes 67592 | tf_op jit(solution)/shard_map/ppermute | solution.py:334
  138.2 0.0 collective-permute-done.22.refs_3_
  138.2 2.1 %collective-permute-done.21.refs_1_ = f32[16,352]{1,0:T(8,128)S(1)} collective-permute-done((f32[16,352]{1,0:T(8,128)S(1)}, f32[16,352]{1,0:T(8,128)S(1)}, u32[]{:S(2)}, u32[]{:S(2)}) %collective-permute-start.21) | collective-permute-done | bytes 22560 | tf_op jit(solution)/shard_map/ppermute | solution.py:334
  140.3 0.0 collective-permute-done.23.refs_5_
  140.3 0.6 copy-done.11
  140.9 0.2 copy-done.8
  141.1 3.5 %unpack.1 = (bf16[128,5632]{1,0:T(8,128)(2,1)}, f32[9,704]{1,0:T(8,128)}, f32[704]{0:T(1024)}) custom-call(s32[5]{0:T(128)} %stack.32.s_ref, f32[16,352]{1,0:T(8,128)} %copy-done.9, f32[16,352]{1,0:T(8,128)} %copy-done.11, bf16[2,2,2,64,352]{4,3,2,1,0:T(8,128)(2,1)} %get-tuple-element.29.refs_2_, bf16[2,2,2,64,352]{4,3,2,1,0:T(8,128)(2,1)} %copy-done.7, ...), custom_call_target="tpu_custom_call" | custom-call | tf_op jit(solution)/shard_map/unpack/pallas_call | solution.py:455
  144.6 0.0 collective-permute-done.19
  144.6 0.9 add_convert_fusion
  (31 shorter events, 0.1 us)
Async XLA Ops:
  0.6 8.2 %copy-start = (bf16[352,2240]{1,0:T(8,128)(2,1)S(1)}, bf16[352,2240]{1,0:T(8,128)(2,1)}, u32[]{:S(2)}) copy-start(bf16[352,2240]{1,0:T(8,128)(2,1)} %param.8) | copy-start | bytes 4730884
  0.6 11.8 %copy-start.12 = (bf16[704]{0:T(1024)(128)(2,1)S(1)}, bf16[704]{0:T(1024)(128)(2,1)}, u32[]{:S(2)}) copy-start(bf16[704]{0:T(1024)(128)(2,1)} %param.7) | copy-start | bytes 4228
  0.7 30.4 %copy-start.10 = (bf16[9,704]{1,0:T(8,128)(2,1)S(1)}, bf16[9,704]{1,0:T(8,128)(2,1)}, u32[]{:S(2)}) copy-start(bf16[9,704]{1,0:T(8,128)(2,1)} %param.6) | copy-start | bytes 38020
  2.9 25.2 %collective-permute-start.11 = (bf16[176,2240]{1,0:T(8,128)(2,1)}, bf16[176,2240]{1,0:T(8,128)(2,1)S(1)}, u32[]{:S(2)}, u32[]{:S(2)}) collective-permute-start(bf16[176,2240]{1,0:T(8,128)(2,1)} %constant_dynamic-slice_fusion), channel_id=1, source_target_pairs={{0,8},{3,11},{4,12},{7,15},{8,0},{11,3},{12,4},{15,7},{16,24},{19,... | collective-permute-start | bytes 2365448 | tf_op jit(solution)/shard_map/ppermute | solution.py:283
  8.8 54.2 %collective-permute-start.6 = (bf16[352,2240]{1,0:T(8,128)(2,1)S(1)}, bf16[352,2240]{1,0:T(8,128)(2,1)}, u32[]{:S(2)}, u32[]{:S(2)}) collective-permute-start(bf16[352,2240]{1,0:T(8,128)(2,1)S(1)} %copy-done), channel_id=1, source_target_pairs={{0,2},{1,3},{2,0},{3,1},{4,6},{5,7},{6,4},{7,5},{8,10},{9,11},{10,... | collective-permute-start | bytes 4730888 | tf_op jit(solution)/shard_map/ppermute | solution.py:283
  8.9 44.5 %collective-permute-start.7 = (bf16[176,2240]{1,0:T(8,128)(2,1)}, bf16[176,2240]{1,0:T(8,128)(2,1)}, u32[]{:S(2)}, u32[]{:S(2)}) collective-permute-start(bf16[176,2240]{1,0:T(8,128)(2,1)} %constant_dynamic-slice_fusion), channel_id=1, source_target_pairs={{0,4},{3,7},{4,0},{7,3},{8,12},{11,15},{12,8},{15,11},{16,20},{19,... | collective-permute-start | bytes 2365448 | tf_op jit(solution)/shard_map/ppermute | solution.py:283
  28.1 67.7 %copy-start.2 = (bf16[176,2240]{1,0:T(8,128)(2,1)}, bf16[176,2240]{1,0:T(8,128)(2,1)S(1)}, u32[]{:S(2)}) copy-start(bf16[176,2240]{1,0:T(8,128)(2,1)S(1)} %collective-permute-done.11.refs_6_) | copy-start | bytes 2365444
  28.1 31.3 %collective-permute-start.15 = (bf16[176,2240]{1,0:T(8,128)(2,1)S(1)}, bf16[176,2240]{1,0:T(8,128)(2,1)}, u32[]{:S(2)}, u32[]{:S(2)}) collective-permute-start(bf16[176,2240]{1,0:T(8,128)(2,1)S(1)} %collective-permute-done.11.refs_6_), channel_id=1, source_target_pairs={{0,4},{3,7},{4,0},{7,3},{8,12},{11,15},{12,8},{15,11},{16,20},{19,... | collective-permute-start | bytes 2365448 | tf_op jit(solution)/shard_map/ppermute | solution.py:283
  31.1 4.2 %collective-permute-start.1 = (bf16[16,352]{1,0:T(8,128)(2,1)S(1)}, bf16[16,352]{1,0:T(8,128)(2,1)S(1)}, u32[]{:S(2)}, u32[]{:S(2)}) collective-permute-start(bf16[16,352]{1,0:T(8,128)(2,1)S(1)} %get-tuple-element.37), channel_id=1, source_target_pairs={{0,2},{1,3},{2,0},{3,1},{4,6},{5,7},{6,4},{7,5},{8,10},{9,11},{10,... | collective-permute-start | bytes 33800 | tf_op jit(solution)/shard_map/ppermute | solution.py:283
  35.2 22.0 %collective-permute-start = (bf16[2,4,2,64,352]{4,3,2,1,0:T(8,128)(2,1)}, bf16[2,4,2,64,352]{4,3,2,1,0:T(8,128)(2,1)S(1)}, u32[]{:S(2)}, u32[]{:S(2)}) collective-permute-start(bf16[2,4,2,64,352]{4,3,2,1,0:T(8,128)(2,1)} %get-tuple-element.21), channel_id=1, source_target_pairs={{0,1},{1,0},{2,3},{3,2},{4,5},{5,4},{6,7},{7,6},{8,9},{9,8},{10,11... | collective-permute-start | bytes 2162696 | tf_op jit(solution)/shard_map/ppermute | solution.py:334
  35.3 0.7 collective-permute-start.2
  36.0 0.7 collective-permute-start.3
  36.7 0.7 collective-permute-start.4
  37.4 19.7 %collective-permute-start.5 = (bf16[8,16,352]{2,1,0:T(8,128)(2,1)S(1)}, bf16[8,16,352]{2,1,0:T(8,128)(2,1)S(1)}, u32[]{:S(2)}, u32[]{:S(2)}) collective-permute-start(bf16[8,16,352]{2,1,0:T(8,128)(2,1)S(1)} %constant_dynamic-update-slice_fusion), channel_id=1, source_target_pairs={{0,2},{1,3},{2,0},{3,1},{4,6},{5,7},{6,4},{7,5},{8,10},{9,11},{10,... | collective-permute-start | bytes 270344 | tf_op jit(solution)/shard_map/ppermute | solution.py:283
  53.4 14.5 %collective-permute-start.8 = (bf16[176,2240]{1,0:T(8,128)(2,1)}, bf16[176,2240]{1,0:T(8,128)(2,1)}, u32[]{:S(2)}, u32[]{:S(2)}) collective-permute-start(bf16[176,2240]{1,0:T(8,128)(2,1)} %collective-permute-done.7.refs_2_.refs_8_), channel_id=1, source_target_pairs={{0,16},{3,19},{4,20},{7,23},{8,24},{11,27},{12,28},{15,31},{16,0},... | collective-permute-start | bytes 2365448 | tf_op jit(solution)/shard_map/ppermute | solution.py:291
  57.1 10.8 %collective-permute-start.9 = (bf16[176,2240]{1,0:T(8,128)(2,1)}, bf16[176,2240]{1,0:T(8,128)(2,1)S(1)}, u32[]{:S(2)}, u32[]{:S(2)}) collective-permute-start(bf16[176,2240]{1,0:T(8,128)(2,1)} %collective-permute-done.7.refs_2_.refs_8_), channel_id=1, source_target_pairs={{0,2},{1,3},{2,0},{3,1},{4,6},{5,7},{6,4},{7,5},{8,10},{9,11},{10,... | collective-permute-start | bytes 2365448 | tf_op jit(solution)/shard_map/ppermute | solution.py:283
  57.2 32.4 %copy-start.1 = (bf16[2,4,2,64,352]{4,3,2,1,0:T(8,128)(2,1)}, bf16[2,4,2,64,352]{4,3,2,1,0:T(8,128)(2,1)S(1)}, u32[]{:S(2)}) copy-start(bf16[2,4,2,64,352]{4,3,2,1,0:T(8,128)(2,1)S(1)} %collective-permute-done.refs_0_) | copy-start | bytes 2162692
  57.2 19.3 %collective-permute-start.12 = (bf16[176,2240]{1,0:T(8,128)(2,1)S(1)}, bf16[176,2240]{1,0:T(8,128)(2,1)}, u32[]{:S(2)}, u32[]{:S(2)}) collective-permute-start(bf16[176,2240]{1,0:T(8,128)(2,1)S(1)} %collective-permute-done.11.refs_6_), channel_id=1, source_target_pairs={{0,16},{3,19},{4,20},{7,23},{8,24},{11,27},{12,28},{15,31},{16,0},... | collective-permute-start | bytes 2365448 | tf_op jit(solution)/shard_map/ppermute | solution.py:291
  59.4 25.9 %collective-permute-start.16 = (bf16[176,2240]{1,0:T(8,128)(2,1)}, bf16[176,2240]{1,0:T(8,128)(2,1)}, u32[]{:S(2)}, u32[]{:S(2)}) collective-permute-start(bf16[176,2240]{1,0:T(8,128)(2,1)} %collective-permute-done.15.refs_10_), channel_id=1, source_target_pairs={{0,16},{3,19},{4,20},{7,23},{8,24},{11,27},{12,28},{15,31},{16,0},... | collective-permute-start | bytes 2365448 | tf_op jit(solution)/shard_map/ppermute | solution.py:291
  63.1 22.2 %collective-permute-start.13 = (bf16[176,2240]{1,0:T(8,128)(2,1)S(1)}, bf16[176,2240]{1,0:T(8,128)(2,1)S(1)}, u32[]{:S(2)}, u32[]{:S(2)}) collective-permute-start(bf16[176,2240]{1,0:T(8,128)(2,1)S(1)} %collective-permute-done.11.refs_6_), channel_id=1, source_target_pairs={{0,2},{1,3},{2,0},{3,1},{4,6},{5,7},{6,4},{7,5},{8,10},{9,11},{10,... | collective-permute-start | bytes 2365448 | tf_op jit(solution)/shard_map/ppermute | solution.py:283
  67.9 27.9 %collective-permute-start.17 = (bf16[176,2240]{1,0:T(8,128)(2,1)}, bf16[176,2240]{1,0:T(8,128)(2,1)S(1)}, u32[]{:S(2)}, u32[]{:S(2)}) collective-permute-start(bf16[176,2240]{1,0:T(8,128)(2,1)} %collective-permute-done.15.refs_10_), channel_id=1, source_target_pairs={{0,2},{1,3},{2,0},{3,1},{4,6},{5,7},{6,4},{7,5},{8,10},{9,11},{10,... | collective-permute-start | bytes 2365448 | tf_op jit(solution)/shard_map/ppermute | solution.py:283
  67.9 17.4 %copy-start.3 = (bf16[176,2240]{1,0:T(8,128)(2,1)}, bf16[176,2240]{1,0:T(8,128)(2,1)S(1)}, u32[]{:S(2)}) copy-start(bf16[176,2240]{1,0:T(8,128)(2,1)S(1)} %collective-permute-done.9.refs_4_.refs_10_) | copy-start | bytes 2365444
  67.9 27.9 %collective-permute-start.10 = (bf16[176,2240]{1,0:T(8,128)(2,1)}, bf16[176,2240]{1,0:T(8,128)(2,1)}, u32[]{:S(2)}, u32[]{:S(2)}) collective-permute-start(bf16[176,2240]{1,0:T(8,128)(2,1)} %collective-permute-done.8.refs_3_.refs_9_), channel_id=1, source_target_pairs={{0,2},{1,3},{2,0},{3,1},{4,6},{5,7},{6,4},{7,5},{8,10},{9,11},{10,... | collective-permute-start | bytes 2365448 | tf_op jit(solution)/shard_map/ppermute | solution.py:283
  76.6 19.2 %collective-permute-start.14 = (bf16[176,2240]{1,0:T(8,128)(2,1)}, bf16[176,2240]{1,0:T(8,128)(2,1)}, u32[]{:S(2)}, u32[]{:S(2)}) collective-permute-start(bf16[176,2240]{1,0:T(8,128)(2,1)} %collective-permute-done.12.refs_7_), channel_id=1, source_target_pairs={{0,2},{1,3},{2,0},{3,1},{4,6},{5,7},{6,4},{7,5},{8,10},{9,11},{10,... | collective-permute-start | bytes 2365448 | tf_op jit(solution)/shard_map/ppermute | solution.py:283
  85.3 10.6 %collective-permute-start.18 = (bf16[176,2240]{1,0:T(8,128)(2,1)}, bf16[176,2240]{1,0:T(8,128)(2,1)}, u32[]{:S(2)}, u32[]{:S(2)}) collective-permute-start(bf16[176,2240]{1,0:T(8,128)(2,1)} %collective-permute-done.16.refs_11_), channel_id=1, source_target_pairs={{0,2},{1,3},{2,0},{3,1},{4,6},{5,7},{6,4},{7,5},{8,10},{9,11},{10,... | collective-permute-start | bytes 2365448 | tf_op jit(solution)/shard_map/ppermute | solution.py:283
  85.3 10.6 %copy-start.4 = (bf16[176,2240]{1,0:T(8,128)(2,1)}, bf16[176,2240]{1,0:T(8,128)(2,1)S(1)}, u32[]{:S(2)}) copy-start(bf16[176,2240]{1,0:T(8,128)(2,1)S(1)} %collective-permute-done.13.refs_8_) | copy-start | bytes 2365444
  85.3 19.0 %collective-permute-start.20 = (bf16[1,2,64,2240]{3,2,1,0:T(8,128)(2,1)}, bf16[1,2,64,2240]{3,2,1,0:T(8,128)(2,1)}, u32[]{:S(2)}, u32[]{:S(2)}) collective-permute-start(bf16[1,2,64,2240]{3,2,1,0:T(8,128)(2,1)} %param.9), channel_id=1, source_target_pairs={{0,1},{1,0},{2,3},{3,2},{4,5},{5,4},{6,7},{7,6},{8,9},{9,8},{10,11... | collective-permute-start | bytes 1720328 | tf_op jit(solution)/shard_map/ppermute | solution.py:334
  95.8 0.9 copy-start.5
  104.0 40.5 %collective-permute-start.19 = (bf16[1,2,64,2240]{3,2,1,0:T(8,128)(2,1)}, bf16[1,2,64,2240]{3,2,1,0:T(8,128)(2,1)S(1)}, u32[]{:S(2)}, u32[]{:S(2)}) collective-permute-start(bf16[1,2,64,2240]{3,2,1,0:T(8,128)(2,1)} %bitcast.28), channel_id=1, source_target_pairs={{0,1},{1,0},{2,3},{3,2},{4,5},{5,4},{6,7},{7,6},{8,9},{9,8},{10,11... | collective-permute-start | bytes 1720328 | tf_op jit(solution)/shard_map/ppermute | solution.py:334
  113.4 24.8 %collective-permute-start.22 = (bf16[2,2,2,64,352]{4,3,2,1,0:T(8,128)(2,1)}, bf16[2,2,2,64,352]{4,3,2,1,0:T(8,128)(2,1)S(1)}, u32[]{:S(2)}, u32[]{:S(2)}) collective-permute-start(bf16[2,2,2,64,352]{4,3,2,1,0:T(8,128)(2,1)} %get-tuple-element.30), channel_id=1, source_target_pairs={{0,1},{1,0},{2,3},{3,2},{4,5},{5,4},{6,7},{7,6},{8,9},{9,8},{10,11... | collective-permute-start | bytes 1081352 | tf_op jit(solution)/shard_map/ppermute | solution.py:334
  124.3 20.2 %copy-start.6 = (f32[128,2240]{1,0:T(8,128)S(1)}, f32[128,2240]{1,0:T(8,128)}, u32[]{:S(2)}) copy-start(f32[128,2240]{1,0:T(8,128)} %get-tuple-element.23) | copy-start | bytes 3440644
  124.4 15.9 %collective-permute-start.23 = (bf16[2,2,2,64,352]{4,3,2,1,0:T(8,128)(2,1)}, bf16[2,2,2,64,352]{4,3,2,1,0:T(8,128)(2,1)S(1)}, u32[]{:S(2)}, u32[]{:S(2)}) collective-permute-start(bf16[2,2,2,64,352]{4,3,2,1,0:T(8,128)(2,1)} %get-tuple-element.32), channel_id=1, source_target_pairs={{0,1},{1,0},{2,3},{3,2},{4,5},{5,4},{6,7},{7,6},{8,9},{9,8},{10,11... | collective-permute-start | bytes 1081352 | tf_op jit(solution)/shard_map/ppermute | solution.py:334
  136.4 3.9 %copy-start.9 = (f32[16,352]{1,0:T(8,128)}, f32[16,352]{1,0:T(8,128)S(1)}, u32[]{:S(2)}) copy-start(f32[16,352]{1,0:T(8,128)S(1)} %reduce_sum.9.refs_0_) | copy-start | bytes 67588
  136.4 3.9 %collective-permute-start.21 = (f32[16,352]{1,0:T(8,128)S(1)}, f32[16,352]{1,0:T(8,128)S(1)}, u32[]{:S(2)}, u32[]{:S(2)}) collective-permute-start(f32[16,352]{1,0:T(8,128)S(1)} %reduce_sum.9.refs_0_), channel_id=1, source_target_pairs={{0,1},{1,0},{2,3},{3,2},{4,5},{5,4},{6,7},{7,6},{8,9},{9,8},{10,11... | collective-permute-start | bytes 67592 | tf_op jit(solution)/shard_map/ppermute | solution.py:334
  138.2 2.1 %copy-start.7 = (bf16[2,2,2,64,352]{4,3,2,1,0:T(8,128)(2,1)}, bf16[2,2,2,64,352]{4,3,2,1,0:T(8,128)(2,1)S(1)}, u32[]{:S(2)}) copy-start(bf16[2,2,2,64,352]{4,3,2,1,0:T(8,128)(2,1)S(1)} %collective-permute-done.22.refs_3_) | copy-start | bytes 1081348
  140.3 0.6 copy-start.11
  140.3 0.8 copy-start.8

commit v5 on v4

--- a/solution.py
+++ b/solution.py
@@ -114,18 +114,22 @@
 
 
 def out_kernel(n, copies, n_w, s_ref, glu, *refs):
-    w_refs, outs, (acc, w_buf, sems) = refs[:n_w], refs[n_w:-3], refs[-3:]
+    w_refs, outs, (acc, pair, w_buf, sems) = refs[:n_w], refs[n_w:-4], refs[-4:]
     for k, copy in enumerate(copies):
         move_weights("start", s_ref, copy, k, w_refs, w_buf, sems)
     tokens, blk = glu.shape[2:]
-    for k, copy in enumerate(copies):
-        move_weights("wait", s_ref, copy, k, w_refs, w_buf, sems)
+    width = pair.shape[1] // blk
+    for low in range(0, len(copies), width):
+        for at in range(width):
+            pair[:, at * blk : (at + 1) * blk] = glu[s_ref[3] ^ (low + at)].reshape(n * tokens, blk)
+        for at in range(width):
+            move_weights("wait", s_ref, copies[low + at], low + at, w_refs, w_buf, sems)
         part = jnp.dot(
-            glu[s_ref[3] ^ k].reshape(n * tokens, blk),
-            w_buf[k].reshape(blk, w_buf.shape[3]),
+            pair[...],
+            w_buf[low : low + width].reshape(width * blk, w_buf.shape[3]),
             preferred_element_type=F32,
         )
-        if k == 0:
+        if low == 0:
             acc[...] = part
         else:
             acc[...] += part
@@ -153,8 +157,9 @@
 
     @pl.when(step == 0)
     def _():
+        move_weights("start", s_ref, copies[0], 0, w_refs, w_buf, sems)
         move_cots("start")
-        for at in range(len(copies)):
+        for at in range(1, len(copies)):
             move_weights("start", s_ref, copies[at], at, w_refs, w_buf, sems)
 
     place_rows(n, rl, b, xs, own, received)
@@ -391,6 +396,7 @@
         out_shape=[jax.ShapeDtypeStruct((tokens, feats), F32 if k == 0 else BF16) for k in range(n)],
         scratch_shapes=[
             pltpu.VMEM((n * tokens, feats), F32),
+            pltpu.VMEM((n * tokens, 2 * blk if fast else blk), BF16),
             pltpu.VMEM((jb, parts, blk // parts, feats), BF16),
             pltpu.SemaphoreType.DMA((jb,)),
         ],

time: 146 us -> 145 us (level)
  transfers between devices with their start and end apart: 24 -> 24, of which waited for: 5 -> 5; matrix products, arithmetic and copies ran while one was open for 1% -> 1% of each run, Pallas kernels for 27% -> 26%
where the time goes in v5:
time: 145 us; the launch traced here: 144 us
  starting transfers between devices  48.7 us (34%)
  waiting for transfers between devices  39.3 us (27%)
  Pallas kernels  37.5 us (26%)
  blocking collectives  11.7 us (8%)
  local copies, waits for them, and re-layouts  4.66 us (3%)
  other arithmetic  1.68 us (1%)
    ppermute x12, starting transfers between devices, across(): return lax.ppermute(x, ('fsdp', 'band'), pairs)  29.2 us
    ppermute x3, waiting for transfers between devices, other_group(): return lax.ppermute(x, every, pairs)  21.6 us
    pallas_call x2, Pallas kernels, unit(): pl.pallas_call(functools.partial(grad_kernel, n, jb, rl, blocks, moves, l...  17.9 us
    ppermute x12, waiting for transfers between devices, across(): return lax.ppermute(x, ('fsdp', 'band'), pairs)  15.5 us
    all_to_all x1, blocking collectives, unit(): pieces = lax.all_to_all(tap_grad, 'fsdp', 0, 0, tiled=True)  11.7 us
    ppermute x3, starting transfers between devices, other_group(): return lax.ppermute(x, every, pairs)  9.53 us
    ppermute x6, starting transfers between devices, turn(): return lax.ppermute(x, 'band', [(i, (i + k) % n) for i in range(n)])  7.97 us
    pallas_call x1, Pallas kernels, unit(): pl.pallas_call(functools.partial(out_kernel, n, moves, len(args)), in_spe...  6.63 us
  transfers between devices with their start and end apart: 24, of which 5 were waited for; matrix products, arithmetic and copies ran while one was open for 1% of the time, Pallas kernels for 26%

profile of v5, /device:TPU:0, one launch (start us, length us, event | category | flops | bytes accessed | tf_op | source)
XLA Modules:
  0.0 144.5 jit_solution(4616708011239986933)
XLA Ops:
  0.6 0.0 copy-start
  0.7 2.2 %constant_dynamic-slice_fusion = bf16[176,2240]{1,0:T(8,128)(2,1)} fusion(bf16[352,2240]{1,0:T(8,128)(2,1)} %param.8, s32[]{:T(128)S(6)} %select_n.38), kind=kLoop, calls=%fused_computation.12 | loop fusion | bytes 1576964 | tf_op jit(solution)/shard_map/dynamic_slice | solution.py:298
  2.9 6.0 %collective-permute-start.11 = (bf16[176,2240]{1,0:T(8,128)(2,1)}, bf16[176,2240]{1,0:T(8,128)(2,1)S(1)}, u32[]{:S(2)}, u32[]{:S(2)}) collective-permute-start(bf16[176,2240]{1,0:T(8,128)(2,1)} %constant_dynamic-slice_fusion), channel_id=1, source_target_pairs={{0,8},{3,11},{4,12},{7,15},{8,0},{11,3},{12,4},{15,7},{16,24},{19,... | collective-permute-start | bytes 2365448 | tf_op jit(solution)/shard_map/ppermute | solution.py:288
  8.8 0.1 collective-permute-start.6
  8.9 3.5 %collective-permute-start.7 = (bf16[176,2240]{1,0:T(8,128)(2,1)}, bf16[176,2240]{1,0:T(8,128)(2,1)}, u32[]{:S(2)}, u32[]{:S(2)}) collective-permute-start(bf16[176,2240]{1,0:T(8,128)(2,1)} %constant_dynamic-slice_fusion), channel_id=1, source_target_pairs={{0,4},{3,7},{4,0},{7,3},{8,12},{11,15},{12,8},{15,11},{16,20},{19,... | collective-permute-start | bytes 2365448 | tf_op jit(solution)/shard_map/ppermute | solution.py:288
  12.5 0.1 pad.4.clone
  12.5 15.5 %collective-permute-done.11.refs_6_ = bf16[176,2240]{1,0:T(8,128)(2,1)S(1)} collective-permute-done((bf16[176,2240]{1,0:T(8,128)(2,1)}, bf16[176,2240]{1,0:T(8,128)(2,1)S(1)}, u32[]{:S(2)}, u32[]{:S(2)}) %collective-permute-start.11) | collective-permute-done | bytes 788512 | tf_op jit(solution)/shard_map/ppermute | solution.py:288
  28.1 2.9 %collective-permute-start.15 = (bf16[176,2240]{1,0:T(8,128)(2,1)S(1)}, bf16[176,2240]{1,0:T(8,128)(2,1)}, u32[]{:S(2)}, u32[]{:S(2)}) collective-permute-start(bf16[176,2240]{1,0:T(8,128)(2,1)S(1)} %collective-permute-done.11.refs_6_), channel_id=1, source_target_pairs={{0,4},{3,7},{4,0},{7,3},{8,12},{11,15},{12,8},{15,11},{16,20},{19,... | collective-permute-start | bytes 2365448 | tf_op jit(solution)/shard_map/ppermute | solution.py:288
  31.0 0.1 constant_dynamic-update-slice_fusion.4
  31.1 0.1 collective-permute-start.1
  31.2 0.6 stack.32.s_ref
  31.8 3.3 %pack.1 = (bf16[2,4,2,64,352]{4,3,2,1,0:T(8,128)(2,1)}, bf16[2,4,2,64,352]{4,3,2,1,0:T(8,128)(2,1)}) custom-call(s32[5]{0:T(128)} %stack.32.s_ref, bf16[128,5632]{1,0:T(8,128)(2,1)} %bitcast.22), custom_call_target="tpu_custom_call" | custom-call | tf_op jit(solution)/shard_map/pack/pallas_call | solution.py:266
  35.2 0.2 collective-permute-start
  35.3 0.0 collective-permute-done.1
  35.3 0.7 collective-permute-start.2
  36.0 0.0 collective-permute-done.2
  36.0 0.7 collective-permute-start.3
  36.7 0.0 collective-permute-done.3
  36.7 0.7 collective-permute-start.4
  37.4 0.0 collective-permute-done.4
  37.4 16.0 %collective-permute-start.5 = (bf16[8,16,352]{2,1,0:T(8,128)(2,1)S(1)}, bf16[8,16,352]{2,1,0:T(8,128)(2,1)S(1)}, u32[]{:S(2)}, u32[]{:S(2)}) collective-permute-start(bf16[8,16,352]{2,1,0:T(8,128)(2,1)S(1)} %constant_dynamic-update-slice_fusion), channel_id=1, source_target_pairs={{0,2},{1,3},{2,0},{3,1},{4,6},{5,7},{6,4},{7,5},{8,10},{9,11},{10,... | collective-permute-start | bytes 270344 | tf_op jit(solution)/shard_map/ppermute | solution.py:288
  53.4 0.0 collective-permute-done.7.refs_2_.refs_8_
  53.4 3.7 %collective-permute-start.8 = (bf16[176,2240]{1,0:T(8,128)(2,1)}, bf16[176,2240]{1,0:T(8,128)(2,1)}, u32[]{:S(2)}, u32[]{:S(2)}) collective-permute-start(bf16[176,2240]{1,0:T(8,128)(2,1)} %collective-permute-done.7.refs_2_.refs_8_), channel_id=1, source_target_pairs={{0,16},{3,19},{4,20},{7,23},{8,24},{11,27},{12,28},{15,31},{16,0},... | collective-permute-start | bytes 2365448 | tf_op jit(solution)/shard_map/ppermute | solution.py:296
  57.1 0.0 collective-permute-done.5
  57.1 0.1 collective-permute-start.9
  57.2 0.0 collective-permute-done.refs_0_
  57.2 2.2 %collective-permute-start.12 = (bf16[176,2240]{1,0:T(8,128)(2,1)S(1)}, bf16[176,2240]{1,0:T(8,128)(2,1)}, u32[]{:S(2)}, u32[]{:S(2)}) collective-permute-start(bf16[176,2240]{1,0:T(8,128)(2,1)S(1)} %collective-permute-done.11.refs_6_), channel_id=1, source_target_pairs={{0,16},{3,19},{4,20},{7,23},{8,24},{11,27},{12,28},{15,31},{16,0},... | collective-permute-start | bytes 2365448 | tf_op jit(solution)/shard_map/ppermute | solution.py:296
  59.4 0.0 collective-permute-done.15.refs_10_
  59.4 3.7 %collective-permute-start.16 = (bf16[176,2240]{1,0:T(8,128)(2,1)}, bf16[176,2240]{1,0:T(8,128)(2,1)}, u32[]{:S(2)}, u32[]{:S(2)}) collective-permute-start(bf16[176,2240]{1,0:T(8,128)(2,1)} %collective-permute-done.15.refs_10_), channel_id=1, source_target_pairs={{0,16},{3,19},{4,20},{7,23},{8,24},{11,27},{12,28},{15,31},{16,0},... | collective-permute-start | bytes 2365448 | tf_op jit(solution)/shard_map/ppermute | solution.py:296
  63.1 0.0 collective-permute-done.6
  63.1 0.1 collective-permute-start.13
  63.2 4.7 %collective-permute-done.8.refs_3_.refs_9_ = bf16[176,2240]{1,0:T(8,128)(2,1)} collective-permute-done((bf16[176,2240]{1,0:T(8,128)(2,1)}, bf16[176,2240]{1,0:T(8,128)(2,1)}, u32[]{:S(2)}, u32[]{:S(2)}) %collective-permute-start.8) | collective-permute-done | bytes 788512 | tf_op jit(solution)/shard_map/ppermute | solution.py:296
  67.9 0.0 collective-permute-start.17
  67.9 0.0 collective-permute-done.9.refs_4_.refs_10_
  67.9 0.5 collective-permute-start.10
  68.4 8.2 %collective-permute-done.12.refs_7_ = bf16[176,2240]{1,0:T(8,128)(2,1)} collective-permute-done((bf16[176,2240]{1,0:T(8,128)(2,1)S(1)}, bf16[176,2240]{1,0:T(8,128)(2,1)}, u32[]{:S(2)}, u32[]{:S(2)}) %collective-permute-start.12) | collective-permute-done | bytes 788512 | tf_op jit(solution)/shard_map/ppermute | solution.py:296
  76.6 0.0 collective-permute-start.14
  76.6 8.7 %collective-permute-done.16.refs_11_ = bf16[176,2240]{1,0:T(8,128)(2,1)} collective-permute-done((bf16[176,2240]{1,0:T(8,128)(2,1)}, bf16[176,2240]{1,0:T(8,128)(2,1)}, u32[]{:S(2)}, u32[]{:S(2)}) %collective-permute-start.16) | collective-permute-done | bytes 788512 | tf_op jit(solution)/shard_map/ppermute | solution.py:296
  85.3 0.0 collective-permute-start.18
  85.3 0.0 collective-permute-done.13.refs_8_
  85.3 3.7 %collective-permute-start.20 = (bf16[1,2,64,2240]{3,2,1,0:T(8,128)(2,1)}, bf16[1,2,64,2240]{3,2,1,0:T(8,128)(2,1)}, u32[]{:S(2)}, u32[]{:S(2)}) collective-permute-start(bf16[1,2,64,2240]{3,2,1,0:T(8,128)(2,1)} %param.9), channel_id=1, source_target_pairs={{0,1},{1,0},{2,3},{3,2},{4,5},{5,4},{6,7},{7,6},{8,9},{9,8},{10,11... | collective-permute-start | bytes 1720328 | tf_op jit(solution)/shard_map/ppermute | solution.py:339
  89.0 0.6 broadcast_select_fusion.refs_1_
  89.7 6.1 %conv.1 = (bf16[4,2,128,352]{3,2,1,0:T(8,128)(2,1)}, f32[4,2,128,352]{3,2,1,0:T(8,128)}, f32[4,2,128,352]{3,2,1,0:T(8,128)}) custom-call(s32[5]{0:T(128)} %stack.32.s_ref, bf16[2,4,2,64,352]{4,3,2,1,0:T(8,128)(2,1)} %get-tuple-element.20.own, bf16[2,4,2,64,352]{4,3,2,1,0:T(8,128)(2,1)} %copy-done.1, bf16[8,16,352]{2,1,0:T(8,128)(2,1)} %broadcast_select_fusion.refs_1_), custom_call_target="tpu_custom_call" | custom-call | tf_op jit(solution)/shard_map/conv/pallas_call | solution.py:349
  95.8 0.0 collective-permute-done.10.refs_5_.refs_11_
  95.8 0.0 collective-permute-done.14.refs_9_
  95.8 0.0 collective-permute-done.17.refs_12_
  95.8 0.0 collective-permute-done.18.refs_13_
  95.8 0.9 copy-done.5
  96.8 6.6 %project.1 = (f32[128,2240]{1,0:T(8,128)}, bf16[128,2240]{1,0:T(8,128)(2,1)}) custom-call(s32[5]{0:T(128)} %stack.32.s_ref, bf16[4,2,128,352]{3,2,1,0:T(8,128)(2,1)} %get-tuple-element.22.glu, bf16[2,176,2240]{2,1,0:T(8,128)(2,1)} %bitcast.18, bf16[2,176,2240]{2,1,0:T(8,128)(2,1)} %bitcast.9.refs_1_.refs_7_, ...), custom_call_target="tpu_custom_call" | custom-call | tf_op jit(solution)/shard_map/project/pallas_call | solution.py:392
  103.4 0.2 collective-permute-start.19
  103.6 0.0 collective-permute-done.20
  103.6 9.2 %shard_map.84 = (bf16[2,2,2,64,352]{4,3,2,1,0:T(8,128)(2,1)}, bf16[2,2,2,64,352]{4,3,2,1,0:T(8,128)(2,1)}, f32[2,4,16,352]{3,2,1,0:T(8,128)}) custom-call(s32[5]{0:T(128)} %stack.32.s_ref, bf16[2,4,2,64,352]{4,3,2,1,0:T(8,128)(2,1)} %get-tuple-element.20.own, bf16[2,4,2,64,352]{4,3,2,1,0:T(8,128)(2,1)} %copy-done.1, ...), custom_call_target="tpu_custom_call" | custom-call | tf_op jit(solution)/shard_map/pallas_call | solution.py:419
  112.8 1.7 %collective-permute-start.22 = (bf16[2,2,2,64,352]{4,3,2,1,0:T(8,128)(2,1)}, bf16[2,2,2,64,352]{4,3,2,1,0:T(8,128)(2,1)S(1)}, u32[]{:S(2)}, u32[]{:S(2)}) collective-permute-start(bf16[2,2,2,64,352]{4,3,2,1,0:T(8,128)(2,1)} %get-tuple-element.30), channel_id=1, source_target_pairs={{0,1},{1,0},{2,3},{3,2},{4,5},{5,4},{6,7},{7,6},{8,9},{9,8},{10,11... | collective-permute-start | bytes 1081352 | tf_op jit(solution)/shard_map/ppermute | solution.py:339
  114.5 8.7 %shard_map.85 = (bf16[2,2,2,64,352]{4,3,2,1,0:T(8,128)(2,1)}, bf16[2,2,2,64,352]{4,3,2,1,0:T(8,128)(2,1)}, f32[2,4,16,352]{3,2,1,0:T(8,128)}) custom-call(s32[5]{0:T(128)} %stack.32.s_ref, bf16[2,4,2,64,352]{4,3,2,1,0:T(8,128)(2,1)} %get-tuple-element.20.own, bf16[2,4,2,64,352]{4,3,2,1,0:T(8,128)(2,1)} %copy-done.1, ...), custom_call_target="tpu_custom_call", output_to_operand_aliasing={{2}: (16, {})} | custom-call | tf_op jit(solution)/shard_map/pallas_call | solution.py:419
  123.2 0.5 collective-permute-start.23
  123.7 11.7 %all_to_all.5 = f32[8,16,352]{2,1,0:T(8,128)S(1)} all-to-all(f32[8,16,352]{2,1,0:T(8,128)} %bitcast.24), channel_id=1, replica_groups=mesh['groups'=2,'fsdp'=8,'band'=2] {'fsdp'}, dimensions={0} | all-to-all | bytes 360448 | tf_op jit(solution)/shard_map/all_to_all | solution.py:448
  135.4 1.7 %collective-permute-start.21 = (f32[16,352]{1,0:T(8,128)S(1)}, f32[16,352]{1,0:T(8,128)S(1)}, u32[]{:S(2)}, u32[]{:S(2)}) collective-permute-start(f32[16,352]{1,0:T(8,128)S(1)} %reduce_sum.9.refs_0_), channel_id=1, source_target_pairs={{0,1},{1,0},{2,3},{3,2},{4,5},{5,4},{6,7},{7,6},{8,9},{9,8},{10,11... | collective-permute-start | bytes 67592 | tf_op jit(solution)/shard_map/ppermute | solution.py:339
  137.1 0.0 collective-permute-done.22.refs_3_
  137.1 2.2 %collective-permute-done.21.refs_1_ = f32[16,352]{1,0:T(8,128)S(1)} collective-permute-done((f32[16,352]{1,0:T(8,128)S(1)}, f32[16,352]{1,0:T(8,128)S(1)}, u32[]{:S(2)}, u32[]{:S(2)}) %collective-permute-start.21) | collective-permute-done | bytes 22560 | tf_op jit(solution)/shard_map/ppermute | solution.py:339
  139.3 0.6 copy-done.11
  139.9 0.2 copy-done.8
  140.1 3.5 %unpack.1 = (bf16[128,5632]{1,0:T(8,128)(2,1)}, f32[9,704]{1,0:T(8,128)}, f32[704]{0:T(1024)}) custom-call(s32[5]{0:T(128)} %stack.32.s_ref, f32[16,352]{1,0:T(8,128)} %copy-done.9, f32[16,352]{1,0:T(8,128)} %copy-done.11, bf16[2,2,2,64,352]{4,3,2,1,0:T(8,128)(2,1)} %get-tuple-element.29.refs_2_, bf16[2,2,2,64,352]{4,3,2,1,0:T(8,128)(2,1)} %copy-done.7, ...), custom_call_target="tpu_custom_call" | custom-call | tf_op jit(solution)/shard_map/unpack/pallas_call | solution.py:461
  143.6 0.0 collective-permute-done.19
  143.6 0.9 add_convert_fusion
  (31 shorter events, 0.1 us)
Async XLA Ops:
  0.6 8.2 %copy-start = (bf16[352,2240]{1,0:T(8,128)(2,1)S(1)}, bf16[352,2240]{1,0:T(8,128)(2,1)}, u32[]{:S(2)}) copy-start(bf16[352,2240]{1,0:T(8,128)(2,1)} %param.8) | copy-start | bytes 4730884
  0.6 11.8 %copy-start.12 = (bf16[704]{0:T(1024)(128)(2,1)S(1)}, bf16[704]{0:T(1024)(128)(2,1)}, u32[]{:S(2)}) copy-start(bf16[704]{0:T(1024)(128)(2,1)} %param.7) | copy-start | bytes 4228
  0.7 30.4 %copy-start.10 = (bf16[9,704]{1,0:T(8,128)(2,1)S(1)}, bf16[9,704]{1,0:T(8,128)(2,1)}, u32[]{:S(2)}) copy-start(bf16[9,704]{1,0:T(8,128)(2,1)} %param.6) | copy-start | bytes 38020
  2.9 25.2 %collective-permute-start.11 = (bf16[176,2240]{1,0:T(8,128)(2,1)}, bf16[176,2240]{1,0:T(8,128)(2,1)S(1)}, u32[]{:S(2)}, u32[]{:S(2)}) collective-permute-start(bf16[176,2240]{1,0:T(8,128)(2,1)} %constant_dynamic-slice_fusion), channel_id=1, source_target_pairs={{0,8},{3,11},{4,12},{7,15},{8,0},{11,3},{12,4},{15,7},{16,24},{19,... | collective-permute-start | bytes 2365448 | tf_op jit(solution)/shard_map/ppermute | solution.py:288
  8.8 54.2 %collective-permute-start.6 = (bf16[352,2240]{1,0:T(8,128)(2,1)S(1)}, bf16[352,2240]{1,0:T(8,128)(2,1)}, u32[]{:S(2)}, u32[]{:S(2)}) collective-permute-start(bf16[352,2240]{1,0:T(8,128)(2,1)S(1)} %copy-done), channel_id=1, source_target_pairs={{0,2},{1,3},{2,0},{3,1},{4,6},{5,7},{6,4},{7,5},{8,10},{9,11},{10,... | collective-permute-start | bytes 4730888 | tf_op jit(solution)/shard_map/ppermute | solution.py:288
  8.9 44.5 %collective-permute-start.7 = (bf16[176,2240]{1,0:T(8,128)(2,1)}, bf16[176,2240]{1,0:T(8,128)(2,1)}, u32[]{:S(2)}, u32[]{:S(2)}) collective-permute-start(bf16[176,2240]{1,0:T(8,128)(2,1)} %constant_dynamic-slice_fusion), channel_id=1, source_target_pairs={{0,4},{3,7},{4,0},{7,3},{8,12},{11,15},{12,8},{15,11},{16,20},{19,... | collective-permute-start | bytes 2365448 | tf_op jit(solution)/shard_map/ppermute | solution.py:288
  28.1 67.7 %copy-start.2 = (bf16[176,2240]{1,0:T(8,128)(2,1)}, bf16[176,2240]{1,0:T(8,128)(2,1)S(1)}, u32[]{:S(2)}) copy-start(bf16[176,2240]{1,0:T(8,128)(2,1)S(1)} %collective-permute-done.11.refs_6_) | copy-start | bytes 2365444
  28.1 31.3 %collective-permute-start.15 = (bf16[176,2240]{1,0:T(8,128)(2,1)S(1)}, bf16[176,2240]{1,0:T(8,128)(2,1)}, u32[]{:S(2)}, u32[]{:S(2)}) collective-permute-start(bf16[176,2240]{1,0:T(8,128)(2,1)S(1)} %collective-permute-done.11.refs_6_), channel_id=1, source_target_pairs={{0,4},{3,7},{4,0},{7,3},{8,12},{11,15},{12,8},{15,11},{16,20},{19,... | collective-permute-start | bytes 2365448 | tf_op jit(solution)/shard_map/ppermute | solution.py:288
  31.1 4.2 %collective-permute-start.1 = (bf16[16,352]{1,0:T(8,128)(2,1)S(1)}, bf16[16,352]{1,0:T(8,128)(2,1)S(1)}, u32[]{:S(2)}, u32[]{:S(2)}) collective-permute-start(bf16[16,352]{1,0:T(8,128)(2,1)S(1)} %get-tuple-element.37), channel_id=1, source_target_pairs={{0,2},{1,3},{2,0},{3,1},{4,6},{5,7},{6,4},{7,5},{8,10},{9,11},{10,... | collective-permute-start | bytes 33800 | tf_op jit(solution)/shard_map/ppermute | solution.py:288
  35.2 22.0 %collective-permute-start = (bf16[2,4,2,64,352]{4,3,2,1,0:T(8,128)(2,1)}, bf16[2,4,2,64,352]{4,3,2,1,0:T(8,128)(2,1)S(1)}, u32[]{:S(2)}, u32[]{:S(2)}) collective-permute-start(bf16[2,4,2,64,352]{4,3,2,1,0:T(8,128)(2,1)} %get-tuple-element.21), channel_id=1, source_target_pairs={{0,1},{1,0},{2,3},{3,2},{4,5},{5,4},{6,7},{7,6},{8,9},{9,8},{10,11... | collective-permute-start | bytes 2162696 | tf_op jit(solution)/shard_map/ppermute | solution.py:339
  35.3 0.7 collective-permute-start.2
  36.0 0.7 collective-permute-start.3
  36.7 0.7 collective-permute-start.4
  37.4 19.7 %collective-permute-start.5 = (bf16[8,16,352]{2,1,0:T(8,128)(2,1)S(1)}, bf16[8,16,352]{2,1,0:T(8,128)(2,1)S(1)}, u32[]{:S(2)}, u32[]{:S(2)}) collective-permute-start(bf16[8,16,352]{2,1,0:T(8,128)(2,1)S(1)} %constant_dynamic-update-slice_fusion), channel_id=1, source_target_pairs={{0,2},{1,3},{2,0},{3,1},{4,6},{5,7},{6,4},{7,5},{8,10},{9,11},{10,... | collective-permute-start | bytes 270344 | tf_op jit(solution)/shard_map/ppermute | solution.py:288
  53.4 14.5 %collective-permute-start.8 = (bf16[176,2240]{1,0:T(8,128)(2,1)}, bf16[176,2240]{1,0:T(8,128)(2,1)}, u32[]{:S(2)}, u32[]{:S(2)}) collective-permute-start(bf16[176,2240]{1,0:T(8,128)(2,1)} %collective-permute-done.7.refs_2_.refs_8_), channel_id=1, source_target_pairs={{0,16},{3,19},{4,20},{7,23},{8,24},{11,27},{12,28},{15,31},{16,0},... | collective-permute-start | bytes 2365448 | tf_op jit(solution)/shard_map/ppermute | solution.py:296
  57.1 10.8 %collective-permute-start.9 = (bf16[176,2240]{1,0:T(8,128)(2,1)}, bf16[176,2240]{1,0:T(8,128)(2,1)S(1)}, u32[]{:S(2)}, u32[]{:S(2)}) collective-permute-start(bf16[176,2240]{1,0:T(8,128)(2,1)} %collective-permute-done.7.refs_2_.refs_8_), channel_id=1, source_target_pairs={{0,2},{1,3},{2,0},{3,1},{4,6},{5,7},{6,4},{7,5},{8,10},{9,11},{10,... | collective-permute-start | bytes 2365448 | tf_op jit(solution)/shard_map/ppermute | solution.py:288
  57.2 32.4 %copy-start.1 = (bf16[2,4,2,64,352]{4,3,2,1,0:T(8,128)(2,1)}, bf16[2,4,2,64,352]{4,3,2,1,0:T(8,128)(2,1)S(1)}, u32[]{:S(2)}) copy-start(bf16[2,4,2,64,352]{4,3,2,1,0:T(8,128)(2,1)S(1)} %collective-permute-done.refs_0_) | copy-start | bytes 2162692
  57.2 19.3 %collective-permute-start.12 = (bf16[176,2240]{1,0:T(8,128)(2,1)S(1)}, bf16[176,2240]{1,0:T(8,128)(2,1)}, u32[]{:S(2)}, u32[]{:S(2)}) collective-permute-start(bf16[176,2240]{1,0:T(8,128)(2,1)S(1)} %collective-permute-done.11.refs_6_), channel_id=1, source_target_pairs={{0,16},{3,19},{4,20},{7,23},{8,24},{11,27},{12,28},{15,31},{16,0},... | collective-permute-start | bytes 2365448 | tf_op jit(solution)/shard_map/ppermute | solution.py:296
  59.4 25.9 %collective-permute-start.16 = (bf16[176,2240]{1,0:T(8,128)(2,1)}, bf16[176,2240]{1,0:T(8,128)(2,1)}, u32[]{:S(2)}, u32[]{:S(2)}) collective-permute-start(bf16[176,2240]{1,0:T(8,128)(2,1)} %collective-permute-done.15.refs_10_), channel_id=1, source_target_pairs={{0,16},{3,19},{4,20},{7,23},{8,24},{11,27},{12,28},{15,31},{16,0},... | collective-permute-start | bytes 2365448 | tf_op jit(solution)/shard_map/ppermute | solution.py:296
  63.1 22.2 %collective-permute-start.13 = (bf16[176,2240]{1,0:T(8,128)(2,1)S(1)}, bf16[176,2240]{1,0:T(8,128)(2,1)S(1)}, u32[]{:S(2)}, u32[]{:S(2)}) collective-permute-start(bf16[176,2240]{1,0:T(8,128)(2,1)S(1)} %collective-permute-done.11.refs_6_), channel_id=1, source_target_pairs={{0,2},{1,3},{2,0},{3,1},{4,6},{5,7},{6,4},{7,5},{8,10},{9,11},{10,... | collective-permute-start | bytes 2365448 | tf_op jit(solution)/shard_map/ppermute | solution.py:288
  67.9 27.9 %collective-permute-start.17 = (bf16[176,2240]{1,0:T(8,128)(2,1)}, bf16[176,2240]{1,0:T(8,128)(2,1)S(1)}, u32[]{:S(2)}, u32[]{:S(2)}) collective-permute-start(bf16[176,2240]{1,0:T(8,128)(2,1)} %collective-permute-done.15.refs_10_), channel_id=1, source_target_pairs={{0,2},{1,3},{2,0},{3,1},{4,6},{5,7},{6,4},{7,5},{8,10},{9,11},{10,... | collective-permute-start | bytes 2365448 | tf_op jit(solution)/shard_map/ppermute | solution.py:288
  67.9 17.4 %copy-start.3 = (bf16[176,2240]{1,0:T(8,128)(2,1)}, bf16[176,2240]{1,0:T(8,128)(2,1)S(1)}, u32[]{:S(2)}) copy-start(bf16[176,2240]{1,0:T(8,128)(2,1)S(1)} %collective-permute-done.9.refs_4_.refs_10_) | copy-start | bytes 2365444
  67.9 27.9 %collective-permute-start.10 = (bf16[176,2240]{1,0:T(8,128)(2,1)}, bf16[176,2240]{1,0:T(8,128)(2,1)}, u32[]{:S(2)}, u32[]{:S(2)}) collective-permute-start(bf16[176,2240]{1,0:T(8,128)(2,1)} %collective-permute-done.8.refs_3_.refs_9_), channel_id=1, source_target_pairs={{0,2},{1,3},{2,0},{3,1},{4,6},{5,7},{6,4},{7,5},{8,10},{9,11},{10,... | collective-permute-start | bytes 2365448 | tf_op jit(solution)/shard_map/ppermute | solution.py:288
  76.6 19.2 %collective-permute-start.14 = (bf16[176,2240]{1,0:T(8,128)(2,1)}, bf16[176,2240]{1,0:T(8,128)(2,1)}, u32[]{:S(2)}, u32[]{:S(2)}) collective-permute-start(bf16[176,2240]{1,0:T(8,128)(2,1)} %collective-permute-done.12.refs_7_), channel_id=1, source_target_pairs={{0,2},{1,3},{2,0},{3,1},{4,6},{5,7},{6,4},{7,5},{8,10},{9,11},{10,... | collective-permute-start | bytes 2365448 | tf_op jit(solution)/shard_map/ppermute | solution.py:288
  85.3 10.6 %collective-permute-start.18 = (bf16[176,2240]{1,0:T(8,128)(2,1)}, bf16[176,2240]{1,0:T(8,128)(2,1)}, u32[]{:S(2)}, u32[]{:S(2)}) collective-permute-start(bf16[176,2240]{1,0:T(8,128)(2,1)} %collective-permute-done.16.refs_11_), channel_id=1, source_target_pairs={{0,2},{1,3},{2,0},{3,1},{4,6},{5,7},{6,4},{7,5},{8,10},{9,11},{10,... | collective-permute-start | bytes 2365448 | tf_op jit(solution)/shard_map/ppermute | solution.py:288
  85.3 10.6 %copy-start.4 = (bf16[176,2240]{1,0:T(8,128)(2,1)}, bf16[176,2240]{1,0:T(8,128)(2,1)S(1)}, u32[]{:S(2)}) copy-start(bf16[176,2240]{1,0:T(8,128)(2,1)S(1)} %collective-permute-done.13.refs_8_) | copy-start | bytes 2365444
  85.3 18.3 %collective-permute-start.20 = (bf16[1,2,64,2240]{3,2,1,0:T(8,128)(2,1)}, bf16[1,2,64,2240]{3,2,1,0:T(8,128)(2,1)}, u32[]{:S(2)}, u32[]{:S(2)}) collective-permute-start(bf16[1,2,64,2240]{3,2,1,0:T(8,128)(2,1)} %param.9), channel_id=1, source_target_pairs={{0,1},{1,0},{2,3},{3,2},{4,5},{5,4},{6,7},{7,6},{8,9},{9,8},{10,11... | collective-permute-start | bytes 1720328 | tf_op jit(solution)/shard_map/ppermute | solution.py:339
  95.8 0.9 copy-start.5
  103.4 40.2 %collective-permute-start.19 = (bf16[1,2,64,2240]{3,2,1,0:T(8,128)(2,1)}, bf16[1,2,64,2240]{3,2,1,0:T(8,128)(2,1)S(1)}, u32[]{:S(2)}, u32[]{:S(2)}) collective-permute-start(bf16[1,2,64,2240]{3,2,1,0:T(8,128)(2,1)} %bitcast.28), channel_id=1, source_target_pairs={{0,1},{1,0},{2,3},{3,2},{4,5},{5,4},{6,7},{7,6},{8,9},{9,8},{10,11... | collective-permute-start | bytes 1720328 | tf_op jit(solution)/shard_map/ppermute | solution.py:339
  112.8 24.3 %collective-permute-start.22 = (bf16[2,2,2,64,352]{4,3,2,1,0:T(8,128)(2,1)}, bf16[2,2,2,64,352]{4,3,2,1,0:T(8,128)(2,1)S(1)}, u32[]{:S(2)}, u32[]{:S(2)}) collective-permute-start(bf16[2,2,2,64,352]{4,3,2,1,0:T(8,128)(2,1)} %get-tuple-element.30), channel_id=1, source_target_pairs={{0,1},{1,0},{2,3},{3,2},{4,5},{5,4},{6,7},{7,6},{8,9},{9,8},{10,11... | collective-permute-start | bytes 1081352 | tf_op jit(solution)/shard_map/ppermute | solution.py:339
  123.2 20.3 %copy-start.6 = (f32[128,2240]{1,0:T(8,128)S(1)}, f32[128,2240]{1,0:T(8,128)}, u32[]{:S(2)}) copy-start(f32[128,2240]{1,0:T(8,128)} %get-tuple-element.23) | copy-start | bytes 3440644
  123.2 16.1 %collective-permute-start.23 = (bf16[2,2,2,64,352]{4,3,2,1,0:T(8,128)(2,1)}, bf16[2,2,2,64,352]{4,3,2,1,0:T(8,128)(2,1)S(1)}, u32[]{:S(2)}, u32[]{:S(2)}) collective-permute-start(bf16[2,2,2,64,352]{4,3,2,1,0:T(8,128)(2,1)} %get-tuple-element.32), channel_id=1, source_target_pairs={{0,1},{1,0},{2,3},{3,2},{4,5},{5,4},{6,7},{7,6},{8,9},{9,8},{10,11... | collective-permute-start | bytes 1081352 | tf_op jit(solution)/shard_map/ppermute | solution.py:339
  135.4 3.9 %copy-start.9 = (f32[16,352]{1,0:T(8,128)}, f32[16,352]{1,0:T(8,128)S(1)}, u32[]{:S(2)}) copy-start(f32[16,352]{1,0:T(8,128)S(1)} %reduce_sum.9.refs_0_) | copy-start | bytes 67588
  135.4 3.9 %collective-permute-start.21 = (f32[16,352]{1,0:T(8,128)S(1)}, f32[16,352]{1,0:T(8,128)S(1)}, u32[]{:S(2)}, u32[]{:S(2)}) collective-permute-start(f32[16,352]{1,0:T(8,128)S(1)} %reduce_sum.9.refs_0_), channel_id=1, source_target_pairs={{0,1},{1,0},{2,3},{3,2},{4,5},{5,4},{6,7},{7,6},{8,9},{9,8},{10,11... | collective-permute-start | bytes 67592 | tf_op jit(solution)/shard_map/ppermute | solution.py:339
  137.1 2.2 %copy-start.7 = (bf16[2,2,2,64,352]{4,3,2,1,0:T(8,128)(2,1)}, bf16[2,2,2,64,352]{4,3,2,1,0:T(8,128)(2,1)S(1)}, u32[]{:S(2)}) copy-start(bf16[2,2,2,64,352]{4,3,2,1,0:T(8,128)(2,1)S(1)} %collective-permute-done.22.refs_3_) | copy-start | bytes 1081348
  139.3 0.6 copy-start.11
  139.3 0.8 copy-start.8
